TPU v7x, 256 devices: a whole 4x4x8 slice. The times are simulated.
256 devices in a mesh: vol: 32 (over z, y), rep: 8 (over x, core).
Axes of the slice: x: 4, y: 4, z: 8, core: 2. Of those that a mesh axis runs over, the one named last changes fastest.
Arguments:
- features: bfloat16 [32, 32, 4, 16384], P('vol', None, None, 'rep'), may hold values from -6 to 6
- deltas: float32 [32, 4, 16384], P('vol', None, 'rep'), may hold values from 0.003125 to 0.03125
- counts: int32 [32, 16384], P('vol', 'rep'), may hold values from 0 to 4
- order_rank: int32 [16384, 32], P('rep'), may hold values from 0 to 31, each once within a row
- cotangent: float32 [3, 16384], P(None, 'rep'), may hold values from -6 to 6
- first_weight: bfloat16 [32, 32, 256], P('vol'), may hold values from -1.5 to 1.5
- middle_weight: bfloat16 [32, 2, 256, 256], P('vol'), may hold values from -0.5 to 0.5
- last_weight: bfloat16 [32, 256, 4], P('vol'), may hold values from -0.375 to 0.375
Outputs:
- first_grad: float32 [32, 32, 256], P('vol')
- middle_grad: float32 [32, 2, 256, 256], P('vol')
- last_grad: float32 [32, 256, 4], P('vol')
Inputs may be any that keep to these rules, and one draw needn't show every extreme that they name: `order_rank`: each ray's row holds every number of 0 .. 31 once.
All inputs are finite; a program needn't handle non-finite values.
Results may differ from a plain program's by a relative error of at most 0.0083.
Values sent between devices are 32-bit elements; how exact they have to be, the bound alone decides.
No kernel may reach another device: no remote copies, remote signals or barrier semaphores. Data moves between devices by JAX's collectives and lax.ppermute only.
A program may use at most 128 MiB of HBM per device.

v0:
```python
import jax
import jax.numpy as jnp
from jax import lax
from jax.sharding import PartitionSpec as P


def contract_first(matrix, rows):
    return lax.dot_general(
        matrix, rows, (((0,), (0,)), ((), ())), preferred_element_type=jnp.float32
    )


def contract_last(left, right):
    return lax.dot_general(
        left, right, (((1,), (1,)), ((), ())), preferred_element_type=jnp.float32
    )


def silu_grad(pre):
    logistic = jax.nn.sigmoid(pre)
    return logistic * (1.0 + pre * (1.0 - logistic))


def forward_network(samples, first_weight, middle_weight, last_weight):
    pre = contract_first(first_weight, samples)
    preacts = [pre]
    layer_inputs = [samples]
    hidden = jax.nn.silu(pre).astype(jnp.bfloat16)
    for depth in range(middle_weight.shape[0]):
        layer_inputs.append(hidden)
        pre = contract_first(middle_weight[depth], hidden)
        preacts.append(pre)
        hidden = jax.nn.silu(pre).astype(jnp.bfloat16)
    layer_inputs.append(hidden)
    head_out = contract_first(last_weight, hidden)
    return (preacts, layer_inputs, head_out)


def render_segment(head_out, deltas, counts):
    density = jax.nn.softplus(head_out[0])
    albedo = jax.nn.sigmoid(head_out[1:])
    live = (lax.broadcasted_iota(jnp.int32, deltas.shape, 0) < counts[None, :]).astype(jnp.float32)
    optical = density * deltas * live
    reached = jnp.cumsum(optical, axis=0)
    passed = reached - optical
    leaving = jnp.exp(-reached)
    sample_weight = jnp.exp(-passed) - leaving
    colour = jnp.sum(sample_weight[None] * albedo, axis=1)
    logt = -reached[-1]
    return (colour, logt, (albedo, leaving, sample_weight, live))


def head_gradient(head_out, deltas, saved, grad_colour, grad_logt):
    albedo, leaving, sample_weight, live = saved
    facing = jnp.sum(grad_colour[:, None, :] * albedo, axis=0)
    weighted = facing * sample_weight
    later = jnp.sum(weighted, axis=0)[None] - jnp.cumsum(weighted, axis=0)
    doptical = facing * leaving - later - grad_logt[None]
    d_density = doptical * deltas * live * jax.nn.sigmoid(head_out[0])
    d_albedo = sample_weight[None] * grad_colour[:, None, :] * albedo * (1.0 - albedo)
    return jnp.concatenate([d_density[None], d_albedo], axis=0).astype(jnp.bfloat16)


def network_gradients(preacts, layer_inputs, head_grad, middle_weight, last_weight, reducers):
    last_grad = reducers[0](contract_last(layer_inputs[-1], head_grad))
    back = (
        jnp.dot(last_weight, head_grad, preferred_element_type=jnp.float32) * silu_grad(preacts[-1])
    ).astype(jnp.bfloat16)
    hidden_grads = []
    for depth in reversed(range(middle_weight.shape[0])):
        hidden_grads.append(reducers[1](contract_last(layer_inputs[depth + 1], back)))
        back = (
            jnp.dot(middle_weight[depth], back, preferred_element_type=jnp.float32)
            * silu_grad(preacts[depth])
        ).astype(jnp.bfloat16)
    first_grad = reducers[2](contract_last(layer_inputs[0], back))
    middle_grad = jnp.stack(hidden_grads[::-1], axis=0)
    return (first_grad, middle_grad, last_grad)


def composite_rays(segments, rank_rows, cotangent):
    logs = segments[:, 3]

    def add_log(index, total):
        other = lax.dynamic_index_in_dim(rank_rows, index, 0, keepdims=True)
        term = lax.dynamic_index_in_dim(logs, index, 0, keepdims=True)
        return total + jnp.where(other < rank_rows, term, 0.0)

    summed = lax.fori_loop(0, rank_rows.shape[0], add_log, jnp.zeros(rank_rows.shape, jnp.float32))
    prefix = jnp.exp(summed)
    facing = jnp.sum(cotangent[None] * segments[:, :3], axis=1) * prefix

    def add_behind(index, total):
        other = lax.dynamic_index_in_dim(rank_rows, index, 0, keepdims=True)
        term = lax.dynamic_index_in_dim(facing, index, 0, keepdims=True)
        return total + jnp.where(other > rank_rows, term, 0.0)

    behind = lax.fori_loop(
        0, rank_rows.shape[0], add_behind, jnp.zeros(rank_rows.shape, jnp.float32)
    )
    return (prefix, behind)


def unchanged(value):
    return value


def per_device(
    features, deltas, counts, order_rank, cotangent, first_weight, middle_weight, last_weight
):
    samples = features[0].reshape(features.shape[1], -1)
    preacts, layer_inputs, head_out = forward_network(
        samples, first_weight[0], middle_weight[0], last_weight[0]
    )
    shaped = head_out.reshape(4, deltas.shape[1], deltas.shape[2])
    colour, logt, saved = render_segment(shaped, deltas[0], counts[0])
    payload = jnp.concatenate([colour, logt[None]], axis=0)
    rank_rows = order_rank.T
    mine = lax.axis_index("vol")
    segments = lax.all_gather(payload[None], "vol", axis=0, tiled=True)
    prefix, behind = composite_rays(segments, rank_rows, cotangent)
    own_prefix = lax.dynamic_index_in_dim(prefix, mine, 0, keepdims=False)
    own_behind = lax.dynamic_index_in_dim(behind, mine, 0, keepdims=False)
    grad_colour = own_prefix[None] * cotangent
    head_grad = head_gradient(shaped, deltas[0], saved, grad_colour, own_behind).reshape(4, -1)
    first_grad, middle_grad, last_grad = network_gradients(
        preacts,
        layer_inputs,
        head_grad,
        middle_weight[0],
        last_weight[0],
        (unchanged, unchanged, unchanged),
    )
    first_grad, middle_grad, last_grad = lax.psum((first_grad, middle_grad, last_grad), "rep")
    return (first_grad[None], middle_grad[None], last_grad[None])


def solution(mesh):
    placed = (
        P("vol", None, None, "rep"),
        P("vol", None, "rep"),
        P("vol", "rep"),
        P("rep", None),
        P(None, "rep"),
        P("vol", None, None),
        P("vol", None, None, None),
        P("vol", None, None),
    )
    return jax.shard_map(
        per_device,
        mesh=mesh,
        in_specs=placed,
        out_specs=(P("vol", None, None), P("vol", None, None, None), P("vol", None, None)),
        check_vma=False,
    )
```

profile of v0, /device:TPU:1, one launch (start us, length us, event | category | flops | bytes accessed | tf_op | source)
XLA Modules:
  0.0 218.6 jit_solution(7346373873611714705)
XLA Ops:
  7.2 1.3 copy.24
  8.6 4.7 %multiply_convert_fusion.2 = (bf16[256,8192]{1,0:T(8,128)(2,1)S(1)}, f32[256,8192]{1,0:T(8,128)}) fusion(bf16[32,8192]{1,0:T(8,128)(2,1)S(1)} %bitcast.145, bf16[1,32,256]{2,1,0:T(8,128)(2,1)S(1)} %copy-done), kind=kOutput, calls=%fused_computation.22 | convolution fusion | flops 144703488 | bytes 13123584 | tf_op jit(solution)/shard_map/dot_general | solution.py:8
  13.3 4.9 %multiply_convert_fusion.1 = (bf16[256,8192]{1,0:T(8,128)(2,1)S(1)}, f32[256,8192]{1,0:T(8,128)}) fusion(bf16[256,8192]{1,0:T(8,128)(2,1)S(1)} %get-tuple-element.217, bf16[1,2,256,256]{3,2,1,0:T(8,128)(2,1)S(1)} %copy-done.7), kind=kOutput, calls=%fused_computation.20 | convolution fusion | flops 1084227584 | bytes 16908288 | tf_op jit(solution)/shard_map/dot_general | solution.py:8
  18.2 4.9 %multiply_convert_fusion = (bf16[256,8192]{1,0:T(8,128)(2,1)S(1)}, f32[256,8192]{1,0:T(8,128)}) fusion(bf16[256,8192]{1,0:T(8,128)(2,1)S(1)} %get-tuple-element.219, bf16[1,2,256,256]{3,2,1,0:T(8,128)(2,1)S(1)} %copy-done.7), kind=kOutput, calls=%fused_computation.18 | convolution fusion | flops 1084227584 | bytes 16908288 | tf_op jit(solution)/shard_map/dot_general | solution.py:8
  23.1 1.9 copy-done.2
  25.0 0.6 convolution_bitcast_fusion.5
  26.4 0.6 maximum_bitcast_fusion.1
  27.1 75.2 %all-gather.4.cloned.1.call-done = f32[32,4,2048]{2,1,0:T(4,128)} async-done(((f32[1,4,2048]{2,1,0:T(4,128)}), f32[32,4,2048]{2,1,0:T(4,128)}) %all-gather.4.cloned.1.call-update) | async-done | bytes 1048592 | tf_op jit(solution)/shard_map/all_gather | solution.py:120
  102.3 1.5 slice.38
  103.9 6.4 %while.28 = (s32[]{:T(128)}, f32[32,2048]{1,0:T(8,128)S(1)}, s32[32,2048]{1,0:T(8,128)S(1)}, f32[32,2048]{1,0:T(8,128)S(1)}, s32[]{:T(128)}, /*index=5*/s32[]{:T(128)}) while((s32[]{:T(128)}, f32[32,2048]{1,0:T(8,128)S(1)}, s32[32,2048]{1,0:T(8,128)S(1)}, f32[32,2048]{1,0:T(8,128)S(1)}, s32[]{:T(128)}, /*index=5*/s32[]{:T(128)}) %tuple.83), condition=%wide.region_3.4_spmd.clone, body=%wide.region_2.3_spmd.clone.sunk | while | flops 262147 | bytes 835679 | solution.py:89
  110.3 1.9 fusion.8
  112.3 6.2 %while.29 = (s32[]{:T(128)}, f32[32,2048]{1,0:T(8,128)S(1)}, s32[32,2048]{1,0:T(8,128)S(1)}, f32[32,2048]{1,0:T(8,128)S(1)}, s32[]{:T(128)}, /*index=5*/s32[]{:T(128)}) while((s32[]{:T(128)}, f32[32,2048]{1,0:T(8,128)S(1)}, s32[32,2048]{1,0:T(8,128)S(1)}, f32[32,2048]{1,0:T(8,128)S(1)}, s32[]{:T(128)}, /*index=5*/s32[]{:T(128)}) %tuple.82), condition=%wide.region_9.10_spmd.clone, body=%wide.region_8.9_spmd.clone.sunk | while | flops 262147 | bytes 835679 | solution.py:98
  118.6 0.2 multiply_reduce_fusion
  119.1 5.8 %fusion.3 = bf16[256,8192]{1,0:T(8,128)(2,1)S(1)} fusion(f32[256,8192]{1,0:T(8,128)} %get-tuple-element.222, bf16[3,8192]{1,0:T(4,128)(2,1)S(1)} %get-tuple-element.212, bf16[1,8192]{1,0:T(2,128)(2,1)S(1)} %bitcast.148, bf16[1,256,4]{1,2,0:T(4,128)(2,1)S(1)} %copy-done.6), kind=kOutput, calls=%fused_computation.14 | convolution fusion | flops 35782656 | bytes 12650496 | tf_op jit(solution)/shard_map/dot_general | solution.py:67
  124.9 1.3 convolution_bitcast_fusion.6
  126.2 6.0 %fusion.4 = bf16[256,8192]{1,0:T(8,128)(2,1)S(1)} fusion(bf16[256,8192]{1,0:T(8,128)(2,1)S(1)} %fusion.3, f32[256,8192]{1,0:T(8,128)} %get-tuple-element.220, bf16[1,2,256,256]{3,2,1,0:T(8,128)(2,1)S(1)} %copy-done.7), kind=kOutput, calls=%fused_computation.15 | convolution fusion | flops 1092616192 | bytes 16908288 | tf_op jit(solution)/shard_map/dot_general | solution.py:73
  132.3 1.3 convolution_bitcast_fusion.7
  133.6 0.7 copy-done.12
  134.2 8.0 %fusion.7 = f32[1,32,256]{2,1,0:T(8,128)S(1)} fusion(bf16[32,8192]{1,0:T(8,128)(2,1)S(1)} %bitcast.146, bf16[256,8192]{1,0:T(8,128)(2,1)} %copy-done.12, f32[256,8192]{1,0:T(8,128)} %get-tuple-element.218, bf16[1,2,256,256]{3,2,1,0:T(8,128)(2,1)S(1)} %copy-done.7), kind=kOutput, calls=%fused_computation.27 | convolution fusion | flops 1226833920 | bytes 13271040 | tf_op jit(solution)/shard_map/dot_general | solution.py:14
  142.3 0.9 maximum_bitcast_fusion
  143.2 3.4 %convolution_bitcast_fusion.8 = f32[1,256,4]{1,2,0:T(4,128)S(1)} fusion(bf16[256,8192]{1,0:T(8,128)(2,1)} %copy-done.2, bf16[3,8192]{1,0:T(4,128)(2,1)S(1)} %get-tuple-element.212, bf16[1,8192]{1,0:T(2,128)(2,1)S(1)} %bitcast.149), kind=kOutput, calls=%fused_computation.28 | convolution fusion | flops 16908288 | bytes 4263936 | tf_op jit(solution)/shard_map/dot_general | solution.py:14
  146.6 27.6 %all-reduce = (f32[1,32,256]{2,1,0:T(8,128)}, f32[1,256,4]{1,2,0:T(4,128)}) all-reduce(f32[1,32,256]{2,1,0:T(8,128)S(1)} %fusion.7, f32[1,256,4]{1,2,0:T(4,128)S(1)} %convolution_bitcast_fusion.8), channel_id=1, replica_groups=mesh['vol'=32,'rep'=8] {'rep'}, use_global_device_ids=true, to_apply=%region_10.11 | all-reduce | flops 9216 | bytes 73728 | tf_op jit(solution)/shard_map/psum | solution.py:134
  174.2 35.7 %all-reduce.3.cloned.1.call-done = f32[1,2,256,256]{3,2,1,0:T(8,128)} async-done(((f32[1,2,256,256]{3,2,1,0:T(8,128)}), f32[1,2,256,256]{3,2,1,0:T(8,128)}) %all-reduce.3.cloned.1.call-update) | async-done | bytes 524304 | tf_op jit(solution)/shard_map/psum | solution.py:134
  209.9 1.9 copy.43
  (246 shorter events, 11.1 us)
Async XLA Ops:
  7.2 1.4 copy-start
  7.2 95.1 %all-gather.4.cloned.1.call-start = ((), (), s32[]{:S(2)}) async-start(), calls=%async_computation.1 | async-start | bytes 1081344 | tf_op jit(solution)/shard_map/all_gather | solution.py:120
  8.6 4.8 %copy-start.7 = (bf16[1,2,256,256]{3,2,1,0:T(8,128)(2,1)S(1)}, bf16[1,2,256,256]{3,2,1,0:T(8,128)(2,1)}, u32[]{:S(2)}) copy-start(bf16[1,2,256,256]{3,2,1,0:T(8,128)(2,1)} %param.18) | copy-start | bytes 786436
  13.3 4.9 %copy-start.8 = (bf16[256,8192]{1,0:T(8,128)(2,1)}, bf16[256,8192]{1,0:T(8,128)(2,1)S(1)}, u32[]{:S(2)}) copy-start(bf16[256,8192]{1,0:T(8,128)(2,1)S(1)} %get-tuple-element.217) | copy-start | bytes 12582916
  18.2 4.9 %copy-start.10 = (bf16[256,8192]{1,0:T(8,128)(2,1)}, bf16[256,8192]{1,0:T(8,128)(2,1)S(1)}, u32[]{:S(2)}) copy-start(bf16[256,8192]{1,0:T(8,128)(2,1)S(1)} %get-tuple-element.219) | copy-start | bytes 12582916
  18.2 6.9 %copy-start.6 = (bf16[1,256,4]{1,2,0:T(4,128)(2,1)S(1)}, bf16[1,256,4]{1,2,0:T(4,128)(2,1)}, u32[]{:S(2)}) copy-start(bf16[1,256,4]{1,2,0:T(4,128)(2,1)} %param.19) | copy-start | bytes 6148
  18.2 7.7 %copy-start.3 = (f32[1,4,2048]{2,1,0:T(4,128)S(1)}, f32[1,4,2048]{2,1,0:T(4,128)}, u32[]{:S(2)}) copy-start(f32[1,4,2048]{2,1,0:T(4,128)} %param.13) | copy-start | bytes 98308
  18.2 7.7 %copy-start.5 = (s32[1,2048]{1,0:T(1,128)S(1)}, s32[1,2048]{1,0:T(1,128)}, u32[]{:S(2)}) copy-start(s32[1,2048]{1,0:T(1,128)} %param.14) | copy-start | bytes 24580
  23.1 2.0 copy-start.2
  23.1 80.8 %copy-start.1 = (s32[2048,32]{0,1:T(8,128)S(1)}, s32[2048,32]{0,1:T(8,128)}, u32[]{:S(2)}) copy-start(s32[2048,32]{0,1:T(8,128)} %param.15) | copy-start | bytes 786436
  23.1 87.2 %copy-start.4 = (f32[3,2048]{1,0:T(4,128)S(1)}, f32[3,2048]{1,0:T(4,128)}, u32[]{:S(2)}) copy-start(f32[3,2048]{1,0:T(4,128)} %param.16) | copy-start | bytes 73732
  27.0 182.9 %all-reduce.3.cloned.1.call-start = ((), (), s32[]{:S(2)}) async-start(), calls=%async_computation | async-start | bytes 1048576 | tf_op jit(solution)/shard_map/psum | solution.py:134
  119.1 5.9 %copy-start.11 = (bf16[256,8192]{1,0:T(8,128)(2,1)S(1)}, bf16[256,8192]{1,0:T(8,128)(2,1)}, u32[]{:S(2)}) copy-start(bf16[256,8192]{1,0:T(8,128)(2,1)} %copy-done.10) | copy-start | bytes 12582916
  126.2 6.1 %copy-start.9 = (bf16[256,8192]{1,0:T(8,128)(2,1)S(1)}, bf16[256,8192]{1,0:T(8,128)(2,1)}, u32[]{:S(2)}) copy-start(bf16[256,8192]{1,0:T(8,128)(2,1)} %copy-done.8) | copy-start | bytes 12582916
  132.3 2.0 copy-start.12
Sparse Core Ops, SparseCore 0:
  27.1 75.1 all-gather.3
  143.3 66.5 all-reduce.2
where the time goes:
time: 220 us; the launch traced here: 219 us
  waiting for transfers between devices  111 us (50%)
  matrix products  40.9 us (19%)
  blocking collectives  27.6 us (13%)
  between operations  14.4 us (7%)
  other arithmetic  12.2 us (6%)
  local copies, waits for them, and re-layouts  9.77 us (4%)
  loops' own time  2.72 us (1%)
    all_gather x1, waiting for transfers between devices, per_device(): segments = lax.all_gather(payload[None], 'vol', axis=0, tiled=True)  75.2 us
    psum x1, waiting for transfers between devices, per_device(): lax.psum((first_grad, middle_grad, last_grad), 'rep')  35.7 us
    psum x1, blocking collectives, per_device(): lax.psum((first_grad, middle_grad, last_grad), 'rep')  27.6 us
    dot_general x4, matrix products, contract_first(): lax.dot_general(matrix, rows, (((0,), (0,)), ((), ())), preferred_element...  15.1 us
    dot_general x4, matrix products, contract_last(): lax.dot_general(left, right, (((1,), (1,)), ((), ())), preferred_element_...  13.9 us
    unnamed x33, local copies, waits for them, and re-layouts  6.07 us
    dot_general x1, matrix products, network_gradients(): jnp.dot(middle_weight[depth], back, preferred_element_type=jnp.float32)  6.04 us
    dot_general x1, matrix products, network_gradients(): jnp.dot(last_weight, head_grad, preferred_element_type=jnp.float32)  5.83 us
  transfers between devices with their start and end apart: 2, of which 2 were waited for; matrix products, arithmetic and copies ran while one was open for 2% of the time, Pallas kernels for 0%

commit v1 on v0

v1 whole, which is shorter than its diff:
```python
import functools

import jax
import jax.numpy as jnp
from jax import lax
from jax.experimental import pallas as pl
from jax.experimental.pallas import tpu as pltpu
from jax.sharding import Mesh, PartitionSpec as P

F32 = jnp.float32
BF16 = jnp.bfloat16
CHUNKS = 2
TILE = 256
SAMP = 4
FEAT = 32
W = 256
NV = 32


def dot(lhs, rhs, lhs_dim, rhs_dim, precision=None):
    return lax.dot_general(
        lhs, rhs, (((lhs_dim,), (rhs_dim,)), ((), ())),
        preferred_element_type=F32, precision=precision,
    )


def group_rows(rows, width):
    i = lax.broadcasted_iota(jnp.int32, (rows, width), 0)
    j = lax.broadcasted_iota(jnp.int32, (rows, width), 1)
    return lax.shift_right_logical(i, 2) == j


def spread(block, fill):
    row = lax.broadcasted_iota(jnp.int32, block.shape, 0)
    parts = [jnp.where((row & 3) == s, block, fill) for s in range(SAMP)]
    return jnp.concatenate(parts, axis=1)


def lane_rows(value):
    return [value[:, 128 * i : 128 * (i + 1)] for i in range(value.shape[1] // 128)]


def forward_kernel(
    x_ref, delta_ref, count_ref, cot_ref, w1_ref, wm_ref, w4_ref,
    save_ref, ab_ref, pay_ref, w1t, wmt, w4t, rows,
):
    step = pl.program_id(0)
    tile = x_ref.shape[1]

    @pl.when(step == 0)
    def _():
        pick = group_rows(FEAT * SAMP, FEAT).astype(BF16)
        w1t[...] = (dot(w1_ref[...], pick, 0, 1) * 0.5).astype(BF16)
        for k in range(2):
            wmt[k] = (wm_ref[k].astype(F32).T * 0.5).astype(BF16)
        pick4 = group_rows(4 * SAMP, 4).astype(BF16)
        w4t[...] = dot(pick4, w4_ref[...], 1, 1).astype(BF16)

    wide = spread(x_ref[...], jnp.zeros((), BF16))
    half = dot(w1t[...], wide, 1, 0)
    for k in range(3):
        bent = 1.0 + jnp.tanh(half)
        hid = half * bent
        slope = bent + hid * (2.0 - bent)
        hidden = hid.astype(BF16)
        save_ref[k] = hidden
        save_ref[3 + k] = slope.astype(BF16)
        if k < 2:
            half = dot(wmt[k], hidden, 1, 0)
    row16 = lax.broadcasted_iota(jnp.int32, (4 * SAMP, W), 0) & 3
    head = jnp.zeros((4 * SAMP, tile), F32)
    for s in range(SAMP):
        head += dot(
            jnp.where(row16 == s, w4t[...], jnp.zeros((), BF16)),
            hidden[:, s * tile : (s + 1) * tile], 1, 0,
        )

    logistic = jax.nn.sigmoid(head)
    density = jnp.maximum(head[:4], 0.0) + jnp.log1p(jnp.exp(-jnp.abs(head[:4])))
    live = lax.broadcasted_iota(jnp.int32, (SAMP, tile), 0) < count_ref[...]
    span = jnp.where(live, delta_ref[...], 0.0)
    optical = density * span
    sums = [optical[0:1]]
    for s in range(1, SAMP):
        sums.append(sums[-1] + optical[s : s + 1])
    reached = jnp.concatenate(sums, axis=0)
    leaving = jnp.exp(-reached)
    entering = jnp.concatenate([jnp.ones((1, tile), F32), leaving[:3]], axis=0)
    share = entering - leaving
    cot = cot_ref[...]
    parts = []
    facing = jnp.zeros((SAMP, tile), F32)
    for c in range(3):
        albedo = logistic[4 * (c + 1) : 4 * (c + 2)]
        lit = cot[c : c + 1] * albedo
        facing += lit
        parts.append(share * lit * (1.0 - albedo))
    weighted = facing * share
    total = weighted[3:4]
    later = [jnp.zeros((1, tile), F32), total]
    for s in (2, 1):
        total = total + weighted[s : s + 1]
        later.append(total)
    whole = total + weighted[0:1]
    later = jnp.concatenate(later[::-1], axis=0)
    own = span * logistic[:4]
    ab_ref[...] = jnp.concatenate(
        [(facing * leaving - later) * own] + parts + [own, jnp.zeros((4, tile), F32)], axis=0
    )
    per = tile // 128
    for i, (a, b) in enumerate(zip(lane_rows(-sums[-1]), lane_rows(whole))):
        rows[pl.ds(step * per + i, 1), :] = a
        rows[pl.ds(8 + step * per + i, 1), :] = b

    @pl.when(step == pl.num_programs(0) - 1)
    def _():
        pay_ref[...] = jnp.broadcast_to(rows[...][None], pay_ref.shape)


def backward_kernel(last, first, *refs):
    refs = list(refs)
    place_ref = refs.pop(0)
    save_ref, ab_ref, x_ref, got_ref, rank_ref, wm_ref, w4_ref = refs[:7]
    refs = refs[7:]
    if not first:
        before = refs[:3]
        refs = refs[3:]
    if last:
        keep_ref, send_ref = refs[:2]
        refs = refs[2:]
        front, own, mids, firsts, lasts = refs
    else:
        mids, firsts, lasts, front, own = refs
    step = pl.program_id(0)
    tile = x_ref.shape[1]

    @pl.when(step == 0)
    def _():
        if first:
            mids[...] = jnp.zeros_like(mids)
            firsts[...] = jnp.zeros_like(firsts)
            lasts[...] = jnp.zeros_like(lasts)
        else:
            mids[...] = before[0][...]
            firsts[...] = before[1][...]
            lasts[...] = before[2][...]

        def one(v, _):
            mine = rank_ref[v]
            total = jnp.zeros((8, 128), F32)
            for u in range(NV):
                total += jnp.where(rank_ref[u] < mine, got_ref[u, :8], 0.0)
            front[v] = jnp.exp(total)
            return 0

        lax.fori_loop(0, NV, one, 0)
        me = place_ref[0]
        mine = rank_ref[me]
        behind = jnp.zeros((8, 128), F32)
        for u in range(NV):
            behind += jnp.where(rank_ref[u] > mine, front[u] * got_ref[u, 8:], 0.0)
        own[:8] = front[me]
        own[8:] = behind

    per = tile // 128
    prefix = jnp.concatenate([own[pl.ds(step * per + i, 1), :] for i in range(per)], axis=1)
    behind = jnp.concatenate([own[pl.ds(8 + step * per + i, 1), :] for i in range(per)], axis=1)
    ghead = ab_ref[:16] * prefix
    ghead = jnp.concatenate([ghead[:4] - ab_ref[16:20] * behind, ghead[4:]], axis=0)
    ghead = spread(ghead.astype(BF16), jnp.zeros((), BF16))

    pick4 = (group_rows(4 * SAMP, 4).astype(F32) * 0.5).astype(BF16)
    lasts[...] += dot(save_ref[2], ghead, 1, 1)
    back = dot(dot(w4_ref[...], pick4, 1, 1).astype(BF16), ghead, 1, 0)
    back = (back * save_ref[5].astype(F32)).astype(BF16)
    for k in (1, 0):
        mids[k] += dot(save_ref[k], back, 1, 1)
        halved = (wm_ref[k].astype(F32) * 0.5).astype(BF16)
        back = (dot(halved, back, 1, 0) * save_ref[3 + k].astype(F32)).astype(BF16)
    firsts[...] += dot(spread(x_ref[...], jnp.zeros((), BF16)), back, 1, 1)

    if last:

        @pl.when(step == pl.num_programs(0) - 1)
        def _():
            highest = lax.Precision.HIGHEST
            pick = group_rows(FEAT * SAMP, FEAT).astype(F32)
            small = dot(pick, firsts[...], 0, 0, highest)
            pick8 = group_rows(4 * SAMP, 8).astype(F32)
            tail = dot(pick8, lasts[...], 0, 1, highest)
            for side in range(2):
                cols = slice(128 * side, 128 * (side + 1))

                def fill(ref):
                    ref[0:256, :] = mids[1][:, cols]
                    ref[256:512, :] = mids[0][:, cols]
                    ref[512:544, :] = small[:, cols]
                    ref[544:552, :] = tail[:, cols]

                @pl.when(place_ref[1] == side)
                def _():
                    fill(keep_ref)

                @pl.when(place_ref[1] != side)
                def _():
                    fill(send_ref)


def unpack_kernel(place_ref, mine_ref, other_ref, first_ref, mid_ref, last_ref):
    for side in range(2):
        cols = slice(128 * side, 128 * (side + 1))

        def emit(ref):
            mid_ref[1, :, cols] = ref[0:256, :]
            mid_ref[0, :, cols] = ref[256:512, :]
            first_ref[:, cols] = ref[512:544, :]
            last_ref[cols, :] = ref[544:552, :].T[:, :4]

        @pl.when(place_ref[0] == side)
        def _():
            emit(mine_ref)

        @pl.when(place_ref[0] != side)
        def _():
            emit(other_ref)


LIMIT = 48 * 1024 * 1024


def forward(chunk, x, deltas, counts, cot, w1, wm, w4):
    rays = x.shape[1] // CHUNKS
    steps = rays // TILE
    at = chunk * steps
    whole2 = lambda i: (0, 0)
    return pl.pallas_call(
        forward_kernel,
        grid=(steps,),
        in_specs=[
            pl.BlockSpec((FEAT * SAMP, TILE), lambda i: (0, at + i)),
            pl.BlockSpec((SAMP, TILE), lambda i: (0, at + i)),
            pl.BlockSpec((1, TILE), lambda i: (0, at + i)),
            pl.BlockSpec((3, TILE), lambda i: (0, at + i)),
            pl.BlockSpec((FEAT, W), whole2),
            pl.BlockSpec((2, W, W), lambda i: (0, 0, 0)),
            pl.BlockSpec((W, 4), whole2),
        ],
        out_specs=[
            pl.BlockSpec((6, W, SAMP * TILE), lambda i: (0, 0, i)),
            pl.BlockSpec((24, TILE), lambda i: (0, i)),
            pl.BlockSpec((NV, 16, 128), lambda i: (0, 0, 0)),
        ],
        out_shape=[
            jax.ShapeDtypeStruct((6, W, SAMP * rays), BF16),
            jax.ShapeDtypeStruct((24, rays), F32),
            jax.ShapeDtypeStruct((NV, 16, 128), F32),
        ],
        scratch_shapes=[
            pltpu.VMEM((W, FEAT * SAMP), BF16),
            pltpu.VMEM((2, W, W), BF16),
            pltpu.VMEM((4 * SAMP, W), BF16),
            pltpu.VMEM((16, 128), F32),
        ],
        compiler_params=pltpu.CompilerParams(vmem_limit_bytes=LIMIT),
        cost_estimate=pl.CostEstimate(
            flops=2 * SAMP * rays * 140288, transcendentals=3 * W * SAMP * rays,
            bytes_accessed=13 * 2**20,
        ),
        name=f"forward{chunk}",
    )(x, deltas, counts, cot, w1, wm, w4)


def backward(chunk, place, saved, x, got, ranks, wm, w4, before):
    save, ab = saved
    rays = ab.shape[1]
    steps = rays // TILE
    at = chunk * steps
    first, last = chunk == 0, chunk == CHUNKS - 1
    sums = [
        ((2, W, W), F32),
        ((FEAT * SAMP, W), F32),
        ((W, 4 * SAMP), F32),
    ]
    const = lambda nd: (lambda i, p: (0,) * nd)
    sum_specs = [pl.BlockSpec(shape, const(len(shape))) for shape, _ in sums]
    in_specs = [
        pl.BlockSpec((6, W, SAMP * TILE), lambda i, p: (0, 0, i)),
        pl.BlockSpec((24, TILE), lambda i, p: (0, i)),
        pl.BlockSpec((FEAT * SAMP, TILE), lambda i, p: (0, at + i)),
        pl.BlockSpec((NV, 16, 128), const(3)),
        pl.BlockSpec((NV, 8, 128), lambda i, p: (0, chunk, 0)),
        pl.BlockSpec((2, W, W), const(3)),
        pl.BlockSpec((W, 4), const(2)),
    ]
    scratch = [pltpu.VMEM((NV, 8, 128), F32), pltpu.VMEM((16, 128), F32)]
    if not first:
        in_specs += sum_specs
    if last:
        out_specs = [pl.BlockSpec((552, 128), const(2))] * 2
        out_shape = [jax.ShapeDtypeStruct((552, 128), F32)] * 2
        scratch += [pltpu.VMEM(shape, kind) for shape, kind in sums]
    else:
        out_specs = sum_specs
        out_shape = [jax.ShapeDtypeStruct(shape, kind) for shape, kind in sums]
    return pl.pallas_call(
        functools.partial(backward_kernel, last, first),
        grid_spec=pltpu.PrefetchScalarGridSpec(
            num_scalar_prefetch=1, grid=(steps,), in_specs=in_specs, out_specs=out_specs,
            scratch_shapes=scratch,
        ),
        out_shape=out_shape,
        compiler_params=pltpu.CompilerParams(vmem_limit_bytes=LIMIT),
        cost_estimate=pl.CostEstimate(
            flops=2 * SAMP * rays * 280000, transcendentals=0, bytes_accessed=13 * 2**20
        ),
        name=f"backward{chunk}",
    )(place, save, ab, x, got, ranks, wm, w4, *before)


PAIR = [(0, 1), (1, 0)]
NEAR = [(0, 1), (1, 0), (2, 3), (3, 2)]
FAR = [(0, 3), (3, 0), (1, 2), (2, 1)]


def per_device(
    features, deltas, counts, order_rank, cotangent, first_weight, middle_weight, last_weight
):
    x = features[0].reshape(FEAT * SAMP, -1)
    core = lax.axis_index("core")
    place = jnp.stack([lax.axis_index(("z", "y")), core]).astype(jnp.int32)
    ranks = order_rank.T.reshape(NV, -1, 128)
    w1, wm, w4 = first_weight[0], middle_weight[0], last_weight[0]
    saved, got = [], []
    for chunk in range(CHUNKS):
        save, ab, pay = forward(chunk, x, deltas[0], counts, cotangent, w1, wm, w4)
        saved.append((save, ab))
        got.append(lax.all_to_all(pay, ("z", "y"), 0, 0, tiled=True))
    sums = ()
    for chunk in range(CHUNKS):
        sums = backward(chunk, place, saved[chunk], x, got[chunk], ranks, wm, w4, sums)
    keep, send = sums
    keep = keep + lax.ppermute(send, "core", PAIR)
    a, b = keep[:280], keep[280:]
    a, b = a + lax.ppermute(a, "x", NEAR), b + lax.ppermute(b, "x", FAR)
    a, b = a + lax.ppermute(a, "x", FAR), b + lax.ppermute(b, "x", NEAR)
    mine = jnp.concatenate([a, b], axis=0)
    other = lax.ppermute(mine, "core", PAIR)
    first, mid, tail = pl.pallas_call(
        unpack_kernel,
        grid_spec=pltpu.PrefetchScalarGridSpec(
            num_scalar_prefetch=1, grid=(1,),
            in_specs=[pl.BlockSpec((552, 128), lambda i, p: (0, 0))] * 2,
            out_specs=[
                pl.BlockSpec((FEAT, W), lambda i, p: (0, 0)),
                pl.BlockSpec((2, W, W), lambda i, p: (0, 0, 0)),
                pl.BlockSpec((W, 4), lambda i, p: (0, 0)),
            ],
        ),
        out_shape=[
            jax.ShapeDtypeStruct((FEAT, W), F32),
            jax.ShapeDtypeStruct((2, W, W), F32),
            jax.ShapeDtypeStruct((W, 4), F32),
        ],
        name="unpack",
    )(core.reshape(1).astype(jnp.int32), mine, other)
    return (first[None], mid[None], tail[None])


def solution(mesh):
    fine = Mesh(mesh.devices.reshape(8, 4, 4, 2), ("z", "y", "x", "core"))
    vol, rep = ("z", "y"), ("x", "core")
    placed = (
        P(vol, None, None, rep),
        P(vol, None, rep),
        P(vol, rep),
        P(rep, None),
        P(None, rep),
        P(vol, None, None),
        P(vol, None, None, None),
        P(vol, None, None),
    )
    return jax.shard_map(
        per_device,
        mesh=fine,
        in_specs=placed,
        out_specs=(P(vol, None, None), P(vol, None, None, None), P(vol, None, None)),
        check_vma=False,
    )
```

time: 220 us -> 94 us (0.43)
  waiting for transfers between devices: 111 us -> 8.38 us
  matrix products: 40.9 us -> 0 us
  Pallas kernels: 0 us -> 38.6 us
  starting transfers between devices: 0.08 us -> 32.8 us
  blocking collectives: 27.6 us -> 0 us
  between operations: 14.4 us -> 0.81 us
  other arithmetic: 12.2 us -> 0.21 us
  loops' own time: 2.72 us -> 0 us
  local copies, waits for them, and re-layouts: 9.77 us -> 12.2 us
    all_gather x1 -> x0, waiting for transfers between devices: 75.2 us -> none  [per_device(): segments = lax.all_gather(payload[None], 'vol', axis=0, tiled=True)]
    dot_general x10 -> x0, matrix products: 40.9 us -> none  [the longest x4 15.1 us: contract_first(): lax.dot_general(matrix, rows, (((0,), (0,)), ((), ())), preferred_element...]
    pallas_call x0 -> x5, Pallas kernels: none -> 38.6 us  [the longest x2 21.4 us: backward(): pl.pallas_call(functools.partial(backward_kernel, last, first), grid_spec...]
    psum x1 -> x0, waiting for transfers between devices: 35.7 us -> none  [per_device(): lax.psum((first_grad, middle_grad, last_grad), 'rep')]
    psum x1 -> x0, blocking collectives: 27.6 us -> none  [per_device(): lax.psum((first_grad, middle_grad, last_grad), 'rep')]
    all_to_all x0 -> x2, starting transfers between devices: none -> 21.2 us  [per_device(): got.append(lax.all_to_all(pay, ('z', 'y'), 0, 0, tiled=True))]
    ppermute x0 -> x6, starting transfers between devices: none -> 11.6 us  [the longest x2 3.22 us: per_device(): a, b = (a + lax.ppermute(a, 'x', NEAR), b + lax.ppermute(b, 'x', FAR))]
    ppermute x0 -> x6, waiting for transfers between devices: none -> 8.38 us  [the longest x2 4.19 us: per_device(): a, b = (a + lax.ppermute(a, 'x', FAR), b + lax.ppermute(b, 'x', NEAR))]
  transfers between devices with their start and end apart: 2 -> 8, of which waited for: 2 -> 4; matrix products, arithmetic and copies ran while one was open for 2% -> 0% of each run, Pallas kernels for 0% -> 19%
where the time goes in v1:
time: 94 us; the launch traced here: 93 us
  Pallas kernels  38.6 us (41%)
  starting transfers between devices  32.8 us (35%)
  local copies, waits for them, and re-layouts  12.2 us (13%)
  waiting for transfers between devices  8.38 us (9%)
    pallas_call x2, Pallas kernels, backward(): pl.pallas_call(functools.partial(backward_kernel, last, first), grid_spec...  21.4 us
    all_to_all x2, starting transfers between devices, per_device(): got.append(lax.all_to_all(pay, ('z', 'y'), 0, 0, tiled=True))  21.2 us
    pallas_call x2, Pallas kernels, forward(): pl.pallas_call(forward_kernel, grid=(steps,), in_specs=[pl.BlockSpec((FEA...  15.2 us
    unnamed x31, local copies, waits for them, and re-layouts  11 us
    ppermute x2, waiting for transfers between devices, per_device(): a, b = (a + lax.ppermute(a, 'x', FAR), b + lax.ppermute(b, 'x', NEAR))  4.19 us
    ppermute x2, starting transfers between devices, per_device(): a, b = (a + lax.ppermute(a, 'x', NEAR), b + lax.ppermute(b, 'x', FAR))  3.22 us
    ppermute x1, starting transfers between devices, per_device(): keep = keep + lax.ppermute(send, 'core', PAIR)  3.22 us
    ppermute x2, starting transfers between devices, per_device(): a, b = (a + lax.ppermute(a, 'x', FAR), b + lax.ppermute(b, 'x', NEAR))  2.67 us
  transfers between devices with their start and end apart: 8, of which 4 were waited for; matrix products, arithmetic and copies ran while one was open for 0% of the time, Pallas kernels for 19%

profile of v1, /device:TPU:1, one launch (start us, length us, event | category | flops | bytes accessed | tf_op | source)
XLA Modules:
  0.0 93.0 jit_solution(5100612532416592690)
XLA Ops:
  0.7 0.9 copy.11
  1.5 1.2 %reshape_squeeze.3.x_ref.refs_3_ = bf16[128,2048]{1,0:T(8,128)(2,1)S(1)} reshape(bf16[1,32,4,2048]{3,2,1,0:T(4,128)(2,1)} %param.8) | data formatting | bytes 1048576 | tf_op jit(solution)/shard_map/reshape;squeeze | solution.py:328
  2.7 0.9 %copy-done = bf16[1,2,256,256]{3,2,1,0:T(8,128)(2,1)S(1)} copy-done((bf16[1,2,256,256]{3,2,1,0:T(8,128)(2,1)S(1)}, bf16[1,2,256,256]{3,2,1,0:T(8,128)(2,1)}, u32[]{:S(2)}) %copy-start) | copy-done | bytes 262168
  3.6 0.8 copy-done.3
  6.6 7.7 %forward0.1 = (bf16[6,256,4096]{2,1,0:T(8,128)(2,1)}, f32[24,1024]{1,0:T(8,128)S(1)}, f32[32,16,128]{2,1,0:T(8,128)}) custom-call(bf16[128,2048]{1,0:T(8,128)(2,1)S(1)} %reshape_squeeze.3.x_ref.refs_3_, f32[4,2048]{1,0:T(4,128)S(1)} %bitcast.22, s32[1,2048]{1,0:T(1,128)S(1)} %copy-done.9, f32[3,2048]{1,0:T(4,128)S(1)} %copy-done.5, ...), custom_call_target="tpu_custom_call" | custom-call | flops 1149239296 | bytes 13631488 | tf_op jit(solution)/shard_map/forward0/pallas_call | solution.py:236
  14.2 12.0 %all-to-all-start.1 = ((f32[32,16,128]{2,1,0:T(8,128)}), f32[32,16,128]{2,1,0:T(8,128)S(1)}, u32[]{:S(2)}, u32[]{:S(2)}) async-start(f32[32,16,128]{2,1,0:T(8,128)} %get-tuple-element.22), calls=%async_computation.1 | async-start | bytes 524288 | tf_op jit(solution)/shard_map/all_to_all | solution.py:337
  26.3 0.9 %copy-done.1 = bf16[1,2,256,256]{3,2,1,0:T(8,128)(2,1)S(1)} copy-done((bf16[1,2,256,256]{3,2,1,0:T(8,128)(2,1)S(1)}, bf16[1,2,256,256]{3,2,1,0:T(8,128)(2,1)}, u32[]{:S(2)}) %copy-start.1) | copy-done | bytes 262168
  27.2 0.8 copy-done.4
  28.0 0.8 copy-done.6
  30.2 7.5 %forward1.1 = (bf16[6,256,4096]{2,1,0:T(8,128)(2,1)}, f32[24,1024]{1,0:T(8,128)S(1)}, f32[32,16,128]{2,1,0:T(8,128)}) custom-call(bf16[128,2048]{1,0:T(8,128)(2,1)S(1)} %reshape_squeeze.3.x_ref.refs_3_, f32[4,2048]{1,0:T(4,128)S(1)} %bitcast.23, s32[1,2048]{1,0:T(1,128)S(1)} %copy-done.10, f32[3,2048]{1,0:T(4,128)S(1)} %copy-done.6, ...), custom_call_target="tpu_custom_call" | custom-call | flops 1149239296 | bytes 13631488 | tf_op jit(solution)/shard_map/forward1/pallas_call | solution.py:236
  37.7 9.2 %all-to-all-start = ((f32[32,16,128]{2,1,0:T(8,128)}), f32[32,16,128]{2,1,0:T(8,128)S(1)}, u32[]{:S(2)}, u32[]{:S(2)}) async-start(f32[32,16,128]{2,1,0:T(8,128)} %get-tuple-element.19), calls=%async_computation | async-start | bytes 524288 | tf_op jit(solution)/shard_map/all_to_all | solution.py:337
  47.0 10.5 %backward0.1 = (f32[2,256,256]{2,1,0:T(8,128)S(1)}, f32[128,256]{1,0:T(8,128)S(1)}, f32[256,16]{1,0:T(8,128)S(1)}) custom-call(s32[2]{0:T(128)S(1)} %pad_add_fusion.refs_0_, bf16[6,256,4096]{2,1,0:T(8,128)(2,1)} %get-tuple-element.20.refs_1_, f32[24,1024]{1,0:T(8,128)S(1)} %get-tuple-element.21.refs_2_, bf16[128,2048]{1,0:T(8,128)(2,1)S(1)} %reshape_squeeze.3.x_ref.refs_3_, ...), custom_call_target="tpu_custom_call" | custom-call | flops 2293760000 | bytes 13631488 | tf_op jit(solution)/shard_map/backward0/pallas_call | solution.py:305
  57.6 10.9 %backward1.1 = (f32[552,128]{1,0:T(8,128)S(1)}, f32[552,128]{1,0:T(8,128)S(1)}) custom-call(s32[2]{0:T(128)S(1)} %pad_add_fusion.refs_0_, bf16[6,256,4096]{2,1,0:T(8,128)(2,1)} %get-tuple-element.17.refs_1_, f32[24,1024]{1,0:T(8,128)S(1)} %get-tuple-element.18.refs_2_, bf16[128,2048]{1,0:T(8,128)(2,1)S(1)} %reshape_squeeze.3.x_ref.refs_3_, ...), custom_call_target="tpu_custom_call" | custom-call | flops 2293760000 | bytes 13631488 | tf_op jit(solution)/shard_map/backward1/pallas_call | solution.py:305
  68.5 3.2 %collective-permute-start = (f32[552,128]{1,0:T(8,128)S(1)}, f32[552,128]{1,0:T(8,128)S(1)}, u32[]{:S(2)}, u32[]{:S(2)}) collective-permute-start(f32[552,128]{1,0:T(8,128)S(1)} %get-tuple-element.27), channel_id=1, source_target_pairs={{0,1},{1,0},{2,3},{3,2},{4,5},{5,4},{6,7},{7,6},{8,9},{9,8},{10,11... | collective-permute-start | bytes 847880 | tf_op jit(solution)/shard_map/ppermute | solution.py:342
  71.7 1.2 %collective-permute-done = f32[552,128]{1,0:T(8,128)S(1)} collective-permute-done((f32[552,128]{1,0:T(8,128)S(1)}, f32[552,128]{1,0:T(8,128)S(1)}, u32[]{:S(2)}, u32[]{:S(2)}) %collective-permute-start) | collective-permute-done | bytes 282656 | tf_op jit(solution)/shard_map/ppermute | solution.py:342
  72.9 1.3 %collective-permute-start.1 = (f32[280,128]{1,0:T(8,128)S(1)}, f32[280,128]{1,0:T(8,128)S(1)}, u32[]{:S(2)}, u32[]{:S(2)}) collective-permute-start(f32[280,128]{1,0:T(8,128)S(1)} %slice.8), channel_id=1, source_target_pairs={{0,2},{2,0},{4,6},{6,4},{1,3},{3,1},{5,7},{7,5},{8,10},{10,8},{12,... | collective-permute-start | bytes 430088 | tf_op jit(solution)/shard_map/ppermute | solution.py:344
  74.3 1.9 %collective-permute-start.3 = (f32[272,128]{1,0:T(8,128)S(1)}, f32[272,128]{1,0:T(8,128)S(1)}, u32[]{:S(2)}, u32[]{:S(2)}) collective-permute-start(f32[272,128]{1,0:T(8,128)S(1)} %slice.9), channel_id=1, source_target_pairs={{0,6},{6,0},{2,4},{4,2},{1,7},{7,1},{3,5},{5,3},{8,14},{14,8},{10,... | collective-permute-start | bytes 417800 | tf_op jit(solution)/shard_map/ppermute | solution.py:344
  76.2 1.8 %collective-permute-done.1 = f32[280,128]{1,0:T(8,128)S(1)} collective-permute-done((f32[280,128]{1,0:T(8,128)S(1)}, f32[280,128]{1,0:T(8,128)S(1)}, u32[]{:S(2)}, u32[]{:S(2)}) %collective-permute-start.1) | collective-permute-done | bytes 143392 | tf_op jit(solution)/shard_map/ppermute | solution.py:344
  78.0 2.6 %collective-permute-start.2 = (f32[280,128]{1,0:T(8,128)S(1)}, f32[280,128]{1,0:T(8,128)S(1)}, u32[]{:S(2)}, u32[]{:S(2)}) collective-permute-start(f32[280,128]{1,0:T(8,128)S(1)} %slice_add_fusion.1), channel_id=1, source_target_pairs={{0,6},{6,0},{2,4},{4,2},{1,7},{7,1},{3,5},{5,3},{8,14},{14,8},{10,... | collective-permute-start | bytes 430088 | tf_op jit(solution)/shard_map/ppermute | solution.py:345
  80.7 4.2 %collective-permute-done.4 = f32[272,128]{1,0:T(8,128)S(1)} collective-permute-done((f32[272,128]{1,0:T(8,128)S(1)}, f32[272,128]{1,0:T(8,128)S(1)}, u32[]{:S(2)}, u32[]{:S(2)}) %collective-permute-start.4) | collective-permute-done | bytes 139296 | tf_op jit(solution)/shard_map/ppermute | solution.py:345
  85.0 2.5 %collective-permute-start.5 = (f32[552,128]{1,0:T(8,128)S(1)}, f32[552,128]{1,0:T(8,128)S(1)}, u32[]{:S(2)}, u32[]{:S(2)}) collective-permute-start(f32[552,128]{1,0:T(8,128)S(1)} %pad_maximum_fusion.mine_ref), channel_id=1, source_target_pairs={{0,1},{1,0},{2,3},{3,2},{4,5},{5,4},{6,7},{7,6},{8,9},{9,8},{10,11... | collective-permute-start | bytes 847880 | tf_op jit(solution)/shard_map/ppermute | solution.py:347
  87.4 1.2 %collective-permute-done.5.other_ref = f32[552,128]{1,0:T(8,128)S(1)} collective-permute-done((f32[552,128]{1,0:T(8,128)S(1)}, f32[552,128]{1,0:T(8,128)S(1)}, u32[]{:S(2)}, u32[]{:S(2)}) %collective-permute-start.5) | collective-permute-done | bytes 282656 | tf_op jit(solution)/shard_map/ppermute | solution.py:347
  89.4 2.1 %unpack.1 = (f32[32,256]{1,0:T(8,128)}, f32[2,256,256]{2,1,0:T(8,128)}, f32[256,4]{1,0:T(8,128)}) custom-call(s32[1]{0:T(128)} %bitcast.place_ref, f32[552,128]{1,0:T(8,128)} %copy-done.11, f32[552,128]{1,0:T(8,128)} %copy-done.12), custom_call_target="tpu_custom_call" | custom-call | tf_op jit(solution)/shard_map/unpack/pallas_call | solution.py:348
  91.4 1.6 %copy.12 = f32[1,256,4]{1,2,0:T(4,128)} copy(f32[1,256,4]{2,1,0:T(8,128)} %bitcast.27) | data formatting | bytes 8192
  (38 shorter events, 4.7 us)
Async XLA Ops:
  0.6 46.4 %copy-start.2 = (bf16[1,2,256,256]{3,2,1,0:T(8,128)(2,1)S(1)}, bf16[1,2,256,256]{3,2,1,0:T(8,128)(2,1)}, u32[]{:S(2)}) copy-start(bf16[1,2,256,256]{3,2,1,0:T(8,128)(2,1)} %param.14) | copy-start | bytes 786436
  0.6 46.2 %copy-start.13 = (s32[2048,32]{0,1:T(8,128)S(1)}, s32[2048,32]{0,1:T(8,128)}, u32[]{:S(2)}) copy-start(s32[2048,32]{0,1:T(8,128)} %param.11) | copy-start | bytes 786436
  2.7 1.0 %copy-start = (bf16[1,2,256,256]{3,2,1,0:T(8,128)(2,1)S(1)}, bf16[1,2,256,256]{3,2,1,0:T(8,128)(2,1)}, u32[]{:S(2)}) copy-start(bf16[1,2,256,256]{3,2,1,0:T(8,128)(2,1)} %param.14) | copy-start | bytes 786436
  3.6 0.8 copy-start.3
  4.4 0.8 copy-start.5
  5.2 0.7 copy-start.7
  5.9 0.7 copy-start.9
  14.2 23.4 %all-to-all-start.1 = ((f32[32,16,128]{2,1,0:T(8,128)}), f32[32,16,128]{2,1,0:T(8,128)S(1)}, u32[]{:S(2)}, u32[]{:S(2)}) async-start(f32[32,16,128]{2,1,0:T(8,128)} %get-tuple-element.22), calls=%async_computation.1 | async-start | bytes 524288 | tf_op jit(solution)/shard_map/all_to_all | solution.py:337
  26.3 1.0 %copy-start.1 = (bf16[1,2,256,256]{3,2,1,0:T(8,128)(2,1)S(1)}, bf16[1,2,256,256]{3,2,1,0:T(8,128)(2,1)}, u32[]{:S(2)}) copy-start(bf16[1,2,256,256]{3,2,1,0:T(8,128)(2,1)} %param.14) | copy-start | bytes 786436
  27.2 0.8 copy-start.4
  28.0 0.8 copy-start.6
  28.7 0.7 copy-start.8
  29.5 0.7 copy-start.10
  37.7 19.9 %all-to-all-start = ((f32[32,16,128]{2,1,0:T(8,128)}), f32[32,16,128]{2,1,0:T(8,128)S(1)}, u32[]{:S(2)}, u32[]{:S(2)}) async-start(f32[32,16,128]{2,1,0:T(8,128)} %get-tuple-element.19), calls=%async_computation | async-start | bytes 524288 | tf_op jit(solution)/shard_map/all_to_all | solution.py:337
  68.5 4.4 %collective-permute-start = (f32[552,128]{1,0:T(8,128)S(1)}, f32[552,128]{1,0:T(8,128)S(1)}, u32[]{:S(2)}, u32[]{:S(2)}) collective-permute-start(f32[552,128]{1,0:T(8,128)S(1)} %get-tuple-element.27), channel_id=1, source_target_pairs={{0,1},{1,0},{2,3},{3,2},{4,5},{5,4},{6,7},{7,6},{8,9},{9,8},{10,11... | collective-permute-start | bytes 847880 | tf_op jit(solution)/shard_map/ppermute | solution.py:342
  72.9 5.0 %collective-permute-start.1 = (f32[280,128]{1,0:T(8,128)S(1)}, f32[280,128]{1,0:T(8,128)S(1)}, u32[]{:S(2)}, u32[]{:S(2)}) collective-permute-start(f32[280,128]{1,0:T(8,128)S(1)} %slice.8), channel_id=1, source_target_pairs={{0,2},{2,0},{4,6},{6,4},{1,3},{3,1},{5,7},{7,5},{8,10},{10,8},{12,... | collective-permute-start | bytes 430088 | tf_op jit(solution)/shard_map/ppermute | solution.py:344
  74.3 6.3 %collective-permute-start.3 = (f32[272,128]{1,0:T(8,128)S(1)}, f32[272,128]{1,0:T(8,128)S(1)}, u32[]{:S(2)}, u32[]{:S(2)}) collective-permute-start(f32[272,128]{1,0:T(8,128)S(1)} %slice.9), channel_id=1, source_target_pairs={{0,6},{6,0},{2,4},{4,2},{1,7},{7,1},{3,5},{5,3},{8,14},{14,8},{10,... | collective-permute-start | bytes 417800 | tf_op jit(solution)/shard_map/ppermute | solution.py:344
  78.0 6.9 %collective-permute-start.2 = (f32[280,128]{1,0:T(8,128)S(1)}, f32[280,128]{1,0:T(8,128)S(1)}, u32[]{:S(2)}, u32[]{:S(2)}) collective-permute-start(f32[280,128]{1,0:T(8,128)S(1)} %slice_add_fusion.1), channel_id=1, source_target_pairs={{0,6},{6,0},{2,4},{4,2},{1,7},{7,1},{3,5},{5,3},{8,14},{14,8},{10,... | collective-permute-start | bytes 430088 | tf_op jit(solution)/shard_map/ppermute | solution.py:345
  80.6 4.3 %collective-permute-start.4 = (f32[272,128]{1,0:T(8,128)S(1)}, f32[272,128]{1,0:T(8,128)S(1)}, u32[]{:S(2)}, u32[]{:S(2)}) collective-permute-start(f32[272,128]{1,0:T(8,128)S(1)} %slice_add_fusion), channel_id=1, source_target_pairs={{0,2},{2,0},{4,6},{6,4},{1,3},{3,1},{5,7},{7,5},{8,10},{10,8},{12,... | collective-permute-start | bytes 417800 | tf_op jit(solution)/shard_map/ppermute | solution.py:345
  85.0 3.7 %copy-start.11 = (f32[552,128]{1,0:T(8,128)}, f32[552,128]{1,0:T(8,128)S(1)}, u32[]{:S(2)}) copy-start(f32[552,128]{1,0:T(8,128)S(1)} %pad_maximum_fusion.mine_ref) | copy-start | bytes 847876
  85.0 3.6 %collective-permute-start.5 = (f32[552,128]{1,0:T(8,128)S(1)}, f32[552,128]{1,0:T(8,128)S(1)}, u32[]{:S(2)}, u32[]{:S(2)}) collective-permute-start(f32[552,128]{1,0:T(8,128)S(1)} %pad_maximum_fusion.mine_ref), channel_id=1, source_target_pairs={{0,1},{1,0},{2,3},{3,2},{4,5},{5,4},{6,7},{7,6},{8,9},{9,8},{10,11... | collective-permute-start | bytes 847880 | tf_op jit(solution)/shard_map/ppermute | solution.py:347
  88.6 0.7 copy-start.12

commit v2 on v0

v2 whole, which is shorter than its diff:
```python
import jax
import jax.numpy as jnp
from jax import lax
from jax.experimental import pallas as pl
from jax.experimental.pallas import tpu as pltpu
from jax.sharding import Mesh, PartitionSpec as P


F32 = jnp.float32
BF16 = jnp.bfloat16
TILE = 512
SAMP = 4
FEAT = 32
W = 256
NV = 32
MIB = 1024 * 1024
HBM = pltpu.MemorySpace.HBM
VMEM = pltpu.MemorySpace.VMEM
SMEM = pltpu.MemorySpace.SMEM
LIMIT = 24 * MIB


def dot(lhs, rhs, lhs_dim, rhs_dim, precision=None):
    return lax.dot_general(
        lhs, rhs, (((lhs_dim,), (rhs_dim,)), ((), ())),
        preferred_element_type=F32, precision=precision,
    )


def group_rows(rows, width):
    i = lax.broadcasted_iota(jnp.int32, (rows, width), 0)
    j = lax.broadcasted_iota(jnp.int32, (rows, width), 1)
    return lax.shift_right_logical(i, 2) == j


def spread(block, fill):
    row = lax.broadcasted_iota(jnp.int32, block.shape, 0)
    parts = [jnp.where((row & 3) == s, block, fill) for s in range(SAMP)]
    return jnp.concatenate(parts, axis=1)


def by_row(ref, row):
    planes, rows, _ = ref.shape
    return ref.reshape(planes * rows, 128)[pl.ds(row, planes, stride=rows), :]


def forward_kernel(
    x_ref, delta_ref, count_ref, cot_ref, w1_ref, wm_ref, w4_ref,
    deep_ref, low_ref, half_ref, ab_ref, pay_ref, w1t, wmt, w4t, heads, given,
):
    step = pl.program_id(0)
    tile = TILE

    @pl.when(step == 0)
    def _():
        pick = group_rows(FEAT * SAMP, FEAT).astype(BF16)
        w1t[...] = (dot(w1_ref[...], pick, 0, 1) * 0.5).astype(BF16)
        for k in range(2):
            wmt[k] = (wm_ref[k].astype(F32).T * 0.5).astype(BF16)
        pick4 = group_rows(4 * SAMP, 4).astype(BF16)
        w4t[...] = dot(pick4, w4_ref[...], 1, 0).astype(BF16)
        for r in range(given.shape[0]):
            lanes = slice(128 * r, 128 * (r + 1))
            given[r, 0:4, :] = delta_ref[:, lanes]
            given[r, 4:5, :] = count_ref[:, lanes].astype(F32)
            given[r, 5:8, :] = cot_ref[:, lanes]

    rays = pl.ds(pl.multiple_of(step * tile, tile), tile)
    wide = spread(x_ref[:, rays], jnp.zeros((), BF16))
    half = dot(w1t[...], wide, 1, 0)
    for k in range(3):
        curve = jnp.tanh(half)
        value = half + half * curve
        hidden = value.astype(BF16)
        if k == 0:
            low_ref[0] = hidden
        else:
            deep_ref[0, k - 1] = hidden
        if k < 2:
            half_ref[0, k] = half.astype(BF16)
            half = dot(wmt[k], hidden, 1, 0)
        else:
            deep_ref[0, 2] = ((1.0 + curve) + value * (1.0 - curve)).astype(BF16)
    row16 = lax.broadcasted_iota(jnp.int32, (4 * SAMP, W), 0) & 3
    head = jnp.zeros((4 * SAMP, tile), F32)
    for s in range(SAMP):
        head += dot(
            jnp.where(row16 == s, w4t[...], jnp.zeros((), BF16)),
            hidden[:, s * tile : (s + 1) * tile], 1, 0,
        )
    for r in range(tile // 128):
        heads[step * (tile // 128) + r] = head[:, 128 * r : 128 * (r + 1)]

    @pl.when(step == pl.num_programs(0) - 1)
    def _():
        render(heads, given, ab_ref, pay_ref)


def render(heads, given, ab_ref, pay_ref):
    planes = heads.shape[0]
    zero = jnp.zeros((planes, 128), F32)
    counts = by_row(given, 4)
    cot = [by_row(given, 5 + c) for c in range(3)]
    reached, leaving = zero, jnp.ones((planes, 128), F32)
    share, left, facing, own = [], [], [], []
    for s in range(SAMP):
        raw = by_row(heads, s)
        density = jnp.maximum(raw, 0.0) + jnp.log1p(jnp.exp(-jnp.abs(raw)))
        span = jnp.where(counts > s, by_row(given, s), 0.0)
        reached = reached + density * span
        entering, leaving = leaving, jnp.exp(-reached)
        share.append(entering - leaving)
        left.append(leaving)
        own.append(span * jax.nn.sigmoid(raw))
        total = zero
        for c in range(3):
            albedo = jax.nn.sigmoid(by_row(heads, 4 * (c + 1) + s))
            lit = cot[c] * albedo
            total = total + lit
            ab_ref[4 * (c + 1) + s] = share[s] * lit * (1.0 - albedo)
        facing.append(total)
    later = zero
    for s in reversed(range(SAMP)):
        ab_ref[s] = (facing[s] * left[s] - later) * own[s]
        ab_ref[16 + s] = own[s]
        later = later + facing[s] * share[s]
    both = jnp.concatenate([-reached, later], axis=0)
    pay_ref[...] = jnp.broadcast_to(both[None], pay_ref.shape)


def slope_kernel(half_ref, low_ref, mid_ref):
    for k, ref in enumerate((low_ref, mid_ref)):
        for at in range(0, W, 64):
            half = half_ref[0, k, at : at + 64, :].astype(F32)
            curve = jnp.tanh(half)
            value = half * curve
            ref[0, at : at + 64, :] = ((1.0 + half) + curve * (1.0 - value)).astype(BF16)


def split(place_ref, keep_ref, send_ref, pieces):
    for side in range(2):
        cols = slice(128 * side, 128 * (side + 1))

        def fill(ref):
            at = 0
            for piece in pieces:
                ref[at : at + piece.shape[0], :] = piece[:, cols]
                at += piece.shape[0]

        @pl.when(place_ref[1] == side)
        def _():
            fill(keep_ref)

        @pl.when(place_ref[1] != side)
        def _():
            fill(send_ref)


def top_kernel(
    place_ref, deep_hbm, ab_ref, got_ref, rank_ref, w4_ref,
    back_ref, keep_ref, send_ref, deep, front, heads, mid, last, w4h, sems,
):
    steps = deep.shape[0]
    for i in range(steps):
        pltpu.make_async_copy(deep_hbm.at[i], deep.at[i], sems.at[i]).start()

    planes = rank_ref.shape[1]

    def one(v, _):
        mine = rank_ref[v]
        total = jnp.zeros((planes, 128), F32)
        for u in range(NV):
            total += jnp.where(rank_ref[u] < mine, got_ref[u, :planes], 0.0)
        front[v] = jnp.exp(total)
        return 0

    lax.fori_loop(0, NV, one, 0)
    me = place_ref[0]
    mine = rank_ref[me]
    behind = jnp.zeros((planes, 128), F32)
    for u in range(NV):
        behind += jnp.where(rank_ref[u] > mine, front[u] * got_ref[u, planes:], 0.0)
    prefix = front[me]
    rows = heads.reshape(planes * 4 * SAMP, 128)
    for r in range(4 * SAMP):
        value = ab_ref[r] * prefix
        if r < SAMP:
            value = value - ab_ref[16 + r] * behind
        rows[pl.ds(r, planes, stride=4 * SAMP), :] = value
    mid[...] = jnp.zeros_like(mid)
    last[...] = jnp.zeros_like(last)
    pick4 = (group_rows(4 * SAMP, 4).astype(F32) * 0.5).astype(BF16)
    w4h[...] = dot(w4_ref[...], pick4, 0, 1).astype(BF16)
    per = TILE // 128

    def step(i, _):
        pltpu.make_async_copy(deep_hbm.at[i], deep.at[i], sems.at[i]).wait()
        ghead = jnp.concatenate([heads[i * per + j] for j in range(per)], axis=1)
        ghead = spread(ghead.astype(BF16), jnp.zeros((), BF16))
        back = dot(w4h[...], ghead, 1, 0)
        back = (back * deep[i, 2].astype(F32)).astype(BF16)
        back_ref[i] = back
        last[...] += dot(deep[i, 1], ghead, 1, 1)
        mid[...] += dot(deep[i, 0], back, 1, 1)
        return 0

    lax.fori_loop(0, steps, step, 0)
    pick8 = group_rows(4 * SAMP, 8).astype(F32)
    tail = dot(pick8, last[...], 0, 1, lax.Precision.HIGHEST)
    split(place_ref, keep_ref, send_ref, (mid[...], tail))


def middle_kernel(
    place_ref, hid_ref, slope_ref, back_ref, wm_ref, down_ref, keep_ref, send_ref, mid, halved
):
    mid[...] = jnp.zeros_like(mid)
    halved[...] = (wm_ref[1].astype(F32) * 0.5).astype(BF16)

    def step(i, _):
        down = dot(halved[...], back_ref[i], 1, 0)
        down = (down * slope_ref[i].astype(F32)).astype(BF16)
        down_ref[i] = down
        mid[...] += dot(hid_ref[i], down, 1, 1)
        return 0

    lax.fori_loop(0, hid_ref.shape[0], step, 0)
    split(place_ref, keep_ref, send_ref, (mid[...],))


def low_kernel(
    place_ref, slope_ref, x_ref, back_ref, wm_ref, keep_ref, send_ref, first, halved
):
    first[...] = jnp.zeros_like(first)
    halved[...] = (wm_ref[0].astype(F32) * 0.5).astype(BF16)

    def step(i, _):
        rays = pl.ds(pl.multiple_of(i * TILE, TILE), TILE)
        down = dot(halved[...], back_ref[i], 1, 0)
        down = (down * slope_ref[i].astype(F32)).astype(BF16)
        first[...] += dot(spread(x_ref[:, rays], jnp.zeros((), BF16)), down, 1, 1)
        return 0

    lax.fori_loop(0, slope_ref.shape[0], step, 0)
    pick = group_rows(FEAT * SAMP, FEAT).astype(F32)
    small = dot(pick, first[...], 0, 0, lax.Precision.HIGHEST)
    split(place_ref, keep_ref, send_ref, (small,))


def unpack_kernel(place_ref, a_ref, a_other, b_ref, b_other, first_ref, mid_ref, last_ref):
    for side in range(2):
        cols = slice(128 * side, 128 * (side + 1))

        def emit(up, down):
            mid_ref[1, :, cols] = up[0:256, :]
            last_ref[:, cols] = up[256:260, :]
            mid_ref[0, :, cols] = down[0:256, :]
            first_ref[:, cols] = down[256:288, :]

        @pl.when(place_ref[1] == side)
        def _():
            emit(a_ref, b_ref)

        @pl.when(place_ref[1] != side)
        def _():
            emit(a_other, b_other)


def far(value):
    return pltpu.with_memory_space_constraint(value, HBM)


def near(value):
    return pltpu.with_memory_space_constraint(value, VMEM)


def forward(x, deltas, counts, cot, w1, wm, w4):
    rays = x.shape[1]
    whole2 = lambda i: (0, 0)
    inside = pl.BlockSpec(memory_space=VMEM)
    return pl.pallas_call(
        forward_kernel,
        grid=(rays // TILE,),
        in_specs=[
            inside,
            pl.BlockSpec((SAMP, rays), whole2),
            pl.BlockSpec((1, rays), whole2),
            pl.BlockSpec((3, rays), whole2),
            pl.BlockSpec((FEAT, W), whole2),
            pl.BlockSpec((2, W, W), lambda i: (0, 0, 0)),
            pl.BlockSpec((4, W), whole2),
        ],
        out_specs=[
            pl.BlockSpec((1, 3, W, SAMP * TILE), lambda i: (i, 0, 0, 0)),
            pl.BlockSpec((1, W, SAMP * TILE), lambda i: (i, 0, 0)),
            pl.BlockSpec((1, 2, W, SAMP * TILE), lambda i: (i, 0, 0, 0)),
        ] + [inside] * 2,
        out_shape=[
            pltpu.HBM((rays // TILE, 3, W, SAMP * TILE), BF16),
            pltpu.HBM((rays // TILE, W, SAMP * TILE), BF16),
            pltpu.HBM((rays // TILE, 2, W, SAMP * TILE), BF16),
            pltpu.VMEM((20, rays // 128, 128), F32),
            pltpu.VMEM((NV, 2 * rays // 128, 128), F32),
        ],
        scratch_shapes=[
            pltpu.VMEM((W, FEAT * SAMP), BF16),
            pltpu.VMEM((2, W, W), BF16),
            pltpu.VMEM((4 * SAMP, W), BF16),
            pltpu.VMEM((rays // 128, 4 * SAMP, 128), F32),
            pltpu.VMEM((rays // 128, 8, 128), F32),
        ],
        compiler_params=pltpu.CompilerParams(vmem_limit_bytes=40 * MIB),
        cost_estimate=pl.CostEstimate(
            flops=2 * SAMP * rays * 140288, transcendentals=3 * W * SAMP * rays,
            bytes_accessed=MIB,
        ),
        name="forward",
    )(near(x), far(deltas), far(counts), far(cot), far(w1), far(wm), far(w4))


def slopes(half):
    steps, _, _, n = half.shape
    block = pl.BlockSpec((1, W, n), lambda i: (i, 0, 0))
    return pl.pallas_call(
        slope_kernel,
        grid=(steps,),
        in_specs=[pl.BlockSpec((1, 2, W, n), lambda i: (i, 0, 0, 0))],
        out_specs=[block] * 2,
        out_shape=[pltpu.HBM((steps, W, n), BF16)] * 2,
        compiler_params=pltpu.CompilerParams(vmem_limit_bytes=LIMIT),
        cost_estimate=pl.CostEstimate(
            flops=6 * half.size, transcendentals=half.size, bytes_accessed=16 * MIB
        ),
        name="slopes",
    )(far(half))


def top(place, deep, ab, got, ranks, w4):
    inside = pl.BlockSpec(memory_space=VMEM)
    steps, _, _, n = deep.shape
    return pl.pallas_call(
        top_kernel,
        in_specs=[pl.BlockSpec(memory_space=SMEM), pl.BlockSpec(memory_space=HBM)] + [inside] * 4,
        out_specs=[inside] * 3,
        out_shape=[
            pltpu.VMEM((steps, W, n), BF16),
            pltpu.VMEM((264, 128), F32),
            pltpu.VMEM((264, 128), F32),
        ],
        scratch_shapes=[
            pltpu.VMEM(deep.shape, BF16),
            pltpu.VMEM((NV,) + ab.shape[1:], F32),
            pltpu.VMEM((ab.shape[1], 4 * SAMP, 128), F32),
            pltpu.VMEM((W, W), F32),
            pltpu.VMEM((W, 4 * SAMP), F32),
            pltpu.VMEM((W, 4 * SAMP), BF16),
            pltpu.SemaphoreType.DMA((steps,)),
        ],
        compiler_params=pltpu.CompilerParams(vmem_limit_bytes=24 * MIB),
        cost_estimate=pl.CostEstimate(
            flops=2 * steps * n * 80000, transcendentals=0, bytes_accessed=12 * MIB
        ),
        name="top",
    )(place, far(deep), near(ab), near(got), near(ranks), near(w4))


def middle(place, hid, slope, back, wm):
    inside = pl.BlockSpec(memory_space=VMEM)
    steps, _, n = hid.shape
    return pl.pallas_call(
        middle_kernel,
        in_specs=[pl.BlockSpec(memory_space=SMEM)] + [inside] * 4,
        out_specs=[inside] * 3,
        out_shape=[
            pltpu.VMEM((steps, W, n), BF16),
            pltpu.VMEM((256, 128), F32),
            pltpu.VMEM((256, 128), F32),
        ],
        scratch_shapes=[pltpu.VMEM((W, W), F32), pltpu.VMEM((W, W), BF16)],
        compiler_params=pltpu.CompilerParams(vmem_limit_bytes=12 * MIB),
        cost_estimate=pl.CostEstimate(
            flops=2 * steps * n * 131072, transcendentals=0, bytes_accessed=8 * MIB
        ),
        name="middle",
    )(place, near(hid), near(slope), near(back), near(wm))


def low(place, slope, x, back, wm):
    inside = pl.BlockSpec(memory_space=VMEM)
    steps, _, n = slope.shape
    return pl.pallas_call(
        low_kernel,
        in_specs=[pl.BlockSpec(memory_space=SMEM)] + [inside] * 4,
        out_specs=[inside] * 2,
        out_shape=[pltpu.VMEM((32, 128), F32), pltpu.VMEM((32, 128), F32)],
        scratch_shapes=[pltpu.VMEM((FEAT * SAMP, W), F32), pltpu.VMEM((W, W), BF16)],
        compiler_params=pltpu.CompilerParams(vmem_limit_bytes=12 * MIB),
        cost_estimate=pl.CostEstimate(
            flops=2 * steps * n * 90000, transcendentals=0, bytes_accessed=8 * MIB
        ),
        name="low",
    )(place, near(slope), near(x), near(back), near(wm))


def unpack(place, a, a_other, b, b_other):
    inside = pl.BlockSpec(memory_space=VMEM)
    return pl.pallas_call(
        unpack_kernel,
        grid=(1,),
        in_specs=[pl.BlockSpec(memory_space=pltpu.MemorySpace.SMEM)] + [inside] * 4,
        out_specs=[
            pl.BlockSpec((FEAT, W), lambda i: (0, 0)),
            pl.BlockSpec((2, W, W), lambda i: (0, 0, 0)),
            pl.BlockSpec((4, W), lambda i: (0, 0)),
        ],
        out_shape=[
            pltpu.HBM((FEAT, W), F32),
            pltpu.HBM((2, W, W), F32),
            pltpu.HBM((4, W), F32),
        ],
        compiler_params=pltpu.CompilerParams(vmem_limit_bytes=12 * MIB),
        name="unpack",
    )(place, near(a), near(a_other), near(b), near(b_other))


PAIR = [(0, 1), (1, 0)]
NEAR = [(0, 1), (1, 0), (2, 3), (3, 2)]
FAR = [(0, 3), (3, 0), (1, 2), (2, 1)]


def over_cores(keep, send):
    got = lax.ppermute(send, "core", PAIR)
    return keep + got


def over_x(value, ring):
    got = lax.ppermute(value, "x", ring)
    return value + got


def per_device(
    features, deltas, counts, order_rank, cotangent, first_weight, middle_weight, last_weight
):
    x = features[0].reshape(FEAT * SAMP, -1)
    place = jnp.stack([lax.axis_index(("z", "y")), lax.axis_index("core")]).astype(jnp.int32)
    ranks = order_rank.T.reshape(NV, -1, 128)
    w1, wm, w4 = first_weight[0], middle_weight[0], last_weight[0].T
    deep, hid, half, ab, pay = forward(x, deltas[0], counts, cotangent, w1, wm, w4)
    got = lax.all_to_all(pay, ("z", "y"), 0, 0, tiled=True)
    low_slope, mid_slope = slopes(half)
    back, *sums = top(place, deep, ab, got, ranks, w4)
    upper = over_cores(*sums)
    back, *sums = middle(place, hid, mid_slope, back, wm)
    upper = over_x(upper, NEAR)
    lower = over_cores(*sums)
    sums = low(place, low_slope, x, back, wm)
    upper = over_x(upper, FAR)
    lower = jnp.concatenate([lower, over_cores(*sums)], axis=0)
    lower = over_x(over_x(lower, NEAR), FAR)
    other = lax.ppermute(upper, "core", PAIR), lax.ppermute(lower, "core", PAIR)
    first, mid, last = unpack(place, upper, other[0], lower, other[1])
    return (first[None], mid[None], last.T[None])


def solution(mesh):
    fine = Mesh(mesh.devices.reshape(8, 4, 4, 2), ("z", "y", "x", "core"))
    vol, rep = ("z", "y"), ("x", "core")
    placed = (
        P(vol, None, None, rep),
        P(vol, None, rep),
        P(vol, rep),
        P(rep, None),
        P(None, rep),
        P(vol, None, None),
        P(vol, None, None, None),
        P(vol, None, None),
    )
    return jax.shard_map(
        per_device,
        mesh=fine,
        in_specs=placed,
        out_specs=(P(vol, None, None), P(vol, None, None, None), P(vol, None, None)),
        check_vma=False,
    )
```

time: 220 us -> 81 us (0.37)
  waiting for transfers between devices: 111 us -> 14.1 us
  matrix products: 40.9 us -> 0 us
  Pallas kernels: 0 us -> 37.6 us
  blocking collectives: 27.6 us -> 0 us
  starting transfers between devices: 0.08 us -> 26.6 us
  between operations: 14.4 us -> 0.77 us
  other arithmetic: 12.2 us -> 0.2 us
  local copies, waits for them, and re-layouts: 9.77 us -> 1.49 us
  loops' own time: 2.72 us -> 0 us
    all_gather x1 -> x0, waiting for transfers between devices: 75.2 us -> none  [per_device(): segments = lax.all_gather(payload[None], 'vol', axis=0, tiled=True)]
    dot_general x10 -> x0, matrix products: 40.9 us -> none  [the longest x4 15.1 us: contract_first(): lax.dot_general(matrix, rows, (((0,), (0,)), ((), ())), preferred_element...]
    pallas_call x0 -> x6, Pallas kernels: none -> 37.6 us  [the longest x1 12.3 us: forward(): pl.pallas_call(forward_kernel, grid=(rays // TILE,), in_specs=[inside, pl...]
    psum x1 -> x0, waiting for transfers between devices: 35.7 us -> none  [per_device(): lax.psum((first_grad, middle_grad, last_grad), 'rep')]
    psum x1 -> x0, blocking collectives: 27.6 us -> none  [per_device(): lax.psum((first_grad, middle_grad, last_grad), 'rep')]
    ppermute x0 -> x9, starting transfers between devices: none -> 14.6 us  [the longest x4 6.58 us: over_x(): got = lax.ppermute(value, 'x', ring)]
    all_to_all x0 -> x1, starting transfers between devices: none -> 12 us  [per_device(): got = lax.all_to_all(pay, ('z', 'y'), 0, 0, tiled=True)]
    add x64 -> x7, other arithmetic: 7.93 us -> 0.12 us  [the longest x4 0.08 us: over_x(): return value + got]
  transfers between devices with their start and end apart: 2 -> 10, of which waited for: 2 -> 7; matrix products, arithmetic and copies ran while one was open for 2% -> 0% of each run, Pallas kernels for 0% -> 16%
where the time goes in v2:
time: 81 us; the launch traced here: 80.7 us
  Pallas kernels  37.6 us (46%)
  starting transfers between devices  26.6 us (33%)
  waiting for transfers between devices  14.1 us (17%)
  local copies, waits for them, and re-layouts  1.49 us (2%)
    pallas_call x1, Pallas kernels, forward(): pl.pallas_call(forward_kernel, grid=(rays // TILE,), in_specs=[inside, pl...  12.3 us
    all_to_all x1, starting transfers between devices, per_device(): got = lax.all_to_all(pay, ('z', 'y'), 0, 0, tiled=True)  12 us
    pallas_call x1, Pallas kernels, slopes(): pl.pallas_call(slope_kernel, grid=(steps,), in_specs=[pl.BlockSpec((1, 2,...  8.4 us
    all_to_all x1, waiting for transfers between devices, per_device(): got = lax.all_to_all(pay, ('z', 'y'), 0, 0, tiled=True)  7.71 us
    pallas_call x1, Pallas kernels, top(): pl.pallas_call(top_kernel, in_specs=[pl.BlockSpec(memory_space=SMEM), pl....  6.83 us
    ppermute x4, starting transfers between devices, over_x(): got = lax.ppermute(value, 'x', ring)  6.58 us
    pallas_call x1, Pallas kernels, low(): pl.pallas_call(low_kernel, in_specs=[pl.BlockSpec(memory_space=SMEM)] + [...  4.4 us
    pallas_call x1, Pallas kernels, middle(): pl.pallas_call(middle_kernel, in_specs=[pl.BlockSpec(memory_space=SMEM)]...  4.18 us
  transfers between devices with their start and end apart: 10, of which 7 were waited for; matrix products, arithmetic and copies ran while one was open for 0% of the time, Pallas kernels for 16%

profile of v2, /device:TPU:1, one launch (start us, length us, event | category | flops | bytes accessed | tf_op | source)
XLA Modules:
  0.0 80.7 jit_solution(169636907317317237)
XLA Ops:
  0.6 1.2 %reshape_squeeze.3.x_ref = bf16[128,2048]{1,0:T(8,128)(2,1)S(1)} reshape(bf16[1,32,4,2048]{3,2,1,0:T(4,128)(2,1)} %param.8) | data formatting | bytes 1048576 | tf_op jit(solution)/shard_map/reshape;squeeze | solution.py:443
  1.8 12.3 %forward.1 = (bf16[4,3,256,2048]{3,2,1,0:T(8,128)(2,1)}, bf16[4,256,2048]{2,1,0:T(8,128)(2,1)}, bf16[4,2,256,2048]{3,2,1,0:T(8,128)(2,1)}, f32[20,16,128]{2,1,0:T(8,128)S(1)}, f32[32,32,128]{2,1,0:T(8,128)}) custom-call(bf16[128,2048]{1,0:T(8,128)(2,1)S(1)} %reshape_squeeze.3.x_ref, f32[4,2048]{1,0:T(4,128)} %bitcast.24, s32[1,2048]{1,0:T(1,128)} %count_ref.1, ...), custom_call_target="tpu_custom_call" | custom-call | flops 2298478592 | bytes 1048576 | tf_op jit(solution)/shard_map/forward/pallas_call | solution.py:280
  14.2 12.0 %all-to-all-start = ((f32[32,32,128]{2,1,0:T(8,128)}), f32[32,32,128]{2,1,0:T(8,128)S(1)}, u32[]{:S(2)}, u32[]{:S(2)}) async-start(f32[32,32,128]{2,1,0:T(8,128)} %get-tuple-element.23), calls=%async_computation | async-start | bytes 1048576 | tf_op jit(solution)/shard_map/all_to_all | solution.py:448
  26.3 8.4 %slopes.1 = (bf16[4,256,2048]{2,1,0:T(8,128)(2,1)}, bf16[4,256,2048]{2,1,0:T(8,128)(2,1)}) custom-call(bf16[4,2,256,2048]{3,2,1,0:T(8,128)(2,1)} %get-tuple-element.27.half_ref), custom_call_target="tpu_custom_call" | custom-call | flops 25165824 | bytes 16777216 | tf_op jit(solution)/shard_map/slopes/pallas_call | solution.py:323
  34.8 7.7 %all-to-all-done.got_ref = f32[32,32,128]{2,1,0:T(8,128)S(1)} async-done(((f32[32,32,128]{2,1,0:T(8,128)}), f32[32,32,128]{2,1,0:T(8,128)S(1)}, u32[]{:S(2)}, u32[]{:S(2)}) %all-to-all-start) | async-done | bytes 524320 | tf_op jit(solution)/shard_map/all_to_all | solution.py:448
  42.5 6.8 %top.1 = (bf16[4,256,2048]{2,1,0:T(8,128)(2,1)S(1)}, f32[264,128]{1,0:T(8,128)S(1)}, f32[264,128]{1,0:T(8,128)S(1)}) custom-call(s32[2]{0:T(128)S(1)} %pad_add_fusion.place_ref, bf16[4,3,256,2048]{3,2,1,0:T(8,128)(2,1)} %get-tuple-element.21.deep_hbm, f32[20,16,128]{2,1,0:T(8,128)S(1)} %get-tuple-element.22.ab_ref, f32[32,32,128]{2,1,0:T(8,128)S(1)} %all-to-all-done.got_ref, ...), custom_call_target="tpu_custom_call" | custom-call | flops 1310720000 | bytes 12582912 | tf_op jit(solution)/shard_map/top/pallas_call | solution.py:340
  49.3 0.2 copy-done.2
  49.6 4.2 %middle.1 = (bf16[4,256,2048]{2,1,0:T(8,128)(2,1)S(1)}, f32[256,128]{1,0:T(8,128)S(1)}, f32[256,128]{1,0:T(8,128)S(1)}) custom-call(s32[2]{0:T(128)S(1)} %pad_add_fusion.place_ref, bf16[4,256,2048]{2,1,0:T(8,128)(2,1)S(1)} %copy-done, bf16[4,256,2048]{2,1,0:T(8,128)(2,1)S(1)} %copy-done.2, bf16[4,256,2048]{2,1,0:T(8,128)(2,1)S(1)} %get-tuple-element.29.back_ref, ...), custom_call_target="tpu_custom_call" | custom-call | flops 2147483648 | bytes 8388608 | tf_op jit(solution)/shard_map/middle/pallas_call | solution.py:369
  53.8 2.5 %collective-permute-start.4 = (f32[256,128]{1,0:T(8,128)S(1)}, f32[256,128]{1,0:T(8,128)S(1)}, u32[]{:S(2)}, u32[]{:S(2)}) collective-permute-start(f32[256,128]{1,0:T(8,128)S(1)} %get-tuple-element.31), channel_id=1, source_target_pairs={{0,1},{1,0},{2,3},{3,2},{4,5},{5,4},{6,7},{7,6},{8,9},{9,8},{10,11... | collective-permute-start | bytes 393224 | tf_op jit(solution)/shard_map/ppermute | solution.py:431
  56.3 4.4 %low.1 = (f32[32,128]{1,0:T(8,128)S(1)}, f32[32,128]{1,0:T(8,128)S(1)}) custom-call(s32[2]{0:T(128)S(1)} %pad_add_fusion.place_ref, bf16[4,256,2048]{2,1,0:T(8,128)(2,1)S(1)} %copy-done.1, bf16[128,2048]{1,0:T(8,128)(2,1)S(1)} %reshape_squeeze.3.x_ref, bf16[4,256,2048]{2,1,0:T(8,128)(2,1)S(1)} %get-tuple-element.33.back_ref, bf16[2,256,256]{2,1,0:T(8,128)(2,1)S(1)} %bitcast.18), custom_call_target="tpu_custom_call" | custom-call | flops 1474560000 | bytes 8388608 | tf_op jit(solution)/shard_map/low/pallas_call | solution.py:390
  60.8 1.1 %collective-permute-done.5 = f32[32,128]{1,0:T(8,128)S(1)} collective-permute-done((f32[32,128]{1,0:T(8,128)S(1)}, f32[32,128]{1,0:T(8,128)S(1)}, u32[]{:S(2)}, u32[]{:S(2)}) %collective-permute-start.5) | collective-permute-done | bytes 16416 | tf_op jit(solution)/shard_map/ppermute | solution.py:431
  62.0 1.3 %collective-permute-start.6 = (f32[288,128]{1,0:T(8,128)S(1)}, f32[288,128]{1,0:T(8,128)S(1)}, u32[]{:S(2)}, u32[]{:S(2)}) collective-permute-start(f32[288,128]{1,0:T(8,128)S(1)} %pad_maximum_fusion), channel_id=1, source_target_pairs={{0,2},{2,0},{4,6},{6,4},{1,3},{3,1},{5,7},{7,5},{8,10},{10,8},{12,... | collective-permute-start | bytes 442376 | tf_op jit(solution)/shard_map/ppermute | solution.py:436
  63.3 0.4 collective-permute-start
  63.8 1.0 %collective-permute-done = f32[264,128]{1,0:T(8,128)S(1)} collective-permute-done((f32[264,128]{1,0:T(8,128)S(1)}, f32[264,128]{1,0:T(8,128)S(1)}, u32[]{:S(2)}, u32[]{:S(2)}) %collective-permute-start) | collective-permute-done | bytes 135200 | tf_op jit(solution)/shard_map/ppermute | solution.py:431
  64.8 0.4 collective-permute-start.1
  65.1 2.2 %collective-permute-done.6 = f32[288,128]{1,0:T(8,128)S(1)} collective-permute-done((f32[288,128]{1,0:T(8,128)S(1)}, f32[288,128]{1,0:T(8,128)S(1)}, u32[]{:S(2)}, u32[]{:S(2)}) %collective-permute-start.6) | collective-permute-done | bytes 147488 | tf_op jit(solution)/shard_map/ppermute | solution.py:436
  67.4 2.6 %collective-permute-start.7 = (f32[288,128]{1,0:T(8,128)S(1)}, f32[288,128]{1,0:T(8,128)S(1)}, u32[]{:S(2)}, u32[]{:S(2)}) collective-permute-start(f32[288,128]{1,0:T(8,128)S(1)} %fusion), channel_id=1, source_target_pairs={{0,6},{6,0},{2,4},{4,2},{1,7},{7,1},{3,5},{5,3},{8,14},{14,8},{10,... | collective-permute-start | bytes 442376 | tf_op jit(solution)/shard_map/ppermute | solution.py:436
  70.0 0.5 collective-permute-done.1
  70.5 2.4 %collective-permute-start.2 = (f32[264,128]{1,0:T(8,128)S(1)}, f32[264,128]{1,0:T(8,128)S(1)}, u32[]{:S(2)}, u32[]{:S(2)}) collective-permute-start(f32[264,128]{1,0:T(8,128)S(1)} %add.26), channel_id=1, source_target_pairs={{0,6},{6,0},{2,4},{4,2},{1,7},{7,1},{3,5},{5,3},{8,14},{14,8},{10,... | collective-permute-start | bytes 405512 | tf_op jit(solution)/shard_map/ppermute | solution.py:436
  72.9 2.9 %collective-permute-start.8 = (f32[288,128]{1,0:T(8,128)S(1)}, f32[288,128]{1,0:T(8,128)S(1)}, u32[]{:S(2)}, u32[]{:S(2)}) collective-permute-start(f32[288,128]{1,0:T(8,128)S(1)} %add.31.b_ref), channel_id=1, source_target_pairs={{0,1},{1,0},{2,3},{3,2},{4,5},{5,4},{6,7},{7,6},{8,9},{9,8},{10,11... | collective-permute-start | bytes 442376 | tf_op jit(solution)/shard_map/ppermute | solution.py:459
  75.8 0.5 collective-permute-done.2
  76.3 2.0 %collective-permute-start.3 = (f32[264,128]{1,0:T(8,128)S(1)}, f32[264,128]{1,0:T(8,128)S(1)}, u32[]{:S(2)}, u32[]{:S(2)}) collective-permute-start(f32[264,128]{1,0:T(8,128)S(1)} %add.27.a_ref), channel_id=1, source_target_pairs={{0,1},{1,0},{2,3},{3,2},{4,5},{5,4},{6,7},{7,6},{8,9},{9,8},{10,11... | collective-permute-start | bytes 405512 | tf_op jit(solution)/shard_map/ppermute | solution.py:459
  78.3 1.0 %collective-permute-done.3.a_other = f32[264,128]{1,0:T(8,128)S(1)} collective-permute-done((f32[264,128]{1,0:T(8,128)S(1)}, f32[264,128]{1,0:T(8,128)S(1)}, u32[]{:S(2)}, u32[]{:S(2)}) %collective-permute-start.3) | collective-permute-done | bytes 135200 | tf_op jit(solution)/shard_map/ppermute | solution.py:459
  79.3 1.4 %unpack.1 = (f32[32,256]{1,0:T(8,128)}, f32[2,256,256]{2,1,0:T(8,128)}, f32[4,256]{1,0:T(4,128)}) custom-call(s32[2]{0:T(128)S(1)} %pad_add_fusion.place_ref, f32[264,128]{1,0:T(8,128)S(1)} %add.27.a_ref, f32[264,128]{1,0:T(8,128)S(1)} %collective-permute-done.3.a_other, f32[288,128]{1,0:T(8,128)S(1)} %add.31.b_ref, ...), custom_call_target="tpu_custom_call" | custom-call | tf_op jit(solution)/shard_map/unpack/pallas_call | solution.py:406
  (25 shorter events, 0.4 us)
Async XLA Ops:
  1.8 24.4 %copy-start.5 = (s32[2048,32]{0,1:T(8,128)S(1)}, s32[2048,32]{0,1:T(8,128)}, u32[]{:S(2)}) copy-start(s32[2048,32]{0,1:T(8,128)} %param.11) | copy-start | bytes 786436
  14.2 28.3 %all-to-all-start = ((f32[32,32,128]{2,1,0:T(8,128)}), f32[32,32,128]{2,1,0:T(8,128)S(1)}, u32[]{:S(2)}, u32[]{:S(2)}) async-start(f32[32,32,128]{2,1,0:T(8,128)} %get-tuple-element.23), calls=%async_computation | async-start | bytes 1048576 | tf_op jit(solution)/shard_map/all_to_all | solution.py:448
  26.3 16.2 %copy-start.4 = (bf16[1,256,4]{1,2,0:T(4,128)(2,1)S(1)}, bf16[1,256,4]{1,2,0:T(4,128)(2,1)}, u32[]{:S(2)}) copy-start(bf16[1,256,4]{1,2,0:T(4,128)(2,1)} %param.15) | copy-start | bytes 6148
  42.5 6.9 %copy-start = (bf16[4,256,2048]{2,1,0:T(8,128)(2,1)S(1)}, bf16[4,256,2048]{2,1,0:T(8,128)(2,1)}, u32[]{:S(2)}) copy-start(bf16[4,256,2048]{2,1,0:T(8,128)(2,1)} %get-tuple-element.26.hid_ref) | copy-start | bytes 12582916
  42.5 7.1 %copy-start.2 = (bf16[4,256,2048]{2,1,0:T(8,128)(2,1)S(1)}, bf16[4,256,2048]{2,1,0:T(8,128)(2,1)}, u32[]{:S(2)}) copy-start(bf16[4,256,2048]{2,1,0:T(8,128)(2,1)} %get-tuple-element.28.slope_ref) | copy-start | bytes 12582916
  42.5 7.1 %copy-start.3 = (bf16[1,2,256,256]{3,2,1,0:T(8,128)(2,1)S(1)}, bf16[1,2,256,256]{3,2,1,0:T(8,128)(2,1)}, u32[]{:S(2)}) copy-start(bf16[1,2,256,256]{3,2,1,0:T(8,128)(2,1)} %param.14) | copy-start | bytes 786436
  49.6 6.7 %copy-start.1 = (bf16[4,256,2048]{2,1,0:T(8,128)(2,1)S(1)}, bf16[4,256,2048]{2,1,0:T(8,128)(2,1)}, u32[]{:S(2)}) copy-start(bf16[4,256,2048]{2,1,0:T(8,128)(2,1)} %get-tuple-element.32.slope_ref) | copy-start | bytes 12582916
  53.8 8.2 %collective-permute-start.4 = (f32[256,128]{1,0:T(8,128)S(1)}, f32[256,128]{1,0:T(8,128)S(1)}, u32[]{:S(2)}, u32[]{:S(2)}) collective-permute-start(f32[256,128]{1,0:T(8,128)S(1)} %get-tuple-element.31), channel_id=1, source_target_pairs={{0,1},{1,0},{2,3},{3,2},{4,5},{5,4},{6,7},{7,6},{8,9},{9,8},{10,11... | collective-permute-start | bytes 393224 | tf_op jit(solution)/shard_map/ppermute | solution.py:431
  60.7 1.3 %collective-permute-start.5 = (f32[32,128]{1,0:T(8,128)S(1)}, f32[32,128]{1,0:T(8,128)S(1)}, u32[]{:S(2)}, u32[]{:S(2)}) collective-permute-start(f32[32,128]{1,0:T(8,128)S(1)} %get-tuple-element.35), channel_id=1, source_target_pairs={{0,1},{1,0},{2,3},{3,2},{4,5},{5,4},{6,7},{7,6},{8,9},{9,8},{10,11... | collective-permute-start | bytes 49160 | tf_op jit(solution)/shard_map/ppermute | solution.py:431
  62.0 5.3 %collective-permute-start.6 = (f32[288,128]{1,0:T(8,128)S(1)}, f32[288,128]{1,0:T(8,128)S(1)}, u32[]{:S(2)}, u32[]{:S(2)}) collective-permute-start(f32[288,128]{1,0:T(8,128)S(1)} %pad_maximum_fusion), channel_id=1, source_target_pairs={{0,2},{2,0},{4,6},{6,4},{1,3},{3,1},{5,7},{7,5},{8,10},{10,8},{12,... | collective-permute-start | bytes 442376 | tf_op jit(solution)/shard_map/ppermute | solution.py:436
  63.3 1.4 %collective-permute-start = (f32[264,128]{1,0:T(8,128)S(1)}, f32[264,128]{1,0:T(8,128)S(1)}, u32[]{:S(2)}, u32[]{:S(2)}) collective-permute-start(f32[264,128]{1,0:T(8,128)S(1)} %get-tuple-element.25), channel_id=1, source_target_pairs={{0,1},{1,0},{2,3},{3,2},{4,5},{5,4},{6,7},{7,6},{8,9},{9,8},{10,11... | collective-permute-start | bytes 405512 | tf_op jit(solution)/shard_map/ppermute | solution.py:431
  64.8 5.7 %collective-permute-start.1 = (f32[264,128]{1,0:T(8,128)S(1)}, f32[264,128]{1,0:T(8,128)S(1)}, u32[]{:S(2)}, u32[]{:S(2)}) collective-permute-start(f32[264,128]{1,0:T(8,128)S(1)} %add.25), channel_id=1, source_target_pairs={{0,2},{2,0},{4,6},{6,4},{1,3},{3,1},{5,7},{7,5},{8,10},{10,8},{12,... | collective-permute-start | bytes 405512 | tf_op jit(solution)/shard_map/ppermute | solution.py:436
  67.4 5.5 %collective-permute-start.7 = (f32[288,128]{1,0:T(8,128)S(1)}, f32[288,128]{1,0:T(8,128)S(1)}, u32[]{:S(2)}, u32[]{:S(2)}) collective-permute-start(f32[288,128]{1,0:T(8,128)S(1)} %fusion), channel_id=1, source_target_pairs={{0,6},{6,0},{2,4},{4,2},{1,7},{7,1},{3,5},{5,3},{8,14},{14,8},{10,... | collective-permute-start | bytes 442376 | tf_op jit(solution)/shard_map/ppermute | solution.py:436
  70.5 5.8 %collective-permute-start.2 = (f32[264,128]{1,0:T(8,128)S(1)}, f32[264,128]{1,0:T(8,128)S(1)}, u32[]{:S(2)}, u32[]{:S(2)}) collective-permute-start(f32[264,128]{1,0:T(8,128)S(1)} %add.26), channel_id=1, source_target_pairs={{0,6},{6,0},{2,4},{4,2},{1,7},{7,1},{3,5},{5,3},{8,14},{14,8},{10,... | collective-permute-start | bytes 405512 | tf_op jit(solution)/shard_map/ppermute | solution.py:436
  72.9 6.4 %collective-permute-start.8 = (f32[288,128]{1,0:T(8,128)S(1)}, f32[288,128]{1,0:T(8,128)S(1)}, u32[]{:S(2)}, u32[]{:S(2)}) collective-permute-start(f32[288,128]{1,0:T(8,128)S(1)} %add.31.b_ref), channel_id=1, source_target_pairs={{0,1},{1,0},{2,3},{3,2},{4,5},{5,4},{6,7},{7,6},{8,9},{9,8},{10,11... | collective-permute-start | bytes 442376 | tf_op jit(solution)/shard_map/ppermute | solution.py:459
  76.3 3.0 %collective-permute-start.3 = (f32[264,128]{1,0:T(8,128)S(1)}, f32[264,128]{1,0:T(8,128)S(1)}, u32[]{:S(2)}, u32[]{:S(2)}) collective-permute-start(f32[264,128]{1,0:T(8,128)S(1)} %add.27.a_ref), channel_id=1, source_target_pairs={{0,1},{1,0},{2,3},{3,2},{4,5},{5,4},{6,7},{7,6},{8,9},{9,8},{10,11... | collective-permute-start | bytes 405512 | tf_op jit(solution)/shard_map/ppermute | solution.py:459

commit v3 on v2

--- a/solution.py
+++ b/solution.py
@@ -9,6 +9,7 @@
 F32 = jnp.float32
 BF16 = jnp.bfloat16
 TILE = 512
+PART = 256
 SAMP = 4
 FEAT = 32
 W = 256
@@ -46,7 +47,7 @@
 
 def forward_kernel(
     x_ref, delta_ref, count_ref, cot_ref, w1_ref, wm_ref, w4_ref,
-    deep_ref, low_ref, half_ref, ab_ref, pay_ref, w1t, wmt, w4t, heads, given,
+    hid_ref, low_ref, ab_ref, pay_ref, w1t, wmt, w4t, heads, given,
 ):
     step = pl.program_id(0)
     tile = TILE
@@ -65,31 +66,30 @@
             given[r, 4:5, :] = count_ref[:, lanes].astype(F32)
             given[r, 5:8, :] = cot_ref[:, lanes]
 
-    rays = pl.ds(pl.multiple_of(step * tile, tile), tile)
-    wide = spread(x_ref[:, rays], jnp.zeros((), BF16))
-    half = dot(w1t[...], wide, 1, 0)
-    for k in range(3):
-        curve = jnp.tanh(half)
-        value = half + half * curve
-        hidden = value.astype(BF16)
-        if k == 0:
-            low_ref[0] = hidden
-        else:
-            deep_ref[0, k - 1] = hidden
-        if k < 2:
-            half_ref[0, k] = half.astype(BF16)
-            half = dot(wmt[k], hidden, 1, 0)
-        else:
-            deep_ref[0, 2] = ((1.0 + curve) + value * (1.0 - curve)).astype(BF16)
     row16 = lax.broadcasted_iota(jnp.int32, (4 * SAMP, W), 0) & 3
-    head = jnp.zeros((4 * SAMP, tile), F32)
-    for s in range(SAMP):
-        head += dot(
-            jnp.where(row16 == s, w4t[...], jnp.zeros((), BF16)),
-            hidden[:, s * tile : (s + 1) * tile], 1, 0,
-        )
-    for r in range(tile // 128):
-        heads[step * (tile // 128) + r] = head[:, 128 * r : 128 * (r + 1)]
+    for part in range(tile // PART):
+        rays = pl.ds(pl.multiple_of(step * tile + part * PART, PART), PART)
+        wide = spread(x_ref[:, rays], jnp.zeros((), BF16))
+        half = dot(w1t[...], wide, 1, 0)
+        for k in range(3):
+            hidden = (half + half * jnp.tanh(half)).astype(BF16)
+            for s in range(SAMP):
+                cols = slice(s * PART, (s + 1) * PART)
+                put = slice(s * tile + part * PART, s * tile + (part + 1) * PART)
+                if k == 0:
+                    low_ref[0, :, put] = hidden[:, cols]
+                else:
+                    hid_ref[0, k - 1, :, put] = hidden[:, cols]
+            if k < 2:
+                half = dot(wmt[k], hidden, 1, 0)
+        head = jnp.zeros((4 * SAMP, PART), F32)
+        for s in range(SAMP):
+            head += dot(
+                jnp.where(row16 == s, w4t[...], jnp.zeros((), BF16)),
+                hidden[:, s * PART : (s + 1) * PART], 1, 0,
+            )
+        for r in range(PART // 128):
+            heads[step * (tile // 128) + part * (PART // 128) + r] = head[:, 128 * r : 128 * (r + 1)]
 
     @pl.when(step == pl.num_programs(0) - 1)
     def _():
@@ -128,13 +128,25 @@
     pay_ref[...] = jnp.broadcast_to(both[None], pay_ref.shape)
 
 
-def slope_kernel(half_ref, low_ref, mid_ref):
-    for k, ref in enumerate((low_ref, mid_ref)):
-        for at in range(0, W, 64):
-            half = half_ref[0, k, at : at + 64, :].astype(F32)
+def slope_kernel(x_ref, low_hid, mid_hid, w1t, wmt, low_ref, mid_ref, top_ref):
+    i = pl.program_id(0)
+    x = x_ref[:, pl.ds(pl.multiple_of(i * TILE, TILE), TILE)]
+    row = lax.broadcasted_iota(jnp.int32, x.shape, 0) & 3
+    for s in range(SAMP):
+        cols = slice(s * TILE, (s + 1) * TILE)
+        wide = jnp.where(row == s, x, jnp.zeros((), BF16))
+        for ref, weight, taken in (
+            (low_ref, w1t[...], wide),
+            (mid_ref, wmt[0], low_hid[0, :, cols]),
+            (top_ref, wmt[1], mid_hid[0, 0, :, cols]),
+        ):
+            half = dot(weight, taken, 1, 0)
             curve = jnp.tanh(half)
-            value = half * curve
-            ref[0, at : at + 64, :] = ((1.0 + half) + curve * (1.0 - value)).astype(BF16)
+            ref[0, :, cols] = (half + curve * (1.0 - half * curve)).astype(BF16)
+
+
+def bend(back, slope):
+    return (back + back * slope.astype(F32)).astype(BF16)
 
 
 def split(place_ref, keep_ref, send_ref, pieces):
@@ -157,12 +169,20 @@
 
 
 def top_kernel(
-    place_ref, deep_hbm, ab_ref, got_ref, rank_ref, w4_ref,
-    back_ref, keep_ref, send_ref, deep, front, heads, mid, last, w4h, sems,
+    place_ref, hid_hbm, slope_hbm, ab_ref, got_ref, rank_ref, w4_ref,
+    back_ref, keep_ref, send_ref, hid, slope, front, heads, mid, last, w4h, sems,
 ):
-    steps = deep.shape[0]
+    steps = hid.shape[0]
+
+    def copies(i):
+        return (
+            pltpu.make_async_copy(slope_hbm.at[i], slope.at[i], sems.at[0, i]),
+            pltpu.make_async_copy(hid_hbm.at[i], hid.at[i], sems.at[1, i]),
+        )
+
     for i in range(steps):
-        pltpu.make_async_copy(deep_hbm.at[i], deep.at[i], sems.at[i]).start()
+        for copy in copies(i):
+            copy.start()
 
     planes = rank_ref.shape[1]
 
@@ -194,19 +214,19 @@
     per = TILE // 128
 
     def step(i, _):
-        pltpu.make_async_copy(deep_hbm.at[i], deep.at[i], sems.at[i]).wait()
-        ghead = jnp.concatenate([heads[i * per + j] for j in range(per)], axis=1)
+        for copy in copies(i):
+            copy.wait()
+        ghead = jnp.concatenate([heads[i * per + k] for k in range(per)], axis=1)
         ghead = spread(ghead.astype(BF16), jnp.zeros((), BF16))
-        back = dot(w4h[...], ghead, 1, 0)
-        back = (back * deep[i, 2].astype(F32)).astype(BF16)
+        back = bend(dot(w4h[...], ghead, 1, 0), slope[i])
         back_ref[i] = back
-        last[...] += dot(deep[i, 1], ghead, 1, 1)
-        mid[...] += dot(deep[i, 0], back, 1, 1)
+        last[...] += dot(ghead, hid[i, 1], 1, 1)
+        mid[...] += dot(hid[i, 0], back, 1, 1)
         return 0
 
     lax.fori_loop(0, steps, step, 0)
     pick8 = group_rows(4 * SAMP, 8).astype(F32)
-    tail = dot(pick8, last[...], 0, 1, lax.Precision.HIGHEST)
+    tail = dot(pick8, last[...], 0, 0, lax.Precision.HIGHEST)
     split(place_ref, keep_ref, send_ref, (mid[...], tail))
 
 
@@ -217,8 +237,7 @@
     halved[...] = (wm_ref[1].astype(F32) * 0.5).astype(BF16)
 
     def step(i, _):
-        down = dot(halved[...], back_ref[i], 1, 0)
-        down = (down * slope_ref[i].astype(F32)).astype(BF16)
+        down = bend(dot(halved[...], back_ref[i], 1, 0), slope_ref[i])
         down_ref[i] = down
         mid[...] += dot(hid_ref[i], down, 1, 1)
         return 0
@@ -227,34 +246,32 @@
     split(place_ref, keep_ref, send_ref, (mid[...],))
 
 
-def low_kernel(
-    place_ref, slope_ref, x_ref, back_ref, wm_ref, keep_ref, send_ref, first, halved
-):
+def low_kernel(slope_ref, x_ref, back_ref, wm_ref, out_ref, first, halved):
     first[...] = jnp.zeros_like(first)
     halved[...] = (wm_ref[0].astype(F32) * 0.5).astype(BF16)
 
     def step(i, _):
         rays = pl.ds(pl.multiple_of(i * TILE, TILE), TILE)
-        down = dot(halved[...], back_ref[i], 1, 0)
-        down = (down * slope_ref[i].astype(F32)).astype(BF16)
+        down = bend(dot(halved[...], back_ref[i], 1, 0), slope_ref[i])
         first[...] += dot(spread(x_ref[:, rays], jnp.zeros((), BF16)), down, 1, 1)
         return 0
 
     lax.fori_loop(0, slope_ref.shape[0], step, 0)
     pick = group_rows(FEAT * SAMP, FEAT).astype(F32)
-    small = dot(pick, first[...], 0, 0, lax.Precision.HIGHEST)
-    split(place_ref, keep_ref, send_ref, (small,))
-
-
-def unpack_kernel(place_ref, a_ref, a_other, b_ref, b_other, first_ref, mid_ref, last_ref):
+    out_ref[...] = dot(pick, first[...], 0, 0, lax.Precision.HIGHEST)
+
+
+def unpack_kernel(
+    place_ref, a_ref, a_other, b_ref, b_other, c_ref, c_other, first_ref, mid_ref, last_ref
+):
+    first_ref[...] = c_ref[...] + c_other[...]
     for side in range(2):
         cols = slice(128 * side, 128 * (side + 1))
 
         def emit(up, down):
             mid_ref[1, :, cols] = up[0:256, :]
             last_ref[:, cols] = up[256:260, :]
-            mid_ref[0, :, cols] = down[0:256, :]
-            first_ref[:, cols] = down[256:288, :]
+            mid_ref[0, :, cols] = down[...]
 
         @pl.when(place_ref[1] == side)
         def _():
@@ -290,20 +307,18 @@
             pl.BlockSpec((4, W), whole2),
         ],
         out_specs=[
-            pl.BlockSpec((1, 3, W, SAMP * TILE), lambda i: (i, 0, 0, 0)),
+            pl.BlockSpec((1, 2, W, SAMP * TILE), lambda i: (i, 0, 0, 0)),
             pl.BlockSpec((1, W, SAMP * TILE), lambda i: (i, 0, 0)),
-            pl.BlockSpec((1, 2, W, SAMP * TILE), lambda i: (i, 0, 0, 0)),
-        ] + [inside] * 2,
+        ] + [inside] * 4,
         out_shape=[
-            pltpu.HBM((rays // TILE, 3, W, SAMP * TILE), BF16),
+            pltpu.HBM((rays // TILE, 2, W, SAMP * TILE), BF16),
             pltpu.HBM((rays // TILE, W, SAMP * TILE), BF16),
-            pltpu.HBM((rays // TILE, 2, W, SAMP * TILE), BF16),
             pltpu.VMEM((20, rays // 128, 128), F32),
             pltpu.VMEM((NV, 2 * rays // 128, 128), F32),
-        ],
-        scratch_shapes=[
             pltpu.VMEM((W, FEAT * SAMP), BF16),
             pltpu.VMEM((2, W, W), BF16),
+        ],
+        scratch_shapes=[
             pltpu.VMEM((4 * SAMP, W), BF16),
             pltpu.VMEM((rays // 128, 4 * SAMP, 128), F32),
             pltpu.VMEM((rays // 128, 8, 128), F32),
@@ -317,29 +332,36 @@
     )(near(x), far(deltas), far(counts), far(cot), far(w1), far(wm), far(w4))
 
 
-def slopes(half):
-    steps, _, _, n = half.shape
+def slopes(x, low_hid, hid, w1t, wmt):
+    steps, _, _, n = hid.shape
     block = pl.BlockSpec((1, W, n), lambda i: (i, 0, 0))
+    inside = pl.BlockSpec(memory_space=VMEM)
     return pl.pallas_call(
         slope_kernel,
         grid=(steps,),
-        in_specs=[pl.BlockSpec((1, 2, W, n), lambda i: (i, 0, 0, 0))],
-        out_specs=[block] * 2,
-        out_shape=[pltpu.HBM((steps, W, n), BF16)] * 2,
+        in_specs=[
+            inside,
+            block,
+            pl.BlockSpec((1, 1, W, n), lambda i: (i, 0, 0, 0)),
+            inside, inside,
+        ],
+        out_specs=[block] * 3,
+        out_shape=[pltpu.HBM((steps, W, n), BF16)] * 3,
         compiler_params=pltpu.CompilerParams(vmem_limit_bytes=LIMIT),
         cost_estimate=pl.CostEstimate(
-            flops=6 * half.size, transcendentals=half.size, bytes_accessed=16 * MIB
+            flops=2 * steps * n * 140000, transcendentals=3 * W * steps * n,
+            bytes_accessed=20 * MIB,
         ),
         name="slopes",
-    )(far(half))
-
-
-def top(place, deep, ab, got, ranks, w4):
+    )(near(x), far(low_hid), far(hid), near(w1t), near(wmt))
+
+
+def top(place, hid, slope, ab, got, ranks, w4):
     inside = pl.BlockSpec(memory_space=VMEM)
-    steps, _, _, n = deep.shape
+    steps, _, _, n = hid.shape
     return pl.pallas_call(
         top_kernel,
-        in_specs=[pl.BlockSpec(memory_space=SMEM), pl.BlockSpec(memory_space=HBM)] + [inside] * 4,
+        in_specs=[pl.BlockSpec(memory_space=SMEM)] + [pl.BlockSpec(memory_space=HBM)] * 2 + [inside] * 4,
         out_specs=[inside] * 3,
         out_shape=[
             pltpu.VMEM((steps, W, n), BF16),
@@ -347,20 +369,21 @@
             pltpu.VMEM((264, 128), F32),
         ],
         scratch_shapes=[
-            pltpu.VMEM(deep.shape, BF16),
+            pltpu.VMEM(hid.shape, BF16),
+            pltpu.VMEM(slope.shape, BF16),
             pltpu.VMEM((NV,) + ab.shape[1:], F32),
             pltpu.VMEM((ab.shape[1], 4 * SAMP, 128), F32),
             pltpu.VMEM((W, W), F32),
-            pltpu.VMEM((W, 4 * SAMP), F32),
+            pltpu.VMEM((4 * SAMP, W), F32),
             pltpu.VMEM((W, 4 * SAMP), BF16),
-            pltpu.SemaphoreType.DMA((steps,)),
+            pltpu.SemaphoreType.DMA((2, steps)),
         ],
         compiler_params=pltpu.CompilerParams(vmem_limit_bytes=24 * MIB),
         cost_estimate=pl.CostEstimate(
             flops=2 * steps * n * 80000, transcendentals=0, bytes_accessed=12 * MIB
         ),
         name="top",
-    )(place, far(deep), near(ab), near(got), near(ranks), near(w4))
+    )(place, far(hid), far(slope), near(ab), near(got), near(ranks), near(w4))
 
 
 def middle(place, hid, slope, back, wm):
@@ -384,29 +407,29 @@
     )(place, near(hid), near(slope), near(back), near(wm))
 
 
-def low(place, slope, x, back, wm):
+def low(slope, x, back, wm):
     inside = pl.BlockSpec(memory_space=VMEM)
     steps, _, n = slope.shape
     return pl.pallas_call(
         low_kernel,
-        in_specs=[pl.BlockSpec(memory_space=SMEM)] + [inside] * 4,
-        out_specs=[inside] * 2,
-        out_shape=[pltpu.VMEM((32, 128), F32), pltpu.VMEM((32, 128), F32)],
+        in_specs=[inside] * 4,
+        out_specs=inside,
+        out_shape=pltpu.VMEM((FEAT, W), F32),
         scratch_shapes=[pltpu.VMEM((FEAT * SAMP, W), F32), pltpu.VMEM((W, W), BF16)],
         compiler_params=pltpu.CompilerParams(vmem_limit_bytes=12 * MIB),
         cost_estimate=pl.CostEstimate(
             flops=2 * steps * n * 90000, transcendentals=0, bytes_accessed=8 * MIB
         ),
         name="low",
-    )(place, near(slope), near(x), near(back), near(wm))
-
-
-def unpack(place, a, a_other, b, b_other):
+    )(near(slope), near(x), near(back), near(wm))
+
+
+def unpack(place, *parts):
     inside = pl.BlockSpec(memory_space=VMEM)
     return pl.pallas_call(
         unpack_kernel,
         grid=(1,),
-        in_specs=[pl.BlockSpec(memory_space=pltpu.MemorySpace.SMEM)] + [inside] * 4,
+        in_specs=[pl.BlockSpec(memory_space=SMEM)] + [inside] * 6,
         out_specs=[
             pl.BlockSpec((FEAT, W), lambda i: (0, 0)),
             pl.BlockSpec((2, W, W), lambda i: (0, 0, 0)),
@@ -419,7 +442,7 @@
         ],
         compiler_params=pltpu.CompilerParams(vmem_limit_bytes=12 * MIB),
         name="unpack",
-    )(place, near(a), near(a_other), near(b), near(b_other))
+    )(place, *map(near, parts))
 
 
 PAIR = [(0, 1), (1, 0)]
@@ -444,20 +467,23 @@
     place = jnp.stack([lax.axis_index(("z", "y")), lax.axis_index("core")]).astype(jnp.int32)
     ranks = order_rank.T.reshape(NV, -1, 128)
     w1, wm, w4 = first_weight[0], middle_weight[0], last_weight[0].T
-    deep, hid, half, ab, pay = forward(x, deltas[0], counts, cotangent, w1, wm, w4)
+    hid, low_hid, ab, pay, w1t, wmt = forward(x, deltas[0], counts, cotangent, w1, wm, w4)
     got = lax.all_to_all(pay, ("z", "y"), 0, 0, tiled=True)
-    low_slope, mid_slope = slopes(half)
-    back, *sums = top(place, deep, ab, got, ranks, w4)
-    upper = over_cores(*sums)
-    back, *sums = middle(place, hid, mid_slope, back, wm)
-    upper = over_x(upper, NEAR)
-    lower = over_cores(*sums)
-    sums = low(place, low_slope, x, back, wm)
+    low_slope, mid_slope, top_slope = slopes(x, low_hid, hid, w1t, wmt)
+    back, *sums = top(place, hid, top_slope, ab, got, ranks, w4)
+    upper = over_x(over_cores(*sums), NEAR)
+    back, *sums = middle(place, low_hid, mid_slope, back, wm)
     upper = over_x(upper, FAR)
-    lower = jnp.concatenate([lower, over_cores(*sums)], axis=0)
-    lower = over_x(over_x(lower, NEAR), FAR)
-    other = lax.ppermute(upper, "core", PAIR), lax.ppermute(lower, "core", PAIR)
-    first, mid, last = unpack(place, upper, other[0], lower, other[1])
+    lower = over_x(over_cores(*sums), NEAR)
+    small = low(low_slope, x, back, wm)
+    small = small + sum(
+        lax.ppermute(small, "x", [(i, (i + s) % 4) for i in range(4)]) for s in (1, 2, 3)
+    )
+    lower = over_x(lower, FAR)
+    parts = []
+    for part in (upper, lower, small):
+        parts += [part, lax.ppermute(part, "core", PAIR)]
+    first, mid, last = unpack(place, *parts)
     return (first[None], mid[None], last.T[None])
 
 

time: 81 us -> 80.8 us (level)
  starting transfers between devices: 26.6 us -> 29.2 us
  waiting for transfers between devices: 14.1 us -> 12.6 us
  Pallas kernels: 37.6 us -> 36.6 us
    ppermute x2 -> x6, starting transfers between devices: 4.92 us -> 9.1 us  [the longest x3 5.88 us: per_device(): parts += [part, lax.ppermute(part, 'core', PAIR)]]
    pallas_call x1, Pallas kernels: 12.3 us -> 9.57 us  [forward(): pl.pallas_call(forward_kernel, grid=(rays // TILE,), in_specs=[inside, pl...]
    all_to_all x1, waiting for transfers between devices: 7.71 us -> 5.5 us  [per_device(): got = lax.all_to_all(pay, ('z', 'y'), 0, 0, tiled=True)]
    ppermute x3 -> x2, waiting for transfers between devices: 2.14 us -> 0.01 us  [over_cores(): got = lax.ppermute(send, 'core', PAIR)]
    ppermute x4, waiting for transfers between devices: 3.23 us -> 5.14 us  [over_x(): got = lax.ppermute(value, 'x', ring)]
    pallas_call x3, Pallas kernels: 19.6 us -> 21.4 us  [the longest x1 10.6 us: slopes(): pl.pallas_call(slope_kernel, grid=(steps,), in_specs=[inside, block, pl.B...]
    ppermute x4, starting transfers between devices: 6.58 us -> 5.35 us  [over_x(): got = lax.ppermute(value, 'x', ring)]
    ppermute x2 -> x6, waiting for transfers between devices: 0.99 us -> 1.91 us  [the longest x3 1.04 us: per_device(): lax.ppermute(small, 'x', [(i, (i + s) % 4) for i in range(4)])]
  transfers between devices with their start and end apart: 10 -> 13, of which waited for: 7 -> 4; matrix products, arithmetic and copies ran while one was open for 0% -> 0% of each run, Pallas kernels for 16% -> 23%
where the time goes in v3:
time: 80.8 us; the launch traced here: 80.5 us
  Pallas kernels  36.6 us (45%)
  starting transfers between devices  29.2 us (36%)
  waiting for transfers between devices  12.6 us (16%)
  local copies, waits for them, and re-layouts  1.24 us (2%)
    all_to_all x1, starting transfers between devices, per_device(): got = lax.all_to_all(pay, ('z', 'y'), 0, 0, tiled=True)  12 us
    pallas_call x1, Pallas kernels, slopes(): pl.pallas_call(slope_kernel, grid=(steps,), in_specs=[inside, block, pl.B...  10.6 us
    pallas_call x1, Pallas kernels, forward(): pl.pallas_call(forward_kernel, grid=(rays // TILE,), in_specs=[inside, pl...  9.57 us
    pallas_call x1, Pallas kernels, top(): pl.pallas_call(top_kernel, in_specs=[pl.BlockSpec(memory_space=SMEM)] + [...  6.9 us
    ppermute x3, starting transfers between devices, per_device(): parts += [part, lax.ppermute(part, 'core', PAIR)]  5.88 us
    all_to_all x1, waiting for transfers between devices, per_device(): got = lax.all_to_all(pay, ('z', 'y'), 0, 0, tiled=True)  5.5 us
    ppermute x4, starting transfers between devices, over_x(): got = lax.ppermute(value, 'x', ring)  5.35 us
    ppermute x4, waiting for transfers between devices, over_x(): got = lax.ppermute(value, 'x', ring)  5.14 us
  transfers between devices with their start and end apart: 13, of which 4 were waited for; matrix products, arithmetic and copies ran while one was open for 0% of the time, Pallas kernels for 23%

profile of v3, /device:TPU:1, one launch (start us, length us, event | category | flops | bytes accessed | tf_op | source)
XLA Modules:
  0.0 80.5 jit_solution(16611065531780632306)
XLA Ops:
  0.6 1.2 %reshape_squeeze.3.x_ref = bf16[128,2048]{1,0:T(8,128)(2,1)S(1)} reshape(bf16[1,32,4,2048]{3,2,1,0:T(4,128)(2,1)} %param.8) | data formatting | bytes 1048576 | tf_op jit(solution)/shard_map/reshape;squeeze | solution.py:466
  1.8 9.6 %forward.1 = (bf16[4,2,256,2048]{3,2,1,0:T(8,128)(2,1)}, bf16[4,256,2048]{2,1,0:T(8,128)(2,1)}, f32[20,16,128]{2,1,0:T(8,128)S(1)}, f32[32,32,128]{2,1,0:T(8,128...) custom-call(bf16[128,2048]{1,0:T(8,128)(2,1)S(1)} %reshape_squeeze.3.x_ref, f32[4,2048]{1,0:T(4,128)} %bitcast.24, ...), custom_call_target="tpu_custom_call" | custom-call | flops 2298478592 | bytes 1048576 | tf_op jit(solution)/shard_map/forward/pallas_call | solution.py:297
  11.4 12.0 %all-to-all-start = ((f32[32,32,128]{2,1,0:T(8,128)}), f32[32,32,128]{2,1,0:T(8,128)S(1)}, u32[]{:S(2)}, u32[]{:S(2)}) async-start(f32[32,32,128]{2,1,0:T(8,128)} %get-tuple-element.27), calls=%async_computation | async-start | bytes 1048576 | tf_op jit(solution)/shard_map/all_to_all | solution.py:471
  23.5 0.1 pad_add_fusion.place_ref
  23.6 10.6 %slopes.1 = (bf16[4,256,2048]{2,1,0:T(8,128)(2,1)}, bf16[4,256,2048]{2,1,0:T(8,128)(2,1)}, bf16[4,256,2048]{2,1,0:T(8,128)(2,1)}) custom-call(bf16[128,2048]{1,0:T(8,128)(2,1)S(1)} %reshape_squeeze.3.x_ref, bf16[4,256,2048]{2,1,0:T(8,128)(2,1)} %get-tuple-element.22.low_hid.hid_ref, bf16[4,2,256,2048]{3,2,1,0:T(8,128)(2,1)} %get-tuple-element.21.mid_hid.hid_hbm, ...), custom_call_target="tpu_custom_call" | custom-call | flops 2293760000 | bytes 20971520 | tf_op jit(solution)/shard_map/slopes/pallas_call | solution.py:339
  34.2 5.5 %all-to-all-done.got_ref = f32[32,32,128]{2,1,0:T(8,128)S(1)} async-done(((f32[32,32,128]{2,1,0:T(8,128)}), f32[32,32,128]{2,1,0:T(8,128)S(1)}, u32[]{:S(2)}, u32[]{:S(2)}) %all-to-all-start) | async-done | bytes 524320 | tf_op jit(solution)/shard_map/all_to_all | solution.py:471
  39.7 6.9 %top.1 = (bf16[4,256,2048]{2,1,0:T(8,128)(2,1)S(1)}, f32[264,128]{1,0:T(8,128)S(1)}, f32[264,128]{1,0:T(8,128)S(1)}) custom-call(s32[2]{0:T(128)S(1)} %pad_add_fusion.place_ref, bf16[4,2,256,2048]{3,2,1,0:T(8,128)(2,1)} %get-tuple-element.21.mid_hid.hid_hbm, bf16[4,256,2048]{2,1,0:T(8,128)(2,1)} %get-tuple-element.25.slope_hbm, ...), custom_call_target="tpu_custom_call" | custom-call | flops 1310720000 | bytes 12582912 | tf_op jit(solution)/shard_map/top/pallas_call | solution.py:362
  46.6 2.5 %collective-permute-start = (f32[264,128]{1,0:T(8,128)S(1)}, f32[264,128]{1,0:T(8,128)S(1)}, u32[]{:S(2)}, u32[]{:S(2)}) collective-permute-start(f32[264,128]{1,0:T(8,128)S(1)} %get-tuple-element.29), channel_id=1, source_target_pairs={{0,1},{1,0},{2,3},{3,2},{4,5},{5,4},{6,7},{7,6},{8,9},{9,8},{10,11... | collective-permute-start | bytes 405512 | tf_op jit(solution)/shard_map/ppermute | solution.py:454
  49.2 4.2 %middle.1 = (bf16[4,256,2048]{2,1,0:T(8,128)(2,1)S(1)}, f32[256,128]{1,0:T(8,128)S(1)}, f32[256,128]{1,0:T(8,128)S(1)}) custom-call(s32[2]{0:T(128)S(1)} %pad_add_fusion.place_ref, bf16[4,256,2048]{2,1,0:T(8,128)(2,1)S(1)} %copy-done, bf16[4,256,2048]{2,1,0:T(8,128)(2,1)S(1)} %copy-done.2, bf16[4,256,2048]{2,1,0:T(8,128)(2,1)S(1)} %get-tuple-element.31.back_ref, ...), custom_call_target="tpu_custom_call" | custom-call | flops 2147483648 | bytes 8388608 | tf_op jit(solution)/shard_map/middle/pallas_call | solution.py:392
  53.4 0.2 collective-permute-start.4
  53.6 1.3 %collective-permute-start.1 = (f32[264,128]{1,0:T(8,128)S(1)}, f32[264,128]{1,0:T(8,128)S(1)}, u32[]{:S(2)}, u32[]{:S(2)}) collective-permute-start(f32[264,128]{1,0:T(8,128)S(1)} %add.31), channel_id=1, source_target_pairs={{0,2},{2,0},{4,6},{6,4},{1,3},{3,1},{5,7},{7,5},{8,10},{10,8},{12,... | collective-permute-start | bytes 405512 | tf_op jit(solution)/shard_map/ppermute | solution.py:459
  54.9 1.2 %collective-permute-start.5 = (f32[256,128]{1,0:T(8,128)S(1)}, f32[256,128]{1,0:T(8,128)S(1)}, u32[]{:S(2)}, u32[]{:S(2)}) collective-permute-start(f32[256,128]{1,0:T(8,128)S(1)} %add.34), channel_id=1, source_target_pairs={{0,2},{2,0},{4,6},{6,4},{1,3},{3,1},{5,7},{7,5},{8,10},{10,8},{12,... | collective-permute-start | bytes 393224 | tf_op jit(solution)/shard_map/ppermute | solution.py:459
  56.1 5.1 %collective-permute-done.5 = f32[256,128]{1,0:T(8,128)S(1)} collective-permute-done((f32[256,128]{1,0:T(8,128)S(1)}, f32[256,128]{1,0:T(8,128)S(1)}, u32[]{:S(2)}, u32[]{:S(2)}) %collective-permute-start.5) | collective-permute-done | bytes 131104 | tf_op jit(solution)/shard_map/ppermute | solution.py:459
  61.3 2.5 %collective-permute-start.6 = (f32[256,128]{1,0:T(8,128)S(1)}, f32[256,128]{1,0:T(8,128)S(1)}, u32[]{:S(2)}, u32[]{:S(2)}) collective-permute-start(f32[256,128]{1,0:T(8,128)S(1)} %add.35), channel_id=1, source_target_pairs={{0,6},{6,0},{2,4},{4,2},{1,7},{7,1},{3,5},{5,3},{8,14},{14,8},{10,... | collective-permute-start | bytes 393224 | tf_op jit(solution)/shard_map/ppermute | solution.py:459
  63.8 0.3 collective-permute-start.2
  64.1 3.9 %low.1 = f32[32,256]{1,0:T(8,128)S(1)} custom-call(bf16[4,256,2048]{2,1,0:T(8,128)(2,1)S(1)} %copy-done.1, bf16[128,2048]{1,0:T(8,128)(2,1)S(1)} %reshape_squeeze.3.x_ref, bf16[4,256,2048]{2,1,0:T(8,128)(2,1)S(1)} %get-tuple-element.35.back_ref, bf16[2,256,256]{2,1,0:T(8,128)(2,1)S(1)} %bitcast.18), custom_call_target="tpu_custom_call" | custom-call | flops 1474560000 | bytes 8388608 | tf_op jit(solution)/shard_map/low/pallas_call | solution.py:413
  68.1 2.5 %collective-permute-start.10 = (f32[32,256]{1,0:T(8,128)S(1)}, f32[32,256]{1,0:T(8,128)S(1)}, u32[]{:S(2)}, u32[]{:S(2)}) collective-permute-start(f32[32,256]{1,0:T(8,128)S(1)} %low.1), channel_id=1, source_target_pairs={{0,6},{2,0},{4,2},{6,4},{1,7},{3,1},{5,3},{7,5},{8,14},{10,8},{12,... | collective-permute-start | bytes 98312 | tf_op jit(solution)/shard_map/ppermute | solution.py:480
  70.6 0.7 collective-permute-start.8
  71.3 2.4 %collective-permute-start.7 = (f32[256,128]{1,0:T(8,128)S(1)}, f32[256,128]{1,0:T(8,128)S(1)}, u32[]{:S(2)}, u32[]{:S(2)}) collective-permute-start(f32[256,128]{1,0:T(8,128)S(1)} %add.36.b_ref), channel_id=1, source_target_pairs={{0,1},{1,0},{2,3},{3,2},{4,5},{5,4},{6,7},{7,6},{8,9},{9,8},{10,11... | collective-permute-start | bytes 393224 | tf_op jit(solution)/shard_map/ppermute | solution.py:485
  73.8 0.1 collective-permute-start.3
  73.9 1.0 %collective-permute-done.9 = f32[32,256]{1,0:T(8,128)S(1)} collective-permute-done((f32[32,256]{1,0:T(8,128)S(1)}, f32[32,256]{1,0:T(8,128)S(1)}, u32[]{:S(2)}, u32[]{:S(2)}) %collective-permute-start.9) | collective-permute-done | bytes 32800 | tf_op jit(solution)/shard_map/ppermute | solution.py:480
  75.0 3.3 %collective-permute-start.11 = (f32[32,256]{1,0:T(8,128)S(1)}, f32[32,256]{1,0:T(8,128)S(1)}, u32[]{:S(2)}, u32[]{:S(2)}) collective-permute-start(f32[32,256]{1,0:T(8,128)S(1)} %add_add_fusion.c_ref), channel_id=1, source_target_pairs={{0,1},{1,0},{2,3},{3,2},{4,5},{5,4},{6,7},{7,6},{8,9},{9,8},{10,11... | collective-permute-start | bytes 98312 | tf_op jit(solution)/shard_map/ppermute | solution.py:485
  78.3 0.9 %collective-permute-done.11.c_other = f32[32,256]{1,0:T(8,128)S(1)} collective-permute-done((f32[32,256]{1,0:T(8,128)S(1)}, f32[32,256]{1,0:T(8,128)S(1)}, u32[]{:S(2)}, u32[]{:S(2)}) %collective-permute-start.11) | collective-permute-done | bytes 32800 | tf_op jit(solution)/shard_map/ppermute | solution.py:485
  79.1 1.4 %unpack.1 = (f32[32,256]{1,0:T(8,128)}, f32[2,256,256]{2,1,0:T(8,128)}, f32[4,256]{1,0:T(4,128)}) custom-call(s32[2]{0:T(128)S(1)} %pad_add_fusion.place_ref, f32[264,128]{1,0:T(8,128)S(1)} %add.33.a_ref, f32[264,128]{1,0:T(8,128)S(1)} %collective-permute-done.3.a_other, f32[256,128]{1,0:T(8,128)S(1)} %add.36.b_ref, ...), custom_call_target="tpu_custom_call" | custom-call | tf_op jit(solution)/shard_map/unpack/pallas_call | solution.py:429
  (30 shorter events, 0.2 us)
Async XLA Ops:
  1.8 21.6 %copy-start.5 = (s32[2048,32]{0,1:T(8,128)S(1)}, s32[2048,32]{0,1:T(8,128)}, u32[]{:S(2)}) copy-start(s32[2048,32]{0,1:T(8,128)} %param.11) | copy-start | bytes 786436
  11.4 28.3 %all-to-all-start = ((f32[32,32,128]{2,1,0:T(8,128)}), f32[32,32,128]{2,1,0:T(8,128)S(1)}, u32[]{:S(2)}, u32[]{:S(2)}) async-start(f32[32,32,128]{2,1,0:T(8,128)} %get-tuple-element.27), calls=%async_computation | async-start | bytes 1048576 | tf_op jit(solution)/shard_map/all_to_all | solution.py:471
  23.6 16.1 %copy-start.4 = (bf16[1,256,4]{1,2,0:T(4,128)(2,1)S(1)}, bf16[1,256,4]{1,2,0:T(4,128)(2,1)}, u32[]{:S(2)}) copy-start(bf16[1,256,4]{1,2,0:T(4,128)(2,1)} %param.15) | copy-start | bytes 6148
  39.7 9.4 %copy-start = (bf16[4,256,2048]{2,1,0:T(8,128)(2,1)S(1)}, bf16[4,256,2048]{2,1,0:T(8,128)(2,1)}, u32[]{:S(2)}) copy-start(bf16[4,256,2048]{2,1,0:T(8,128)(2,1)} %get-tuple-element.22.low_hid.hid_ref) | copy-start | bytes 12582916
  39.7 9.4 %copy-start.2 = (bf16[4,256,2048]{2,1,0:T(8,128)(2,1)S(1)}, bf16[4,256,2048]{2,1,0:T(8,128)(2,1)}, u32[]{:S(2)}) copy-start(bf16[4,256,2048]{2,1,0:T(8,128)(2,1)} %get-tuple-element.30.slope_ref) | copy-start | bytes 12582916
  39.7 9.4 %copy-start.3 = (bf16[1,2,256,256]{3,2,1,0:T(8,128)(2,1)S(1)}, bf16[1,2,256,256]{3,2,1,0:T(8,128)(2,1)}, u32[]{:S(2)}) copy-start(bf16[1,2,256,256]{3,2,1,0:T(8,128)(2,1)} %param.14) | copy-start | bytes 786436
  46.6 6.9 %collective-permute-start = (f32[264,128]{1,0:T(8,128)S(1)}, f32[264,128]{1,0:T(8,128)S(1)}, u32[]{:S(2)}, u32[]{:S(2)}) collective-permute-start(f32[264,128]{1,0:T(8,128)S(1)} %get-tuple-element.29), channel_id=1, source_target_pairs={{0,1},{1,0},{2,3},{3,2},{4,5},{5,4},{6,7},{7,6},{8,9},{9,8},{10,11... | collective-permute-start | bytes 405512 | tf_op jit(solution)/shard_map/ppermute | solution.py:454
  49.2 15.0 %copy-start.1 = (bf16[4,256,2048]{2,1,0:T(8,128)(2,1)S(1)}, bf16[4,256,2048]{2,1,0:T(8,128)(2,1)}, u32[]{:S(2)}) copy-start(bf16[4,256,2048]{2,1,0:T(8,128)(2,1)} %get-tuple-element.34.slope_ref) | copy-start | bytes 12582916
  53.4 1.5 %collective-permute-start.4 = (f32[256,128]{1,0:T(8,128)S(1)}, f32[256,128]{1,0:T(8,128)S(1)}, u32[]{:S(2)}, u32[]{:S(2)}) collective-permute-start(f32[256,128]{1,0:T(8,128)S(1)} %get-tuple-element.33), channel_id=1, source_target_pairs={{0,1},{1,0},{2,3},{3,2},{4,5},{5,4},{6,7},{7,6},{8,9},{9,8},{10,11... | collective-permute-start | bytes 393224 | tf_op jit(solution)/shard_map/ppermute | solution.py:454
  53.6 10.2 %collective-permute-start.1 = (f32[264,128]{1,0:T(8,128)S(1)}, f32[264,128]{1,0:T(8,128)S(1)}, u32[]{:S(2)}, u32[]{:S(2)}) collective-permute-start(f32[264,128]{1,0:T(8,128)S(1)} %add.31), channel_id=1, source_target_pairs={{0,2},{2,0},{4,6},{6,4},{1,3},{3,1},{5,7},{7,5},{8,10},{10,8},{12,... | collective-permute-start | bytes 405512 | tf_op jit(solution)/shard_map/ppermute | solution.py:459
  54.9 6.3 %collective-permute-start.5 = (f32[256,128]{1,0:T(8,128)S(1)}, f32[256,128]{1,0:T(8,128)S(1)}, u32[]{:S(2)}, u32[]{:S(2)}) collective-permute-start(f32[256,128]{1,0:T(8,128)S(1)} %add.34), channel_id=1, source_target_pairs={{0,2},{2,0},{4,6},{6,4},{1,3},{3,1},{5,7},{7,5},{8,10},{10,8},{12,... | collective-permute-start | bytes 393224 | tf_op jit(solution)/shard_map/ppermute | solution.py:459
  61.3 10.0 %collective-permute-start.6 = (f32[256,128]{1,0:T(8,128)S(1)}, f32[256,128]{1,0:T(8,128)S(1)}, u32[]{:S(2)}, u32[]{:S(2)}) collective-permute-start(f32[256,128]{1,0:T(8,128)S(1)} %add.35), channel_id=1, source_target_pairs={{0,6},{6,0},{2,4},{4,2},{1,7},{7,1},{3,5},{5,3},{8,14},{14,8},{10,... | collective-permute-start | bytes 393224 | tf_op jit(solution)/shard_map/ppermute | solution.py:459
  63.8 9.9 %collective-permute-start.2 = (f32[264,128]{1,0:T(8,128)S(1)}, f32[264,128]{1,0:T(8,128)S(1)}, u32[]{:S(2)}, u32[]{:S(2)}) collective-permute-start(f32[264,128]{1,0:T(8,128)S(1)} %add.32), channel_id=1, source_target_pairs={{0,6},{6,0},{2,4},{4,2},{1,7},{7,1},{3,5},{5,3},{8,14},{14,8},{10,... | collective-permute-start | bytes 405512 | tf_op jit(solution)/shard_map/ppermute | solution.py:459
  68.1 5.8 %collective-permute-start.10 = (f32[32,256]{1,0:T(8,128)S(1)}, f32[32,256]{1,0:T(8,128)S(1)}, u32[]{:S(2)}, u32[]{:S(2)}) collective-permute-start(f32[32,256]{1,0:T(8,128)S(1)} %low.1), channel_id=1, source_target_pairs={{0,6},{2,0},{4,2},{6,4},{1,7},{3,1},{5,3},{7,5},{8,14},{10,8},{12,... | collective-permute-start | bytes 98312 | tf_op jit(solution)/shard_map/ppermute | solution.py:480
  70.6 4.3 %collective-permute-start.9 = (f32[32,256]{1,0:T(8,128)S(1)}, f32[32,256]{1,0:T(8,128)S(1)}, u32[]{:S(2)}, u32[]{:S(2)}) collective-permute-start(f32[32,256]{1,0:T(8,128)S(1)} %low.1), channel_id=1, source_target_pairs={{0,4},{2,6},{4,0},{6,2},{1,5},{3,7},{5,1},{7,3},{8,12},{10,14},{12... | collective-permute-start | bytes 98312 | tf_op jit(solution)/shard_map/ppermute | solution.py:480
  70.6 4.3 %collective-permute-start.8 = (f32[32,256]{1,0:T(8,128)S(1)}, f32[32,256]{1,0:T(8,128)S(1)}, u32[]{:S(2)}, u32[]{:S(2)}) collective-permute-start(f32[32,256]{1,0:T(8,128)S(1)} %low.1), channel_id=1, source_target_pairs={{0,2},{2,4},{4,6},{6,0},{1,3},{3,5},{5,7},{7,1},{8,10},{10,12},{12... | collective-permute-start | bytes 98312 | tf_op jit(solution)/shard_map/ppermute | solution.py:480
  71.3 7.8 %collective-permute-start.7 = (f32[256,128]{1,0:T(8,128)S(1)}, f32[256,128]{1,0:T(8,128)S(1)}, u32[]{:S(2)}, u32[]{:S(2)}) collective-permute-start(f32[256,128]{1,0:T(8,128)S(1)} %add.36.b_ref), channel_id=1, source_target_pairs={{0,1},{1,0},{2,3},{3,2},{4,5},{5,4},{6,7},{7,6},{8,9},{9,8},{10,11... | collective-permute-start | bytes 393224 | tf_op jit(solution)/shard_map/ppermute | solution.py:485
  73.8 5.4 %collective-permute-start.3 = (f32[264,128]{1,0:T(8,128)S(1)}, f32[264,128]{1,0:T(8,128)S(1)}, u32[]{:S(2)}, u32[]{:S(2)}) collective-permute-start(f32[264,128]{1,0:T(8,128)S(1)} %add.33.a_ref), channel_id=1, source_target_pairs={{0,1},{1,0},{2,3},{3,2},{4,5},{5,4},{6,7},{7,6},{8,9},{9,8},{10,11... | collective-permute-start | bytes 405512 | tf_op jit(solution)/shard_map/ppermute | solution.py:485
  75.0 4.2 %collective-permute-start.11 = (f32[32,256]{1,0:T(8,128)S(1)}, f32[32,256]{1,0:T(8,128)S(1)}, u32[]{:S(2)}, u32[]{:S(2)}) collective-permute-start(f32[32,256]{1,0:T(8,128)S(1)} %add_add_fusion.c_ref), channel_id=1, source_target_pairs={{0,1},{1,0},{2,3},{3,2},{4,5},{5,4},{6,7},{7,6},{8,9},{9,8},{10,11... | collective-permute-start | bytes 98312 | tf_op jit(solution)/shard_map/ppermute | solution.py:485

commit v4 on v3

--- a/solution.py
+++ b/solution.py
@@ -67,12 +67,17 @@
             given[r, 5:8, :] = cot_ref[:, lanes]
 
     row16 = lax.broadcasted_iota(jnp.int32, (4 * SAMP, W), 0) & 3
-    for part in range(tile // PART):
+    parts = range(tile // PART)
+    halves = []
+    for part in parts:
         rays = pl.ds(pl.multiple_of(step * tile + part * PART, PART), PART)
-        wide = spread(x_ref[:, rays], jnp.zeros((), BF16))
-        half = dot(w1t[...], wide, 1, 0)
-        for k in range(3):
+        halves.append(dot(w1t[...], spread(x_ref[:, rays], jnp.zeros((), BF16)), 1, 0))
+    for k in range(3):
+        hiddens = []
+        for part in parts:
+            half = halves[part]
             hidden = (half + half * jnp.tanh(half)).astype(BF16)
+            hiddens.append(hidden)
             for s in range(SAMP):
                 cols = slice(s * PART, (s + 1) * PART)
                 put = slice(s * tile + part * PART, s * tile + (part + 1) * PART)
@@ -81,12 +86,13 @@
                 else:
                     hid_ref[0, k - 1, :, put] = hidden[:, cols]
             if k < 2:
-                half = dot(wmt[k], hidden, 1, 0)
+                halves[part] = dot(wmt[k], hidden, 1, 0)
+    for part in parts:
         head = jnp.zeros((4 * SAMP, PART), F32)
         for s in range(SAMP):
             head += dot(
                 jnp.where(row16 == s, w4t[...], jnp.zeros((), BF16)),
-                hidden[:, s * PART : (s + 1) * PART], 1, 0,
+                hiddens[part][:, s * PART : (s + 1) * PART], 1, 0,
             )
         for r in range(PART // 128):
             heads[step * (tile // 128) + part * (PART // 128) + r] = head[:, 128 * r : 128 * (r + 1)]
@@ -224,7 +230,7 @@
         mid[...] += dot(hid[i, 0], back, 1, 1)
         return 0
 
-    lax.fori_loop(0, steps, step, 0)
+    lax.fori_loop(0, steps, step, 0, unroll=2)
     pick8 = group_rows(4 * SAMP, 8).astype(F32)
     tail = dot(pick8, last[...], 0, 0, lax.Precision.HIGHEST)
     split(place_ref, keep_ref, send_ref, (mid[...], tail))
@@ -242,7 +248,7 @@
         mid[...] += dot(hid_ref[i], down, 1, 1)
         return 0
 
-    lax.fori_loop(0, hid_ref.shape[0], step, 0)
+    lax.fori_loop(0, hid_ref.shape[0], step, 0, unroll=2)
     split(place_ref, keep_ref, send_ref, (mid[...],))
 
 
@@ -256,7 +262,7 @@
         first[...] += dot(spread(x_ref[:, rays], jnp.zeros((), BF16)), down, 1, 1)
         return 0
 
-    lax.fori_loop(0, slope_ref.shape[0], step, 0)
+    lax.fori_loop(0, slope_ref.shape[0], step, 0, unroll=2)
     pick = group_rows(FEAT * SAMP, FEAT).astype(F32)
     out_ref[...] = dot(pick, first[...], 0, 0, lax.Precision.HIGHEST)
 
@@ -473,13 +479,13 @@
     back, *sums = top(place, hid, top_slope, ab, got, ranks, w4)
     upper = over_x(over_cores(*sums), NEAR)
     back, *sums = middle(place, low_hid, mid_slope, back, wm)
+    lower = over_x(over_cores(*sums), FAR)
+    small = low(low_slope, x, back, wm)
     upper = over_x(upper, FAR)
-    lower = over_x(over_cores(*sums), NEAR)
-    small = low(low_slope, x, back, wm)
     small = small + sum(
         lax.ppermute(small, "x", [(i, (i + s) % 4) for i in range(4)]) for s in (1, 2, 3)
     )
-    lower = over_x(lower, FAR)
+    lower = over_x(lower, NEAR)
     parts = []
     for part in (upper, lower, small):
         parts += [part, lax.ppermute(part, "core", PAIR)]

time: 80.8 us -> 78 us (0.965)
  Pallas kernels: 36.6 us -> 34.1 us
  waiting for transfers between devices: 12.6 us -> 11.7 us
    ppermute x4, waiting for transfers between devices: 5.14 us -> 3.53 us  [over_x(): got = lax.ppermute(value, 'x', ring)]
    pallas_call x1, Pallas kernels: 9.57 us -> 8.61 us  [forward(): pl.pallas_call(forward_kernel, grid=(rays // TILE,), in_specs=[inside, pl...]
    ppermute x4, starting transfers between devices: 5.35 us -> 6.29 us  [over_x(): got = lax.ppermute(value, 'x', ring)]
  transfers between devices with their start and end apart: 13 -> 13, of which waited for: 4 -> 4; matrix products, arithmetic and copies ran while one was open for 0% -> 0% of each run, Pallas kernels for 23% -> 22%
where the time goes in v4:
time: 78 us; the launch traced here: 77.7 us
  Pallas kernels  34.1 us (44%)
  starting transfers between devices  29.7 us (38%)
  waiting for transfers between devices  11.7 us (15%)
  local copies, waits for them, and re-layouts  1.24 us (2%)
    all_to_all x1, starting transfers between devices, per_device(): got = lax.all_to_all(pay, ('z', 'y'), 0, 0, tiled=True)  12 us
    pallas_call x1, Pallas kernels, slopes(): pl.pallas_call(slope_kernel, grid=(steps,), in_specs=[inside, block, pl.B...  10.6 us
    pallas_call x1, Pallas kernels, forward(): pl.pallas_call(forward_kernel, grid=(rays // TILE,), in_specs=[inside, pl...  8.61 us
    pallas_call x1, Pallas kernels, top(): pl.pallas_call(top_kernel, in_specs=[pl.BlockSpec(memory_space=SMEM)] + [...  6.76 us
    ppermute x4, starting transfers between devices, over_x(): got = lax.ppermute(value, 'x', ring)  6.29 us
    ppermute x3, starting transfers between devices, per_device(): parts += [part, lax.ppermute(part, 'core', PAIR)]  5.63 us
    all_to_all x1, waiting for transfers between devices, per_device(): got = lax.all_to_all(pay, ('z', 'y'), 0, 0, tiled=True)  5.5 us
    ppermute x4, waiting for transfers between devices, over_x(): got = lax.ppermute(value, 'x', ring)  3.53 us
  transfers between devices with their start and end apart: 13, of which 4 were waited for; matrix products, arithmetic and copies ran while one was open for 0% of the time, Pallas kernels for 22%

profile of v4, /device:TPU:1, one launch (start us, length us, event | category | flops | bytes accessed | tf_op | source)
XLA Modules:
  0.0 77.7 jit_solution(1534211065813081975)
XLA Ops:
  0.6 1.2 %reshape_squeeze.3.x_ref = bf16[128,2048]{1,0:T(8,128)(2,1)S(1)} reshape(bf16[1,32,4,2048]{3,2,1,0:T(4,128)(2,1)} %param.8) | data formatting | bytes 1048576 | tf_op jit(solution)/shard_map/reshape;squeeze | solution.py:472
  1.8 8.6 %forward.1 = (bf16[4,2,256,2048]{3,2,1,0:T(8,128)(2,1)}, bf16[4,256,2048]{2,1,0:T(8,128)(2,1)}, f32[20,16,128]{2,1,0:T(8,128)S(1)}, f32[32,32,128]{2,1,0:T(8,128...) custom-call(bf16[128,2048]{1,0:T(8,128)(2,1)S(1)} %reshape_squeeze.3.x_ref, f32[4,2048]{1,0:T(4,128)} %bitcast.24, ...), custom_call_target="tpu_custom_call" | custom-call | flops 2298478592 | bytes 1048576 | tf_op jit(solution)/shard_map/forward/pallas_call | solution.py:303
  10.4 12.0 %all-to-all-start = ((f32[32,32,128]{2,1,0:T(8,128)}), f32[32,32,128]{2,1,0:T(8,128)S(1)}, u32[]{:S(2)}, u32[]{:S(2)}) async-start(f32[32,32,128]{2,1,0:T(8,128)} %get-tuple-element.27), calls=%async_computation | async-start | bytes 1048576 | tf_op jit(solution)/shard_map/all_to_all | solution.py:477
  22.5 0.1 pad_add_fusion.place_ref
  22.6 10.6 %slopes.1 = (bf16[4,256,2048]{2,1,0:T(8,128)(2,1)}, bf16[4,256,2048]{2,1,0:T(8,128)(2,1)}, bf16[4,256,2048]{2,1,0:T(8,128)(2,1)}) custom-call(bf16[128,2048]{1,0:T(8,128)(2,1)S(1)} %reshape_squeeze.3.x_ref, bf16[4,256,2048]{2,1,0:T(8,128)(2,1)} %get-tuple-element.22.low_hid.hid_ref, bf16[4,2,256,2048]{3,2,1,0:T(8,128)(2,1)} %get-tuple-element.21.mid_hid.hid_hbm, ...), custom_call_target="tpu_custom_call" | custom-call | flops 2293760000 | bytes 20971520 | tf_op jit(solution)/shard_map/slopes/pallas_call | solution.py:345
  33.2 5.5 %all-to-all-done.got_ref = f32[32,32,128]{2,1,0:T(8,128)S(1)} async-done(((f32[32,32,128]{2,1,0:T(8,128)}), f32[32,32,128]{2,1,0:T(8,128)S(1)}, u32[]{:S(2)}, u32[]{:S(2)}) %all-to-all-start) | async-done | bytes 524320 | tf_op jit(solution)/shard_map/all_to_all | solution.py:477
  38.8 6.8 %top.1 = (bf16[4,256,2048]{2,1,0:T(8,128)(2,1)S(1)}, f32[264,128]{1,0:T(8,128)S(1)}, f32[264,128]{1,0:T(8,128)S(1)}) custom-call(s32[2]{0:T(128)S(1)} %pad_add_fusion.place_ref, bf16[4,2,256,2048]{3,2,1,0:T(8,128)(2,1)} %get-tuple-element.21.mid_hid.hid_hbm, bf16[4,256,2048]{2,1,0:T(8,128)(2,1)} %get-tuple-element.25.slope_hbm, ...), custom_call_target="tpu_custom_call" | custom-call | flops 1310720000 | bytes 12582912 | tf_op jit(solution)/shard_map/top/pallas_call | solution.py:368
  45.5 2.5 %collective-permute-start = (f32[264,128]{1,0:T(8,128)S(1)}, f32[264,128]{1,0:T(8,128)S(1)}, u32[]{:S(2)}, u32[]{:S(2)}) collective-permute-start(f32[264,128]{1,0:T(8,128)S(1)} %get-tuple-element.29), channel_id=1, source_target_pairs={{0,1},{1,0},{2,3},{3,2},{4,5},{5,4},{6,7},{7,6},{8,9},{9,8},{10,11... | collective-permute-start | bytes 405512 | tf_op jit(solution)/shard_map/ppermute | solution.py:460
  48.0 3.5 %middle.1 = (bf16[4,256,2048]{2,1,0:T(8,128)(2,1)S(1)}, f32[256,128]{1,0:T(8,128)S(1)}, f32[256,128]{1,0:T(8,128)S(1)}) custom-call(s32[2]{0:T(128)S(1)} %pad_add_fusion.place_ref, bf16[4,256,2048]{2,1,0:T(8,128)(2,1)S(1)} %copy-done, bf16[4,256,2048]{2,1,0:T(8,128)(2,1)S(1)} %copy-done.2, bf16[4,256,2048]{2,1,0:T(8,128)(2,1)S(1)} %get-tuple-element.31.back_ref, ...), custom_call_target="tpu_custom_call" | custom-call | flops 2147483648 | bytes 8388608 | tf_op jit(solution)/shard_map/middle/pallas_call | solution.py:398
  51.5 0.4 collective-permute-start.4
  51.9 1.3 %collective-permute-start.1 = (f32[264,128]{1,0:T(8,128)S(1)}, f32[264,128]{1,0:T(8,128)S(1)}, u32[]{:S(2)}, u32[]{:S(2)}) collective-permute-start(f32[264,128]{1,0:T(8,128)S(1)} %add.31), channel_id=1, source_target_pairs={{0,2},{2,0},{4,6},{6,4},{1,3},{3,1},{5,7},{7,5},{8,10},{10,8},{12,... | collective-permute-start | bytes 405512 | tf_op jit(solution)/shard_map/ppermute | solution.py:465
  53.2 2.3 %collective-permute-start.5 = (f32[256,128]{1,0:T(8,128)S(1)}, f32[256,128]{1,0:T(8,128)S(1)}, u32[]{:S(2)}, u32[]{:S(2)}) collective-permute-start(f32[256,128]{1,0:T(8,128)S(1)} %add.34), channel_id=1, source_target_pairs={{0,6},{6,0},{2,4},{4,2},{1,7},{7,1},{3,5},{5,3},{8,14},{14,8},{10,... | collective-permute-start | bytes 393224 | tf_op jit(solution)/shard_map/ppermute | solution.py:465
  55.5 3.5 %collective-permute-done.5 = f32[256,128]{1,0:T(8,128)S(1)} collective-permute-done((f32[256,128]{1,0:T(8,128)S(1)}, f32[256,128]{1,0:T(8,128)S(1)}, u32[]{:S(2)}, u32[]{:S(2)}) %collective-permute-start.5) | collective-permute-done | bytes 131104 | tf_op jit(solution)/shard_map/ppermute | solution.py:465
  59.1 0.1 collective-permute-start.6
  59.2 2.6 %collective-permute-start.2 = (f32[264,128]{1,0:T(8,128)S(1)}, f32[264,128]{1,0:T(8,128)S(1)}, u32[]{:S(2)}, u32[]{:S(2)}) collective-permute-start(f32[264,128]{1,0:T(8,128)S(1)} %add.32), channel_id=1, source_target_pairs={{0,6},{6,0},{2,4},{4,2},{1,7},{7,1},{3,5},{5,3},{8,14},{14,8},{10,... | collective-permute-start | bytes 405512 | tf_op jit(solution)/shard_map/ppermute | solution.py:465
  61.8 3.3 %low.1 = f32[32,256]{1,0:T(8,128)S(1)} custom-call(bf16[4,256,2048]{2,1,0:T(8,128)(2,1)S(1)} %copy-done.1, bf16[128,2048]{1,0:T(8,128)(2,1)S(1)} %reshape_squeeze.3.x_ref, bf16[4,256,2048]{2,1,0:T(8,128)(2,1)S(1)} %get-tuple-element.35.back_ref, bf16[2,256,256]{2,1,0:T(8,128)(2,1)S(1)} %bitcast.18), custom_call_target="tpu_custom_call" | custom-call | flops 1474560000 | bytes 8388608 | tf_op jit(solution)/shard_map/low/pallas_call | solution.py:419
  65.1 0.5 collective-permute-start.10
  65.5 2.4 %collective-permute-start.9 = (f32[32,256]{1,0:T(8,128)S(1)}, f32[32,256]{1,0:T(8,128)S(1)}, u32[]{:S(2)}, u32[]{:S(2)}) collective-permute-start(f32[32,256]{1,0:T(8,128)S(1)} %low.1), channel_id=1, source_target_pairs={{0,4},{2,6},{4,0},{6,2},{1,5},{3,7},{5,1},{7,3},{8,12},{10,14},{12... | collective-permute-start | bytes 98312 | tf_op jit(solution)/shard_map/ppermute | solution.py:486
  68.0 2.3 %collective-permute-start.7 = (f32[256,128]{1,0:T(8,128)S(1)}, f32[256,128]{1,0:T(8,128)S(1)}, u32[]{:S(2)}, u32[]{:S(2)}) collective-permute-start(f32[256,128]{1,0:T(8,128)S(1)} %add.36.b_ref), channel_id=1, source_target_pairs={{0,1},{1,0},{2,3},{3,2},{4,5},{5,4},{6,7},{7,6},{8,9},{9,8},{10,11... | collective-permute-start | bytes 393224 | tf_op jit(solution)/shard_map/ppermute | solution.py:491
  70.3 0.1 collective-permute-start.3
  70.4 1.8 %collective-permute-done.8 = f32[32,256]{1,0:T(8,128)S(1)} collective-permute-done((f32[32,256]{1,0:T(8,128)S(1)}, f32[32,256]{1,0:T(8,128)S(1)}, u32[]{:S(2)}, u32[]{:S(2)}) %collective-permute-start.8) | collective-permute-done | bytes 32800 | tf_op jit(solution)/shard_map/ppermute | solution.py:486
  72.2 3.2 %collective-permute-start.11 = (f32[32,256]{1,0:T(8,128)S(1)}, f32[32,256]{1,0:T(8,128)S(1)}, u32[]{:S(2)}, u32[]{:S(2)}) collective-permute-start(f32[32,256]{1,0:T(8,128)S(1)} %add_add_fusion.c_ref), channel_id=1, source_target_pairs={{0,1},{1,0},{2,3},{3,2},{4,5},{5,4},{6,7},{7,6},{8,9},{9,8},{10,11... | collective-permute-start | bytes 98312 | tf_op jit(solution)/shard_map/ppermute | solution.py:491
  75.4 0.9 %collective-permute-done.11.c_other = f32[32,256]{1,0:T(8,128)S(1)} collective-permute-done((f32[32,256]{1,0:T(8,128)S(1)}, f32[32,256]{1,0:T(8,128)S(1)}, u32[]{:S(2)}, u32[]{:S(2)}) %collective-permute-start.11) | collective-permute-done | bytes 32800 | tf_op jit(solution)/shard_map/ppermute | solution.py:491
  76.3 1.4 %unpack.1 = (f32[32,256]{1,0:T(8,128)}, f32[2,256,256]{2,1,0:T(8,128)}, f32[4,256]{1,0:T(4,128)}) custom-call(s32[2]{0:T(128)S(1)} %pad_add_fusion.place_ref, f32[264,128]{1,0:T(8,128)S(1)} %add.33.a_ref, f32[264,128]{1,0:T(8,128)S(1)} %collective-permute-done.3.a_other, f32[256,128]{1,0:T(8,128)S(1)} %add.36.b_ref, ...), custom_call_target="tpu_custom_call" | custom-call | tf_op jit(solution)/shard_map/unpack/pallas_call | solution.py:435
  (30 shorter events, 0.2 us)
Async XLA Ops:
  1.8 20.7 %copy-start.5 = (s32[2048,32]{0,1:T(8,128)S(1)}, s32[2048,32]{0,1:T(8,128)}, u32[]{:S(2)}) copy-start(s32[2048,32]{0,1:T(8,128)} %param.11) | copy-start | bytes 786436
  10.4 28.3 %all-to-all-start = ((f32[32,32,128]{2,1,0:T(8,128)}), f32[32,32,128]{2,1,0:T(8,128)S(1)}, u32[]{:S(2)}, u32[]{:S(2)}) async-start(f32[32,32,128]{2,1,0:T(8,128)} %get-tuple-element.27), calls=%async_computation | async-start | bytes 1048576 | tf_op jit(solution)/shard_map/all_to_all | solution.py:477
  22.6 16.1 %copy-start.4 = (bf16[1,256,4]{1,2,0:T(4,128)(2,1)S(1)}, bf16[1,256,4]{1,2,0:T(4,128)(2,1)}, u32[]{:S(2)}) copy-start(bf16[1,256,4]{1,2,0:T(4,128)(2,1)} %param.15) | copy-start | bytes 6148
  38.7 9.3 %copy-start = (bf16[4,256,2048]{2,1,0:T(8,128)(2,1)S(1)}, bf16[4,256,2048]{2,1,0:T(8,128)(2,1)}, u32[]{:S(2)}) copy-start(bf16[4,256,2048]{2,1,0:T(8,128)(2,1)} %get-tuple-element.22.low_hid.hid_ref) | copy-start | bytes 12582916
  38.8 9.3 %copy-start.2 = (bf16[4,256,2048]{2,1,0:T(8,128)(2,1)S(1)}, bf16[4,256,2048]{2,1,0:T(8,128)(2,1)}, u32[]{:S(2)}) copy-start(bf16[4,256,2048]{2,1,0:T(8,128)(2,1)} %get-tuple-element.30.slope_ref) | copy-start | bytes 12582916
  38.8 9.3 %copy-start.3 = (bf16[1,2,256,256]{3,2,1,0:T(8,128)(2,1)S(1)}, bf16[1,2,256,256]{3,2,1,0:T(8,128)(2,1)}, u32[]{:S(2)}) copy-start(bf16[1,2,256,256]{3,2,1,0:T(8,128)(2,1)} %param.14) | copy-start | bytes 786436
  45.5 6.4 %collective-permute-start = (f32[264,128]{1,0:T(8,128)S(1)}, f32[264,128]{1,0:T(8,128)S(1)}, u32[]{:S(2)}, u32[]{:S(2)}) collective-permute-start(f32[264,128]{1,0:T(8,128)S(1)} %get-tuple-element.29), channel_id=1, source_target_pairs={{0,1},{1,0},{2,3},{3,2},{4,5},{5,4},{6,7},{7,6},{8,9},{9,8},{10,11... | collective-permute-start | bytes 405512 | tf_op jit(solution)/shard_map/ppermute | solution.py:460
  48.0 13.8 %copy-start.1 = (bf16[4,256,2048]{2,1,0:T(8,128)(2,1)S(1)}, bf16[4,256,2048]{2,1,0:T(8,128)(2,1)}, u32[]{:S(2)}) copy-start(bf16[4,256,2048]{2,1,0:T(8,128)(2,1)} %get-tuple-element.34.slope_ref) | copy-start | bytes 12582916
  51.5 1.7 %collective-permute-start.4 = (f32[256,128]{1,0:T(8,128)S(1)}, f32[256,128]{1,0:T(8,128)S(1)}, u32[]{:S(2)}, u32[]{:S(2)}) collective-permute-start(f32[256,128]{1,0:T(8,128)S(1)} %get-tuple-element.33), channel_id=1, source_target_pairs={{0,1},{1,0},{2,3},{3,2},{4,5},{5,4},{6,7},{7,6},{8,9},{9,8},{10,11... | collective-permute-start | bytes 393224 | tf_op jit(solution)/shard_map/ppermute | solution.py:460
  51.9 7.3 %collective-permute-start.1 = (f32[264,128]{1,0:T(8,128)S(1)}, f32[264,128]{1,0:T(8,128)S(1)}, u32[]{:S(2)}, u32[]{:S(2)}) collective-permute-start(f32[264,128]{1,0:T(8,128)S(1)} %add.31), channel_id=1, source_target_pairs={{0,2},{2,0},{4,6},{6,4},{1,3},{3,1},{5,7},{7,5},{8,10},{10,8},{12,... | collective-permute-start | bytes 405512 | tf_op jit(solution)/shard_map/ppermute | solution.py:465
  53.2 5.8 %collective-permute-start.5 = (f32[256,128]{1,0:T(8,128)S(1)}, f32[256,128]{1,0:T(8,128)S(1)}, u32[]{:S(2)}, u32[]{:S(2)}) collective-permute-start(f32[256,128]{1,0:T(8,128)S(1)} %add.34), channel_id=1, source_target_pairs={{0,6},{6,0},{2,4},{4,2},{1,7},{7,1},{3,5},{5,3},{8,14},{14,8},{10,... | collective-permute-start | bytes 393224 | tf_op jit(solution)/shard_map/ppermute | solution.py:465
  59.1 8.9 %collective-permute-start.6 = (f32[256,128]{1,0:T(8,128)S(1)}, f32[256,128]{1,0:T(8,128)S(1)}, u32[]{:S(2)}, u32[]{:S(2)}) collective-permute-start(f32[256,128]{1,0:T(8,128)S(1)} %add.35), channel_id=1, source_target_pairs={{0,2},{2,0},{4,6},{6,4},{1,3},{3,1},{5,7},{7,5},{8,10},{10,8},{12,... | collective-permute-start | bytes 393224 | tf_op jit(solution)/shard_map/ppermute | solution.py:465
  59.2 11.1 %collective-permute-start.2 = (f32[264,128]{1,0:T(8,128)S(1)}, f32[264,128]{1,0:T(8,128)S(1)}, u32[]{:S(2)}, u32[]{:S(2)}) collective-permute-start(f32[264,128]{1,0:T(8,128)S(1)} %add.32), channel_id=1, source_target_pairs={{0,6},{6,0},{2,4},{4,2},{1,7},{7,1},{3,5},{5,3},{8,14},{14,8},{10,... | collective-permute-start | bytes 405512 | tf_op jit(solution)/shard_map/ppermute | solution.py:465
  65.1 5.4 %collective-permute-start.10 = (f32[32,256]{1,0:T(8,128)S(1)}, f32[32,256]{1,0:T(8,128)S(1)}, u32[]{:S(2)}, u32[]{:S(2)}) collective-permute-start(f32[32,256]{1,0:T(8,128)S(1)} %low.1), channel_id=1, source_target_pairs={{0,6},{2,0},{4,2},{6,4},{1,7},{3,1},{5,3},{7,5},{8,14},{10,8},{12,... | collective-permute-start | bytes 98312 | tf_op jit(solution)/shard_map/ppermute | solution.py:486
  65.5 4.9 %collective-permute-start.9 = (f32[32,256]{1,0:T(8,128)S(1)}, f32[32,256]{1,0:T(8,128)S(1)}, u32[]{:S(2)}, u32[]{:S(2)}) collective-permute-start(f32[32,256]{1,0:T(8,128)S(1)} %low.1), channel_id=1, source_target_pairs={{0,4},{2,6},{4,0},{6,2},{1,5},{3,7},{5,1},{7,3},{8,12},{10,14},{12... | collective-permute-start | bytes 98312 | tf_op jit(solution)/shard_map/ppermute | solution.py:486
  67.9 4.3 %collective-permute-start.8 = (f32[32,256]{1,0:T(8,128)S(1)}, f32[32,256]{1,0:T(8,128)S(1)}, u32[]{:S(2)}, u32[]{:S(2)}) collective-permute-start(f32[32,256]{1,0:T(8,128)S(1)} %low.1), channel_id=1, source_target_pairs={{0,2},{2,4},{4,6},{6,0},{1,3},{3,5},{5,7},{7,1},{8,10},{10,12},{12... | collective-permute-start | bytes 98312 | tf_op jit(solution)/shard_map/ppermute | solution.py:486
  68.0 8.3 %collective-permute-start.7 = (f32[256,128]{1,0:T(8,128)S(1)}, f32[256,128]{1,0:T(8,128)S(1)}, u32[]{:S(2)}, u32[]{:S(2)}) collective-permute-start(f32[256,128]{1,0:T(8,128)S(1)} %add.36.b_ref), channel_id=1, source_target_pairs={{0,1},{1,0},{2,3},{3,2},{4,5},{5,4},{6,7},{7,6},{8,9},{9,8},{10,11... | collective-permute-start | bytes 393224 | tf_op jit(solution)/shard_map/ppermute | solution.py:491
  70.3 6.0 %collective-permute-start.3 = (f32[264,128]{1,0:T(8,128)S(1)}, f32[264,128]{1,0:T(8,128)S(1)}, u32[]{:S(2)}, u32[]{:S(2)}) collective-permute-start(f32[264,128]{1,0:T(8,128)S(1)} %add.33.a_ref), channel_id=1, source_target_pairs={{0,1},{1,0},{2,3},{3,2},{4,5},{5,4},{6,7},{7,6},{8,9},{9,8},{10,11... | collective-permute-start | bytes 405512 | tf_op jit(solution)/shard_map/ppermute | solution.py:491
  72.2 4.0 %collective-permute-start.11 = (f32[32,256]{1,0:T(8,128)S(1)}, f32[32,256]{1,0:T(8,128)S(1)}, u32[]{:S(2)}, u32[]{:S(2)}) collective-permute-start(f32[32,256]{1,0:T(8,128)S(1)} %add_add_fusion.c_ref), channel_id=1, source_target_pairs={{0,1},{1,0},{2,3},{3,2},{4,5},{5,4},{6,7},{7,6},{8,9},{9,8},{10,11... | collective-permute-start | bytes 98312 | tf_op jit(solution)/shard_map/ppermute | solution.py:491

commit v5 on v4

--- a/solution.py
+++ b/solution.py
@@ -264,20 +264,24 @@
 
     lax.fori_loop(0, slope_ref.shape[0], step, 0, unroll=2)
     pick = group_rows(FEAT * SAMP, FEAT).astype(F32)
-    out_ref[...] = dot(pick, first[...], 0, 0, lax.Precision.HIGHEST)
+    small = dot(pick, first[...], 0, 0, lax.Precision.HIGHEST)
+    out_ref[:FEAT] = small[:, :128]
+    out_ref[FEAT:] = small[:, 128:]
 
 
 def unpack_kernel(
-    place_ref, a_ref, a_other, b_ref, b_other, c_ref, c_other, first_ref, mid_ref, last_ref
+    place_ref, a_ref, a_other, b_ref, b_other, first_ref, mid_ref, last_ref
 ):
-    first_ref[...] = c_ref[...] + c_other[...]
     for side in range(2):
         cols = slice(128 * side, 128 * (side + 1))
+
+        rows = slice(256 + FEAT * side, 256 + FEAT * (side + 1))
+        first_ref[:, cols] = b_ref[rows, :] + b_other[rows, :]
 
         def emit(up, down):
             mid_ref[1, :, cols] = up[0:256, :]
             last_ref[:, cols] = up[256:260, :]
-            mid_ref[0, :, cols] = down[...]
+            mid_ref[0, :, cols] = down[0:256, :]
 
         @pl.when(place_ref[1] == side)
         def _():
@@ -420,7 +424,7 @@
         low_kernel,
         in_specs=[inside] * 4,
         out_specs=inside,
-        out_shape=pltpu.VMEM((FEAT, W), F32),
+        out_shape=pltpu.VMEM((2 * FEAT, 128), F32),
         scratch_shapes=[pltpu.VMEM((FEAT * SAMP, W), F32), pltpu.VMEM((W, W), BF16)],
         compiler_params=pltpu.CompilerParams(vmem_limit_bytes=12 * MIB),
         cost_estimate=pl.CostEstimate(
@@ -435,7 +439,7 @@
     return pl.pallas_call(
         unpack_kernel,
         grid=(1,),
-        in_specs=[pl.BlockSpec(memory_space=SMEM)] + [inside] * 6,
+        in_specs=[pl.BlockSpec(memory_space=SMEM)] + [inside] * 4,
         out_specs=[
             pl.BlockSpec((FEAT, W), lambda i: (0, 0)),
             pl.BlockSpec((2, W, W), lambda i: (0, 0, 0)),
@@ -477,17 +481,15 @@
     got = lax.all_to_all(pay, ("z", "y"), 0, 0, tiled=True)
     low_slope, mid_slope, top_slope = slopes(x, low_hid, hid, w1t, wmt)
     back, *sums = top(place, hid, top_slope, ab, got, ranks, w4)
-    upper = over_x(over_cores(*sums), NEAR)
+    upper = over_cores(*sums)
     back, *sums = middle(place, low_hid, mid_slope, back, wm)
-    lower = over_x(over_cores(*sums), FAR)
+    lower = over_cores(*sums)
     small = low(low_slope, x, back, wm)
-    upper = over_x(upper, FAR)
-    small = small + sum(
-        lax.ppermute(small, "x", [(i, (i + s) % 4) for i in range(4)]) for s in (1, 2, 3)
-    )
-    lower = over_x(lower, NEAR)
+    lower = jnp.concatenate([lower, small], axis=0)
+    upper, lower = over_x(upper, NEAR), over_x(lower, FAR)
+    upper, lower = over_x(upper, FAR), over_x(lower, NEAR)
     parts = []
-    for part in (upper, lower, small):
+    for part in (upper, lower):
         parts += [part, lax.ppermute(part, "core", PAIR)]
     first, mid, last = unpack(place, *parts)
     return (first[None], mid[None], last.T[None])

time: 78 us -> 74.3 us (0.953)
  starting transfers between devices: 29.7 us -> 22.7 us
  waiting for transfers between devices: 11.7 us -> 14.7 us
    ppermute x4, waiting for transfers between devices: 3.53 us -> 7.15 us  [over_x(): got = lax.ppermute(value, 'x', ring)]
    ppermute x3 -> x0, starting transfers between devices: 2.88 us -> none  [per_device(): lax.ppermute(small, 'x', [(i, (i + s) % 4) for i in range(4)])]
    ppermute x4, starting transfers between devices: 6.29 us -> 3.62 us  [over_x(): got = lax.ppermute(value, 'x', ring)]
    ppermute x3 -> x0, waiting for transfers between devices: 1.78 us -> none  [per_device(): lax.ppermute(small, 'x', [(i, (i + s) % 4) for i in range(4)])]
    ppermute x3 -> x2, starting transfers between devices: 5.63 us -> 4.21 us  [per_device(): parts += [part, lax.ppermute(part, 'core', PAIR)]]
    ppermute x2, waiting for transfers between devices: 0.01 us -> 1.05 us  [over_cores(): got = lax.ppermute(send, 'core', PAIR)]
  transfers between devices with their start and end apart: 13 -> 9, of which waited for: 4 -> 7; matrix products, arithmetic and copies ran while one was open for 0% -> 0% of each run, Pallas kernels for 22% -> 19%
where the time goes in v5:
time: 74.3 us; the launch traced here: 74 us
  Pallas kernels  34 us (46%)
  starting transfers between devices  22.7 us (31%)
  waiting for transfers between devices  14.7 us (20%)
  local copies, waits for them, and re-layouts  1.57 us (2%)
  between operations  0.78 us (1%)
    all_to_all x1, starting transfers between devices, per_device(): got = lax.all_to_all(pay, ('z', 'y'), 0, 0, tiled=True)  12 us
    pallas_call x1, Pallas kernels, slopes(): pl.pallas_call(slope_kernel, grid=(steps,), in_specs=[inside, block, pl.B...  10.6 us
    pallas_call x1, Pallas kernels, forward(): pl.pallas_call(forward_kernel, grid=(rays // TILE,), in_specs=[inside, pl...  8.63 us
    ppermute x4, waiting for transfers between devices, over_x(): got = lax.ppermute(value, 'x', ring)  7.15 us
    pallas_call x1, Pallas kernels, top(): pl.pallas_call(top_kernel, in_specs=[pl.BlockSpec(memory_space=SMEM)] + [...  6.76 us
    all_to_all x1, waiting for transfers between devices, per_device(): got = lax.all_to_all(pay, ('z', 'y'), 0, 0, tiled=True)  5.52 us
    ppermute x2, starting transfers between devices, per_device(): parts += [part, lax.ppermute(part, 'core', PAIR)]  4.21 us
    ppermute x4, starting transfers between devices, over_x(): got = lax.ppermute(value, 'x', ring)  3.62 us
  transfers between devices with their start and end apart: 9, of which 7 were waited for; matrix products, arithmetic and copies ran while one was open for 0% of the time, Pallas kernels for 19%

profile of v5, /device:TPU:1, one launch (start us, length us, event | category | flops | bytes accessed | tf_op | source)
XLA Modules:
  0.0 74.0 jit_solution(17276876772237476306)
XLA Ops:
  0.6 1.2 %reshape_squeeze.3.x_ref = bf16[128,2048]{1,0:T(8,128)(2,1)S(1)} reshape(bf16[1,32,4,2048]{3,2,1,0:T(4,128)(2,1)} %param.8) | data formatting | bytes 1048576 | tf_op jit(solution)/shard_map/reshape;squeeze | solution.py:476
  1.8 8.6 %forward.1 = (bf16[4,2,256,2048]{3,2,1,0:T(8,128)(2,1)}, bf16[4,256,2048]{2,1,0:T(8,128)(2,1)}, f32[20,16,128]{2,1,0:T(8,128)S(1)}, f32[32,32,128]{2,1,0:T(8,128...) custom-call(bf16[128,2048]{1,0:T(8,128)(2,1)S(1)} %reshape_squeeze.3.x_ref, f32[4,2048]{1,0:T(4,128)} %bitcast.24, ...), custom_call_target="tpu_custom_call" | custom-call | flops 2298478592 | bytes 1048576 | tf_op jit(solution)/shard_map/forward/pallas_call | solution.py:307
  10.4 12.0 %all-to-all-start = ((f32[32,32,128]{2,1,0:T(8,128)}), f32[32,32,128]{2,1,0:T(8,128)S(1)}, u32[]{:S(2)}, u32[]{:S(2)}) async-start(f32[32,32,128]{2,1,0:T(8,128)} %get-tuple-element.27), calls=%async_computation | async-start | bytes 1048576 | tf_op jit(solution)/shard_map/all_to_all | solution.py:481
  22.6 10.6 %slopes.1 = (bf16[4,256,2048]{2,1,0:T(8,128)(2,1)}, bf16[4,256,2048]{2,1,0:T(8,128)(2,1)}, bf16[4,256,2048]{2,1,0:T(8,128)(2,1)}) custom-call(bf16[128,2048]{1,0:T(8,128)(2,1)S(1)} %reshape_squeeze.3.x_ref, bf16[4,256,2048]{2,1,0:T(8,128)(2,1)} %get-tuple-element.22.low_hid.hid_ref, bf16[4,2,256,2048]{3,2,1,0:T(8,128)(2,1)} %get-tuple-element.21.mid_hid.hid_hbm, ...), custom_call_target="tpu_custom_call" | custom-call | flops 2293760000 | bytes 20971520 | tf_op jit(solution)/shard_map/slopes/pallas_call | solution.py:349
  33.2 5.5 %all-to-all-done.got_ref = f32[32,32,128]{2,1,0:T(8,128)S(1)} async-done(((f32[32,32,128]{2,1,0:T(8,128)}), f32[32,32,128]{2,1,0:T(8,128)S(1)}, u32[]{:S(2)}, u32[]{:S(2)}) %all-to-all-start) | async-done | bytes 524320 | tf_op jit(solution)/shard_map/all_to_all | solution.py:481
  38.8 6.8 %top.1 = (bf16[4,256,2048]{2,1,0:T(8,128)(2,1)S(1)}, f32[264,128]{1,0:T(8,128)S(1)}, f32[264,128]{1,0:T(8,128)S(1)}) custom-call(s32[2]{0:T(128)S(1)} %pad_add_fusion.place_ref, bf16[4,2,256,2048]{3,2,1,0:T(8,128)(2,1)} %get-tuple-element.21.mid_hid.hid_hbm, bf16[4,256,2048]{2,1,0:T(8,128)(2,1)} %get-tuple-element.25.slope_hbm, ...), custom_call_target="tpu_custom_call" | custom-call | flops 1310720000 | bytes 12582912 | tf_op jit(solution)/shard_map/top/pallas_call | solution.py:372
  45.6 0.3 copy-done.2
  45.9 3.5 %middle.1 = (bf16[4,256,2048]{2,1,0:T(8,128)(2,1)S(1)}, f32[256,128]{1,0:T(8,128)S(1)}, f32[256,128]{1,0:T(8,128)S(1)}) custom-call(s32[2]{0:T(128)S(1)} %pad_add_fusion.place_ref, bf16[4,256,2048]{2,1,0:T(8,128)(2,1)S(1)} %copy-done, bf16[4,256,2048]{2,1,0:T(8,128)(2,1)S(1)} %copy-done.2, bf16[4,256,2048]{2,1,0:T(8,128)(2,1)S(1)} %get-tuple-element.31.back_ref, ...), custom_call_target="tpu_custom_call" | custom-call | flops 2147483648 | bytes 8388608 | tf_op jit(solution)/shard_map/middle/pallas_call | solution.py:402
  49.4 2.5 %collective-permute-start.4 = (f32[256,128]{1,0:T(8,128)S(1)}, f32[256,128]{1,0:T(8,128)S(1)}, u32[]{:S(2)}, u32[]{:S(2)}) collective-permute-start(f32[256,128]{1,0:T(8,128)S(1)} %get-tuple-element.33), channel_id=1, source_target_pairs={{0,1},{1,0},{2,3},{3,2},{4,5},{5,4},{6,7},{7,6},{8,9},{9,8},{10,11... | collective-permute-start | bytes 393224 | tf_op jit(solution)/shard_map/ppermute | solution.py:464
  51.9 3.1 %low.1 = f32[64,128]{1,0:T(8,128)S(1)} custom-call(bf16[4,256,2048]{2,1,0:T(8,128)(2,1)S(1)} %copy-done.1, bf16[128,2048]{1,0:T(8,128)(2,1)S(1)} %reshape_squeeze.3.x_ref, bf16[4,256,2048]{2,1,0:T(8,128)(2,1)S(1)} %get-tuple-element.35.back_ref, bf16[2,256,256]{2,1,0:T(8,128)(2,1)S(1)} %bitcast.18), custom_call_target="tpu_custom_call" | custom-call | flops 1474560000 | bytes 8388608 | tf_op jit(solution)/shard_map/low/pallas_call | solution.py:423
  55.1 2.6 %collective-permute-start.5 = (f32[320,128]{1,0:T(8,128)S(1)}, f32[320,128]{1,0:T(8,128)S(1)}, u32[]{:S(2)}, u32[]{:S(2)}) collective-permute-start(f32[320,128]{1,0:T(8,128)S(1)} %pad_maximum_fusion), channel_id=1, source_target_pairs={{0,6},{6,0},{2,4},{4,2},{1,7},{7,1},{3,5},{5,3},{8,14},{14,8},{10,... | collective-permute-start | bytes 491528 | tf_op jit(solution)/shard_map/ppermute | solution.py:469
  57.7 0.3 collective-permute-start
  58.0 1.1 %collective-permute-done = f32[264,128]{1,0:T(8,128)S(1)} collective-permute-done((f32[264,128]{1,0:T(8,128)S(1)}, f32[264,128]{1,0:T(8,128)S(1)}, u32[]{:S(2)}, u32[]{:S(2)}) %collective-permute-start) | collective-permute-done | bytes 135200 | tf_op jit(solution)/shard_map/ppermute | solution.py:464
  59.1 0.1 collective-permute-start.1
  59.2 3.0 %collective-permute-done.5 = f32[320,128]{1,0:T(8,128)S(1)} collective-permute-done((f32[320,128]{1,0:T(8,128)S(1)}, f32[320,128]{1,0:T(8,128)S(1)}, u32[]{:S(2)}, u32[]{:S(2)}) %collective-permute-start.5) | collective-permute-done | bytes 163872 | tf_op jit(solution)/shard_map/ppermute | solution.py:469
  62.2 0.1 collective-permute-start.6
  62.3 1.7 %collective-permute-done.1 = f32[264,128]{1,0:T(8,128)S(1)} collective-permute-done((f32[264,128]{1,0:T(8,128)S(1)}, f32[264,128]{1,0:T(8,128)S(1)}, u32[]{:S(2)}, u32[]{:S(2)}) %collective-permute-start.1) | collective-permute-done | bytes 135200 | tf_op jit(solution)/shard_map/ppermute | solution.py:469
  64.0 0.9 %collective-permute-start.2 = (f32[264,128]{1,0:T(8,128)S(1)}, f32[264,128]{1,0:T(8,128)S(1)}, u32[]{:S(2)}, u32[]{:S(2)}) collective-permute-start(f32[264,128]{1,0:T(8,128)S(1)} %add.23), channel_id=1, source_target_pairs={{0,6},{6,0},{2,4},{4,2},{1,7},{7,1},{3,5},{5,3},{8,14},{14,8},{10,... | collective-permute-start | bytes 405512 | tf_op jit(solution)/shard_map/ppermute | solution.py:469
  64.9 2.3 %collective-permute-done.6 = f32[320,128]{1,0:T(8,128)S(1)} collective-permute-done((f32[320,128]{1,0:T(8,128)S(1)}, f32[320,128]{1,0:T(8,128)S(1)}, u32[]{:S(2)}, u32[]{:S(2)}) %collective-permute-start.6) | collective-permute-done | bytes 163872 | tf_op jit(solution)/shard_map/ppermute | solution.py:469
  67.2 1.8 %collective-permute-start.7 = (f32[320,128]{1,0:T(8,128)S(1)}, f32[320,128]{1,0:T(8,128)S(1)}, u32[]{:S(2)}, u32[]{:S(2)}) collective-permute-start(f32[320,128]{1,0:T(8,128)S(1)} %add.27.b_ref), channel_id=1, source_target_pairs={{0,1},{1,0},{2,3},{3,2},{4,5},{5,4},{6,7},{7,6},{8,9},{9,8},{10,11... | collective-permute-start | bytes 491528 | tf_op jit(solution)/shard_map/ppermute | solution.py:493
  69.0 0.2 collective-permute-done.2
  69.2 2.4 %collective-permute-start.3 = (f32[264,128]{1,0:T(8,128)S(1)}, f32[264,128]{1,0:T(8,128)S(1)}, u32[]{:S(2)}, u32[]{:S(2)}) collective-permute-start(f32[264,128]{1,0:T(8,128)S(1)} %add.24.a_ref), channel_id=1, source_target_pairs={{0,1},{1,0},{2,3},{3,2},{4,5},{5,4},{6,7},{7,6},{8,9},{9,8},{10,11... | collective-permute-start | bytes 405512 | tf_op jit(solution)/shard_map/ppermute | solution.py:493
  71.6 1.0 %collective-permute-done.3.a_other = f32[264,128]{1,0:T(8,128)S(1)} collective-permute-done((f32[264,128]{1,0:T(8,128)S(1)}, f32[264,128]{1,0:T(8,128)S(1)}, u32[]{:S(2)}, u32[]{:S(2)}) %collective-permute-start.3) | collective-permute-done | bytes 135200 | tf_op jit(solution)/shard_map/ppermute | solution.py:493
  72.6 1.4 %unpack.1 = (f32[32,256]{1,0:T(8,128)}, f32[2,256,256]{2,1,0:T(8,128)}, f32[4,256]{1,0:T(4,128)}) custom-call(s32[2]{0:T(128)S(1)} %pad_add_fusion.place_ref, f32[264,128]{1,0:T(8,128)S(1)} %add.24.a_ref, f32[264,128]{1,0:T(8,128)S(1)} %collective-permute-done.3.a_other, f32[320,128]{1,0:T(8,128)S(1)} %add.27.b_ref, ...), custom_call_target="tpu_custom_call" | custom-call | tf_op jit(solution)/shard_map/unpack/pallas_call | solution.py:439
  (22 shorter events, 0.3 us)
Async XLA Ops:
  1.8 20.7 %copy-start.5 = (s32[2048,32]{0,1:T(8,128)S(1)}, s32[2048,32]{0,1:T(8,128)}, u32[]{:S(2)}) copy-start(s32[2048,32]{0,1:T(8,128)} %param.11) | copy-start | bytes 786436
  10.4 28.3 %all-to-all-start = ((f32[32,32,128]{2,1,0:T(8,128)}), f32[32,32,128]{2,1,0:T(8,128)S(1)}, u32[]{:S(2)}, u32[]{:S(2)}) async-start(f32[32,32,128]{2,1,0:T(8,128)} %get-tuple-element.27), calls=%async_computation | async-start | bytes 1048576 | tf_op jit(solution)/shard_map/all_to_all | solution.py:481
  22.6 16.1 %copy-start.4 = (bf16[1,256,4]{1,2,0:T(4,128)(2,1)S(1)}, bf16[1,256,4]{1,2,0:T(4,128)(2,1)}, u32[]{:S(2)}) copy-start(bf16[1,256,4]{1,2,0:T(4,128)(2,1)} %param.15) | copy-start | bytes 6148
  38.8 6.8 %copy-start = (bf16[4,256,2048]{2,1,0:T(8,128)(2,1)S(1)}, bf16[4,256,2048]{2,1,0:T(8,128)(2,1)}, u32[]{:S(2)}) copy-start(bf16[4,256,2048]{2,1,0:T(8,128)(2,1)} %get-tuple-element.22.low_hid.hid_ref) | copy-start | bytes 12582916
  38.8 7.1 %copy-start.2 = (bf16[4,256,2048]{2,1,0:T(8,128)(2,1)S(1)}, bf16[4,256,2048]{2,1,0:T(8,128)(2,1)}, u32[]{:S(2)}) copy-start(bf16[4,256,2048]{2,1,0:T(8,128)(2,1)} %get-tuple-element.30.slope_ref) | copy-start | bytes 12582916
  38.8 7.1 %copy-start.3 = (bf16[1,2,256,256]{3,2,1,0:T(8,128)(2,1)S(1)}, bf16[1,2,256,256]{3,2,1,0:T(8,128)(2,1)}, u32[]{:S(2)}) copy-start(bf16[1,2,256,256]{3,2,1,0:T(8,128)(2,1)} %param.14) | copy-start | bytes 786436
  45.9 6.0 %copy-start.1 = (bf16[4,256,2048]{2,1,0:T(8,128)(2,1)S(1)}, bf16[4,256,2048]{2,1,0:T(8,128)(2,1)}, u32[]{:S(2)}) copy-start(bf16[4,256,2048]{2,1,0:T(8,128)(2,1)} %get-tuple-element.34.slope_ref) | copy-start | bytes 12582916
  49.4 5.7 %collective-permute-start.4 = (f32[256,128]{1,0:T(8,128)S(1)}, f32[256,128]{1,0:T(8,128)S(1)}, u32[]{:S(2)}, u32[]{:S(2)}) collective-permute-start(f32[256,128]{1,0:T(8,128)S(1)} %get-tuple-element.33), channel_id=1, source_target_pairs={{0,1},{1,0},{2,3},{3,2},{4,5},{5,4},{6,7},{7,6},{8,9},{9,8},{10,11... | collective-permute-start | bytes 393224 | tf_op jit(solution)/shard_map/ppermute | solution.py:464
  55.1 7.0 %collective-permute-start.5 = (f32[320,128]{1,0:T(8,128)S(1)}, f32[320,128]{1,0:T(8,128)S(1)}, u32[]{:S(2)}, u32[]{:S(2)}) collective-permute-start(f32[320,128]{1,0:T(8,128)S(1)} %pad_maximum_fusion), channel_id=1, source_target_pairs={{0,6},{6,0},{2,4},{4,2},{1,7},{7,1},{3,5},{5,3},{8,14},{14,8},{10,... | collective-permute-start | bytes 491528 | tf_op jit(solution)/shard_map/ppermute | solution.py:469
  57.7 1.4 %collective-permute-start = (f32[264,128]{1,0:T(8,128)S(1)}, f32[264,128]{1,0:T(8,128)S(1)}, u32[]{:S(2)}, u32[]{:S(2)}) collective-permute-start(f32[264,128]{1,0:T(8,128)S(1)} %get-tuple-element.29), channel_id=1, source_target_pairs={{0,1},{1,0},{2,3},{3,2},{4,5},{5,4},{6,7},{7,6},{8,9},{9,8},{10,11... | collective-permute-start | bytes 405512 | tf_op jit(solution)/shard_map/ppermute | solution.py:464
  59.1 4.9 %collective-permute-start.1 = (f32[264,128]{1,0:T(8,128)S(1)}, f32[264,128]{1,0:T(8,128)S(1)}, u32[]{:S(2)}, u32[]{:S(2)}) collective-permute-start(f32[264,128]{1,0:T(8,128)S(1)} %add.22), channel_id=1, source_target_pairs={{0,2},{2,0},{4,6},{6,4},{1,3},{3,1},{5,7},{7,5},{8,10},{10,8},{12,... | collective-permute-start | bytes 405512 | tf_op jit(solution)/shard_map/ppermute | solution.py:469
  62.2 5.0 %collective-permute-start.6 = (f32[320,128]{1,0:T(8,128)S(1)}, f32[320,128]{1,0:T(8,128)S(1)}, u32[]{:S(2)}, u32[]{:S(2)}) collective-permute-start(f32[320,128]{1,0:T(8,128)S(1)} %fusion), channel_id=1, source_target_pairs={{0,2},{2,0},{4,6},{6,4},{1,3},{3,1},{5,7},{7,5},{8,10},{10,8},{12,... | collective-permute-start | bytes 491528 | tf_op jit(solution)/shard_map/ppermute | solution.py:469
  64.0 5.2 %collective-permute-start.2 = (f32[264,128]{1,0:T(8,128)S(1)}, f32[264,128]{1,0:T(8,128)S(1)}, u32[]{:S(2)}, u32[]{:S(2)}) collective-permute-start(f32[264,128]{1,0:T(8,128)S(1)} %add.23), channel_id=1, source_target_pairs={{0,6},{6,0},{2,4},{4,2},{1,7},{7,1},{3,5},{5,3},{8,14},{14,8},{10,... | collective-permute-start | bytes 405512 | tf_op jit(solution)/shard_map/ppermute | solution.py:469
  67.2 5.4 %collective-permute-start.7 = (f32[320,128]{1,0:T(8,128)S(1)}, f32[320,128]{1,0:T(8,128)S(1)}, u32[]{:S(2)}, u32[]{:S(2)}) collective-permute-start(f32[320,128]{1,0:T(8,128)S(1)} %add.27.b_ref), channel_id=1, source_target_pairs={{0,1},{1,0},{2,3},{3,2},{4,5},{5,4},{6,7},{7,6},{8,9},{9,8},{10,11... | collective-permute-start | bytes 491528 | tf_op jit(solution)/shard_map/ppermute | solution.py:493
  69.2 3.4 %collective-permute-start.3 = (f32[264,128]{1,0:T(8,128)S(1)}, f32[264,128]{1,0:T(8,128)S(1)}, u32[]{:S(2)}, u32[]{:S(2)}) collective-permute-start(f32[264,128]{1,0:T(8,128)S(1)} %add.24.a_ref), channel_id=1, source_target_pairs={{0,1},{1,0},{2,3},{3,2},{4,5},{5,4},{6,7},{7,6},{8,9},{9,8},{10,11... | collective-permute-start | bytes 405512 | tf_op jit(solution)/shard_map/ppermute | solution.py:493

commit v6 on v5

--- a/solution.py
+++ b/solution.py
@@ -200,7 +200,7 @@
         front[v] = jnp.exp(total)
         return 0
 
-    lax.fori_loop(0, NV, one, 0)
+    lax.fori_loop(0, NV, one, 0, unroll=4)
     me = place_ref[0]
     mine = rank_ref[me]
     behind = jnp.zeros((planes, 128), F32)
@@ -248,7 +248,7 @@
         mid[...] += dot(hid_ref[i], down, 1, 1)
         return 0
 
-    lax.fori_loop(0, hid_ref.shape[0], step, 0, unroll=2)
+    lax.fori_loop(0, hid_ref.shape[0], step, 0, unroll=4)
     split(place_ref, keep_ref, send_ref, (mid[...],))
 
 
@@ -262,7 +262,7 @@
         first[...] += dot(spread(x_ref[:, rays], jnp.zeros((), BF16)), down, 1, 1)
         return 0
 
-    lax.fori_loop(0, slope_ref.shape[0], step, 0, unroll=2)
+    lax.fori_loop(0, slope_ref.shape[0], step, 0, unroll=4)
     pick = group_rows(FEAT * SAMP, FEAT).astype(F32)
     small = dot(pick, first[...], 0, 0, lax.Precision.HIGHEST)
     out_ref[:FEAT] = small[:, :128]

time: 74.3 us -> 73.5 us (0.989)
  transfers between devices with their start and end apart: 9 -> 9, of which waited for: 7 -> 7; matrix products, arithmetic and copies ran while one was open for 0% -> 0% of each run, Pallas kernels for 19% -> 18%
where the time goes in v6:
time: 73.5 us; the launch traced here: 73.2 us
  Pallas kernels  33.3 us (45%)
  starting transfers between devices  22.7 us (31%)
  waiting for transfers between devices  14.7 us (20%)
  local copies, waits for them, and re-layouts  1.57 us (2%)
  between operations  0.77 us (1%)
    all_to_all x1, starting transfers between devices, per_device(): got = lax.all_to_all(pay, ('z', 'y'), 0, 0, tiled=True)  12 us
    pallas_call x1, Pallas kernels, slopes(): pl.pallas_call(slope_kernel, grid=(steps,), in_specs=[inside, block, pl.B...  10.6 us
    pallas_call x1, Pallas kernels, forward(): pl.pallas_call(forward_kernel, grid=(rays // TILE,), in_specs=[inside, pl...  8.63 us
    ppermute x4, waiting for transfers between devices, over_x(): got = lax.ppermute(value, 'x', ring)  7.15 us
    pallas_call x1, Pallas kernels, top(): pl.pallas_call(top_kernel, in_specs=[pl.BlockSpec(memory_space=SMEM)] + [...  6.76 us
    all_to_all x1, waiting for transfers between devices, per_device(): got = lax.all_to_all(pay, ('z', 'y'), 0, 0, tiled=True)  5.52 us
    ppermute x2, starting transfers between devices, per_device(): parts += [part, lax.ppermute(part, 'core', PAIR)]  4.21 us
    ppermute x4, starting transfers between devices, over_x(): got = lax.ppermute(value, 'x', ring)  3.62 us
  transfers between devices with their start and end apart: 9, of which 7 were waited for; matrix products, arithmetic and copies ran while one was open for 0% of the time, Pallas kernels for 18%

profile of v6, /device:TPU:1, one launch (start us, length us, event | category | flops | bytes accessed | tf_op | source)
XLA Modules:
  0.0 73.2 jit_solution(10925836965665191830)
XLA Ops:
  0.6 1.2 %reshape_squeeze.3.x_ref = bf16[128,2048]{1,0:T(8,128)(2,1)S(1)} reshape(bf16[1,32,4,2048]{3,2,1,0:T(4,128)(2,1)} %param.8) | data formatting | bytes 1048576 | tf_op jit(solution)/shard_map/reshape;squeeze | solution.py:476
  1.8 8.6 %forward.1 = (bf16[4,2,256,2048]{3,2,1,0:T(8,128)(2,1)}, bf16[4,256,2048]{2,1,0:T(8,128)(2,1)}, f32[20,16,128]{2,1,0:T(8,128)S(1)}, f32[32,32,128]{2,1,0:T(8,128...) custom-call(bf16[128,2048]{1,0:T(8,128)(2,1)S(1)} %reshape_squeeze.3.x_ref, f32[4,2048]{1,0:T(4,128)} %bitcast.24, ...), custom_call_target="tpu_custom_call" | custom-call | flops 2298478592 | bytes 1048576 | tf_op jit(solution)/shard_map/forward/pallas_call | solution.py:307
  10.4 12.0 %all-to-all-start = ((f32[32,32,128]{2,1,0:T(8,128)}), f32[32,32,128]{2,1,0:T(8,128)S(1)}, u32[]{:S(2)}, u32[]{:S(2)}) async-start(f32[32,32,128]{2,1,0:T(8,128)} %get-tuple-element.27), calls=%async_computation | async-start | bytes 1048576 | tf_op jit(solution)/shard_map/all_to_all | solution.py:481
  22.6 10.6 %slopes.1 = (bf16[4,256,2048]{2,1,0:T(8,128)(2,1)}, bf16[4,256,2048]{2,1,0:T(8,128)(2,1)}, bf16[4,256,2048]{2,1,0:T(8,128)(2,1)}) custom-call(bf16[128,2048]{1,0:T(8,128)(2,1)S(1)} %reshape_squeeze.3.x_ref, bf16[4,256,2048]{2,1,0:T(8,128)(2,1)} %get-tuple-element.22.low_hid.hid_ref, bf16[4,2,256,2048]{3,2,1,0:T(8,128)(2,1)} %get-tuple-element.21.mid_hid.hid_hbm, ...), custom_call_target="tpu_custom_call" | custom-call | flops 2293760000 | bytes 20971520 | tf_op jit(solution)/shard_map/slopes/pallas_call | solution.py:349
  33.2 5.5 %all-to-all-done.got_ref = f32[32,32,128]{2,1,0:T(8,128)S(1)} async-done(((f32[32,32,128]{2,1,0:T(8,128)}), f32[32,32,128]{2,1,0:T(8,128)S(1)}, u32[]{:S(2)}, u32[]{:S(2)}) %all-to-all-start) | async-done | bytes 524320 | tf_op jit(solution)/shard_map/all_to_all | solution.py:481
  38.8 6.8 %top.1 = (bf16[4,256,2048]{2,1,0:T(8,128)(2,1)S(1)}, f32[264,128]{1,0:T(8,128)S(1)}, f32[264,128]{1,0:T(8,128)S(1)}) custom-call(s32[2]{0:T(128)S(1)} %pad_add_fusion.place_ref, bf16[4,2,256,2048]{3,2,1,0:T(8,128)(2,1)} %get-tuple-element.21.mid_hid.hid_hbm, bf16[4,256,2048]{2,1,0:T(8,128)(2,1)} %get-tuple-element.25.slope_hbm, ...), custom_call_target="tpu_custom_call" | custom-call | flops 1310720000 | bytes 12582912 | tf_op jit(solution)/shard_map/top/pallas_call | solution.py:372
  45.6 0.3 copy-done.2
  45.9 3.1 %middle.1 = (bf16[4,256,2048]{2,1,0:T(8,128)(2,1)S(1)}, f32[256,128]{1,0:T(8,128)S(1)}, f32[256,128]{1,0:T(8,128)S(1)}) custom-call(s32[2]{0:T(128)S(1)} %pad_add_fusion.place_ref, bf16[4,256,2048]{2,1,0:T(8,128)(2,1)S(1)} %copy-done, bf16[4,256,2048]{2,1,0:T(8,128)(2,1)S(1)} %copy-done.2, bf16[4,256,2048]{2,1,0:T(8,128)(2,1)S(1)} %get-tuple-element.31.back_ref, ...), custom_call_target="tpu_custom_call" | custom-call | flops 2147483648 | bytes 8388608 | tf_op jit(solution)/shard_map/middle/pallas_call | solution.py:402
  49.0 2.5 %collective-permute-start.4 = (f32[256,128]{1,0:T(8,128)S(1)}, f32[256,128]{1,0:T(8,128)S(1)}, u32[]{:S(2)}, u32[]{:S(2)}) collective-permute-start(f32[256,128]{1,0:T(8,128)S(1)} %get-tuple-element.33), channel_id=1, source_target_pairs={{0,1},{1,0},{2,3},{3,2},{4,5},{5,4},{6,7},{7,6},{8,9},{9,8},{10,11... | collective-permute-start | bytes 393224 | tf_op jit(solution)/shard_map/ppermute | solution.py:464
  51.5 2.8 %low.1 = f32[64,128]{1,0:T(8,128)S(1)} custom-call(bf16[4,256,2048]{2,1,0:T(8,128)(2,1)S(1)} %copy-done.1, bf16[128,2048]{1,0:T(8,128)(2,1)S(1)} %reshape_squeeze.3.x_ref, bf16[4,256,2048]{2,1,0:T(8,128)(2,1)S(1)} %get-tuple-element.35.back_ref, bf16[2,256,256]{2,1,0:T(8,128)(2,1)S(1)} %bitcast.18), custom_call_target="tpu_custom_call" | custom-call | flops 1474560000 | bytes 8388608 | tf_op jit(solution)/shard_map/low/pallas_call | solution.py:423
  54.4 2.6 %collective-permute-start.5 = (f32[320,128]{1,0:T(8,128)S(1)}, f32[320,128]{1,0:T(8,128)S(1)}, u32[]{:S(2)}, u32[]{:S(2)}) collective-permute-start(f32[320,128]{1,0:T(8,128)S(1)} %pad_maximum_fusion), channel_id=1, source_target_pairs={{0,6},{6,0},{2,4},{4,2},{1,7},{7,1},{3,5},{5,3},{8,14},{14,8},{10,... | collective-permute-start | bytes 491528 | tf_op jit(solution)/shard_map/ppermute | solution.py:469
  56.9 0.3 collective-permute-start
  57.2 1.1 %collective-permute-done = f32[264,128]{1,0:T(8,128)S(1)} collective-permute-done((f32[264,128]{1,0:T(8,128)S(1)}, f32[264,128]{1,0:T(8,128)S(1)}, u32[]{:S(2)}, u32[]{:S(2)}) %collective-permute-start) | collective-permute-done | bytes 135200 | tf_op jit(solution)/shard_map/ppermute | solution.py:464
  58.3 0.1 collective-permute-start.1
  58.4 3.0 %collective-permute-done.5 = f32[320,128]{1,0:T(8,128)S(1)} collective-permute-done((f32[320,128]{1,0:T(8,128)S(1)}, f32[320,128]{1,0:T(8,128)S(1)}, u32[]{:S(2)}, u32[]{:S(2)}) %collective-permute-start.5) | collective-permute-done | bytes 163872 | tf_op jit(solution)/shard_map/ppermute | solution.py:469
  61.4 0.1 collective-permute-start.6
  61.5 1.7 %collective-permute-done.1 = f32[264,128]{1,0:T(8,128)S(1)} collective-permute-done((f32[264,128]{1,0:T(8,128)S(1)}, f32[264,128]{1,0:T(8,128)S(1)}, u32[]{:S(2)}, u32[]{:S(2)}) %collective-permute-start.1) | collective-permute-done | bytes 135200 | tf_op jit(solution)/shard_map/ppermute | solution.py:469
  63.3 0.9 %collective-permute-start.2 = (f32[264,128]{1,0:T(8,128)S(1)}, f32[264,128]{1,0:T(8,128)S(1)}, u32[]{:S(2)}, u32[]{:S(2)}) collective-permute-start(f32[264,128]{1,0:T(8,128)S(1)} %add.23), channel_id=1, source_target_pairs={{0,6},{6,0},{2,4},{4,2},{1,7},{7,1},{3,5},{5,3},{8,14},{14,8},{10,... | collective-permute-start | bytes 405512 | tf_op jit(solution)/shard_map/ppermute | solution.py:469
  64.1 2.3 %collective-permute-done.6 = f32[320,128]{1,0:T(8,128)S(1)} collective-permute-done((f32[320,128]{1,0:T(8,128)S(1)}, f32[320,128]{1,0:T(8,128)S(1)}, u32[]{:S(2)}, u32[]{:S(2)}) %collective-permute-start.6) | collective-permute-done | bytes 163872 | tf_op jit(solution)/shard_map/ppermute | solution.py:469
  66.4 1.8 %collective-permute-start.7 = (f32[320,128]{1,0:T(8,128)S(1)}, f32[320,128]{1,0:T(8,128)S(1)}, u32[]{:S(2)}, u32[]{:S(2)}) collective-permute-start(f32[320,128]{1,0:T(8,128)S(1)} %add.27.b_ref), channel_id=1, source_target_pairs={{0,1},{1,0},{2,3},{3,2},{4,5},{5,4},{6,7},{7,6},{8,9},{9,8},{10,11... | collective-permute-start | bytes 491528 | tf_op jit(solution)/shard_map/ppermute | solution.py:493
  68.2 0.2 collective-permute-done.2
  68.4 2.4 %collective-permute-start.3 = (f32[264,128]{1,0:T(8,128)S(1)}, f32[264,128]{1,0:T(8,128)S(1)}, u32[]{:S(2)}, u32[]{:S(2)}) collective-permute-start(f32[264,128]{1,0:T(8,128)S(1)} %add.24.a_ref), channel_id=1, source_target_pairs={{0,1},{1,0},{2,3},{3,2},{4,5},{5,4},{6,7},{7,6},{8,9},{9,8},{10,11... | collective-permute-start | bytes 405512 | tf_op jit(solution)/shard_map/ppermute | solution.py:493
  70.8 1.0 %collective-permute-done.3.a_other = f32[264,128]{1,0:T(8,128)S(1)} collective-permute-done((f32[264,128]{1,0:T(8,128)S(1)}, f32[264,128]{1,0:T(8,128)S(1)}, u32[]{:S(2)}, u32[]{:S(2)}) %collective-permute-start.3) | collective-permute-done | bytes 135200 | tf_op jit(solution)/shard_map/ppermute | solution.py:493
  71.8 1.4 %unpack.1 = (f32[32,256]{1,0:T(8,128)}, f32[2,256,256]{2,1,0:T(8,128)}, f32[4,256]{1,0:T(4,128)}) custom-call(s32[2]{0:T(128)S(1)} %pad_add_fusion.place_ref, f32[264,128]{1,0:T(8,128)S(1)} %add.24.a_ref, f32[264,128]{1,0:T(8,128)S(1)} %collective-permute-done.3.a_other, f32[320,128]{1,0:T(8,128)S(1)} %add.27.b_ref, ...), custom_call_target="tpu_custom_call" | custom-call | tf_op jit(solution)/shard_map/unpack/pallas_call | solution.py:439
  (22 shorter events, 0.3 us)
Async XLA Ops:
  1.8 20.7 %copy-start.5 = (s32[2048,32]{0,1:T(8,128)S(1)}, s32[2048,32]{0,1:T(8,128)}, u32[]{:S(2)}) copy-start(s32[2048,32]{0,1:T(8,128)} %param.11) | copy-start | bytes 786436
  10.4 28.3 %all-to-all-start = ((f32[32,32,128]{2,1,0:T(8,128)}), f32[32,32,128]{2,1,0:T(8,128)S(1)}, u32[]{:S(2)}, u32[]{:S(2)}) async-start(f32[32,32,128]{2,1,0:T(8,128)} %get-tuple-element.27), calls=%async_computation | async-start | bytes 1048576 | tf_op jit(solution)/shard_map/all_to_all | solution.py:481
  22.6 16.1 %copy-start.4 = (bf16[1,256,4]{1,2,0:T(4,128)(2,1)S(1)}, bf16[1,256,4]{1,2,0:T(4,128)(2,1)}, u32[]{:S(2)}) copy-start(bf16[1,256,4]{1,2,0:T(4,128)(2,1)} %param.15) | copy-start | bytes 6148
  38.8 6.8 %copy-start = (bf16[4,256,2048]{2,1,0:T(8,128)(2,1)S(1)}, bf16[4,256,2048]{2,1,0:T(8,128)(2,1)}, u32[]{:S(2)}) copy-start(bf16[4,256,2048]{2,1,0:T(8,128)(2,1)} %get-tuple-element.22.low_hid.hid_ref) | copy-start | bytes 12582916
  38.8 7.1 %copy-start.2 = (bf16[4,256,2048]{2,1,0:T(8,128)(2,1)S(1)}, bf16[4,256,2048]{2,1,0:T(8,128)(2,1)}, u32[]{:S(2)}) copy-start(bf16[4,256,2048]{2,1,0:T(8,128)(2,1)} %get-tuple-element.30.slope_ref) | copy-start | bytes 12582916
  38.8 7.1 %copy-start.3 = (bf16[1,2,256,256]{3,2,1,0:T(8,128)(2,1)S(1)}, bf16[1,2,256,256]{3,2,1,0:T(8,128)(2,1)}, u32[]{:S(2)}) copy-start(bf16[1,2,256,256]{3,2,1,0:T(8,128)(2,1)} %param.14) | copy-start | bytes 786436
  45.9 5.6 %copy-start.1 = (bf16[4,256,2048]{2,1,0:T(8,128)(2,1)S(1)}, bf16[4,256,2048]{2,1,0:T(8,128)(2,1)}, u32[]{:S(2)}) copy-start(bf16[4,256,2048]{2,1,0:T(8,128)(2,1)} %get-tuple-element.34.slope_ref) | copy-start | bytes 12582916
  49.0 5.3 %collective-permute-start.4 = (f32[256,128]{1,0:T(8,128)S(1)}, f32[256,128]{1,0:T(8,128)S(1)}, u32[]{:S(2)}, u32[]{:S(2)}) collective-permute-start(f32[256,128]{1,0:T(8,128)S(1)} %get-tuple-element.33), channel_id=1, source_target_pairs={{0,1},{1,0},{2,3},{3,2},{4,5},{5,4},{6,7},{7,6},{8,9},{9,8},{10,11... | collective-permute-start | bytes 393224 | tf_op jit(solution)/shard_map/ppermute | solution.py:464
  54.4 7.0 %collective-permute-start.5 = (f32[320,128]{1,0:T(8,128)S(1)}, f32[320,128]{1,0:T(8,128)S(1)}, u32[]{:S(2)}, u32[]{:S(2)}) collective-permute-start(f32[320,128]{1,0:T(8,128)S(1)} %pad_maximum_fusion), channel_id=1, source_target_pairs={{0,6},{6,0},{2,4},{4,2},{1,7},{7,1},{3,5},{5,3},{8,14},{14,8},{10,... | collective-permute-start | bytes 491528 | tf_op jit(solution)/shard_map/ppermute | solution.py:469
  56.9 1.4 %collective-permute-start = (f32[264,128]{1,0:T(8,128)S(1)}, f32[264,128]{1,0:T(8,128)S(1)}, u32[]{:S(2)}, u32[]{:S(2)}) collective-permute-start(f32[264,128]{1,0:T(8,128)S(1)} %get-tuple-element.29), channel_id=1, source_target_pairs={{0,1},{1,0},{2,3},{3,2},{4,5},{5,4},{6,7},{7,6},{8,9},{9,8},{10,11... | collective-permute-start | bytes 405512 | tf_op jit(solution)/shard_map/ppermute | solution.py:464
  58.3 4.9 %collective-permute-start.1 = (f32[264,128]{1,0:T(8,128)S(1)}, f32[264,128]{1,0:T(8,128)S(1)}, u32[]{:S(2)}, u32[]{:S(2)}) collective-permute-start(f32[264,128]{1,0:T(8,128)S(1)} %add.22), channel_id=1, source_target_pairs={{0,2},{2,0},{4,6},{6,4},{1,3},{3,1},{5,7},{7,5},{8,10},{10,8},{12,... | collective-permute-start | bytes 405512 | tf_op jit(solution)/shard_map/ppermute | solution.py:469
  61.4 5.0 %collective-permute-start.6 = (f32[320,128]{1,0:T(8,128)S(1)}, f32[320,128]{1,0:T(8,128)S(1)}, u32[]{:S(2)}, u32[]{:S(2)}) collective-permute-start(f32[320,128]{1,0:T(8,128)S(1)} %fusion), channel_id=1, source_target_pairs={{0,2},{2,0},{4,6},{6,4},{1,3},{3,1},{5,7},{7,5},{8,10},{10,8},{12,... | collective-permute-start | bytes 491528 | tf_op jit(solution)/shard_map/ppermute | solution.py:469
  63.3 5.2 %collective-permute-start.2 = (f32[264,128]{1,0:T(8,128)S(1)}, f32[264,128]{1,0:T(8,128)S(1)}, u32[]{:S(2)}, u32[]{:S(2)}) collective-permute-start(f32[264,128]{1,0:T(8,128)S(1)} %add.23), channel_id=1, source_target_pairs={{0,6},{6,0},{2,4},{4,2},{1,7},{7,1},{3,5},{5,3},{8,14},{14,8},{10,... | collective-permute-start | bytes 405512 | tf_op jit(solution)/shard_map/ppermute | solution.py:469
  66.4 5.4 %collective-permute-start.7 = (f32[320,128]{1,0:T(8,128)S(1)}, f32[320,128]{1,0:T(8,128)S(1)}, u32[]{:S(2)}, u32[]{:S(2)}) collective-permute-start(f32[320,128]{1,0:T(8,128)S(1)} %add.27.b_ref), channel_id=1, source_target_pairs={{0,1},{1,0},{2,3},{3,2},{4,5},{5,4},{6,7},{7,6},{8,9},{9,8},{10,11... | collective-permute-start | bytes 491528 | tf_op jit(solution)/shard_map/ppermute | solution.py:493
  68.4 3.4 %collective-permute-start.3 = (f32[264,128]{1,0:T(8,128)S(1)}, f32[264,128]{1,0:T(8,128)S(1)}, u32[]{:S(2)}, u32[]{:S(2)}) collective-permute-start(f32[264,128]{1,0:T(8,128)S(1)} %add.24.a_ref), channel_id=1, source_target_pairs={{0,1},{1,0},{2,3},{3,2},{4,5},{5,4},{6,7},{7,6},{8,9},{9,8},{10,11... | collective-permute-start | bytes 405512 | tf_op jit(solution)/shard_map/ppermute | solution.py:493
